TPU v7x, 128 devices: a whole 4x4x4 slice. The times are simulated.
128 devices in a mesh: seq: 16 (over x_hi, y, core), chan: 8 (over z, x_lo).
Axes of the slice: x: 4 (x_hi: 2, x_lo: 2; x = x_hi * 2 + x_lo), y: 4, z: 4, core: 2. Of those that a mesh axis runs over, the one named last changes fastest.
Arguments:
- projected: bfloat16 [2048, 3, 4096], P('seq', None, 'chan'), may hold values from -6 to 6
- short_filter: float32 [3, 3, 4096], P(None, None, 'chan'), may hold values from -3 to 3
- long_filter: float32 [2048, 4096], P('seq', 'chan'), may hold values from -1.1 to 1.1
- w_out: bfloat16 [4096, 4096], P('chan', 'seq'), may hold values from -0.09375 to 0.09375
- d_out: bfloat16 [2048, 4096], P('seq', 'chan'), may hold values from -0.75 to 0.75
Outputs:
- output: bfloat16 [2048, 4096], P('seq', 'chan')
- d_projected: bfloat16 [2048, 3, 4096], P('seq', None, 'chan')
- d_wout: float32 [4096, 4096], P('chan', 'seq')
- d_filter: float32 [2048, 4096], P('seq', 'chan')
All inputs are finite; a program needn't handle non-finite values.
Results may differ from a plain program's by a relative error of at most 0.0049.
Values may be sent and summed in bfloat16 or wider, within the bound.
No kernel may reach another device: no remote copies, remote signals or barrier semaphores. Data moves between devices by JAX's collectives and lax.ppermute only.
A program may use at most 64 MiB of HBM per device.

v0:
```python
import numpy as np
import ml_dtypes

import jax
import jax.numpy as jnp
from jax import lax
from jax.experimental import pallas as pl
from jax.experimental.pallas import tpu as pltpu
from jax.sharding import PartitionSpec as P

BF16 = jnp.bfloat16
F32 = jnp.float32

SEQ = 16
CHAN = 8
TOKENS = 2048
ROWS = 128
COLS = 512
LANE = 32
NEAR = 4
FAR = SEQ // NEAR
HALF = 33
MID = 72
BACK = 80
VMEM_LIMIT = 48 * 1024 * 1024


def device(seq_at, chan_at):
    return seq_at * CHAN + chan_at


def swap_pairs():
    pairs = []
    for seq_at in range(SEQ):
        for chan_at in range(CHAN):
            a, i = divmod(seq_at, NEAR)
            b, p = divmod(chan_at, CHAN // FAR)
            pairs.append(
                (device(seq_at, chan_at), device(b * NEAR + i, a * (CHAN // FAR) + p))
            )
    return pairs


def swapped(array):
    return lax.ppermute(array, ("seq", "chan"), swap_pairs())


def near_pairs(step):
    return [(i, i ^ step) for i in range(SEQ)]


def exchange(array, axis):
    return lax.all_to_all(array, axis, 0, 0, tiled=True)


def thrice(table):
    high = table.astype(ml_dtypes.bfloat16)
    low = (table - high.astype(np.float64)).astype(ml_dtypes.bfloat16)
    return np.concatenate([high, high, low], axis=-1)


def tables():
    n1 = np.arange(32)
    n2 = np.arange(64)
    k1 = np.arange(HALF)
    k2 = np.arange(64)
    time = 64 * n1[None, None, :] + n2[:, None, None]
    outer = 2.0 * np.pi / 4096.0 * ((time * k1[None, :, None]) % 4096)
    inner = 2.0 * np.pi / 64.0 * ((k2[:, None] * n2[None, :]) % 64)
    weight = np.where((k1 == 0) | (k1 == 32), 1.0, 2.0)[None, :, None] / 4096.0
    first = np.zeros((64, MID, 32))
    first[:, :HALF] = np.cos(outer)
    first[:, HALF : 2 * HALF] = -np.sin(outer)
    last = np.zeros((64, 32, BACK))
    last[:, :, 0 : 2 * HALF : 2] = (np.cos(outer) * weight).transpose(0, 2, 1)
    last[:, :, 1 : 2 * HALF : 2] = (-np.sin(outer) * weight).transpose(0, 2, 1)
    cos, sin = np.cos(inner), np.sin(inner)
    ahead = np.block([[cos, sin], [-sin, cos]])
    return thrice(first), thrice(ahead), thrice(ahead.T), thrice(last)


def pieces(array):
    high = array.astype(BF16)
    low = (array - high.astype(F32)).astype(BF16)
    return jnp.concatenate([high, low, high], axis=0)


def matmul(left, right):
    return jnp.dot(left, right, preferred_element_type=F32)


def every(count, width, step):
    def body(block, carry):
        for at in range(width):
            step(block * width + at)
        return carry

    lax.fori_loop(0, count // width, body, 0)


def lanes_of(rows):
    return lax.broadcasted_iota(jnp.int32, (rows, 4 * LANE), 1)


def ahead_rows(mid_ref, k1):
    return jnp.concatenate(
        [mid_ref[pl.ds(k1, 64, stride=MID), :], mid_ref[pl.ds(HALF + k1, 64, stride=MID), :]],
        axis=0,
    )


def forward_kernel(
    signal_ref, taps_ref, first_ref, ahead_ref, behind_ref, last_ref,
    gated_ref, kept_ref, spec_ref,
    wide_ref, mid_ref, back_ref, column_ref,
):
    wide_ref[0:8, :] = jnp.zeros((8, 4 * LANE), F32)
    wide_ref[8:, :] = signal_ref[...].astype(F32)
    back_ref[2 * HALF * 64 :, :] = jnp.zeros(((BACK - 2 * HALF) * 64, 4 * LANE), F32)
    lane = lanes_of(32)
    tap0, tap1, tap2 = (jnp.broadcast_to(taps_ref[j : j + 1, :], (32, 4 * LANE)) for j in range(3))

    def outer(n2):
        now = wide_ref[pl.ds(n2 + 8, 32, stride=64), :]
        before = wide_ref[pl.ds(n2 + 7, 32, stride=64), :]
        earlier = wide_ref[pl.ds(n2 + 6, 32, stride=64), :]
        mixed = tap0 * now + tap1 * before + tap2 * earlier
        kept_ref[pl.ds(n2, 32, stride=64), :] = mixed
        carried = mixed * pltpu.roll(mixed, LANE, 1)
        data = jnp.where((lane >= 2 * LANE) & (lane < 3 * LANE), carried, mixed)
        mid_ref[pl.ds(pl.multiple_of(n2 * MID, 8), MID), :] = matmul(first_ref[n2], pieces(data))

    every(64, 4, outer)

    def inner(k1):
        spec = matmul(ahead_ref[...], pieces(ahead_rows(mid_ref, k1)))
        spec_ref[k1] = spec
        other = pltpu.roll(spec, 3 * LANE, 1)
        re, im, other_re, other_im = spec[:64], spec[64:], other[:64], other[64:]
        both = jnp.concatenate(
            [re * other_re - im * other_im, re * other_im + im * other_re], axis=0
        )
        back_ref[pl.ds(pl.multiple_of(k1 * 128, 128), 128), :] = matmul(
            behind_ref[...], pieces(both)
        )

    every(HALF, 3, inner)

    def final(n2):
        conv = matmul(last_ref[n2], pieces(back_ref[pl.ds(n2, BACK, stride=64), :]))
        mixed = kept_ref[pl.ds(n2, 32, stride=64), :]
        column_ref[pl.ds(n2, 32, stride=64), :] = mixed * pltpu.roll(conv, 2 * LANE, 1)
        kept_ref[pl.ds(n2, 32, stride=64), :] = jnp.where(
            lane < 3 * LANE, mixed, pltpu.roll(conv, LANE, 1)
        )

    every(64, 4, final)

    for block in range(SEQ):
        a, i = divmod(block, NEAR)
        turned = column_ref[block * ROWS : (block + 1) * ROWS, :].T
        gated_ref[i, :, a * ROWS : (a + 1) * ROWS] = turned[:LANE].astype(BF16)


def backward_kernel(
    share_ref, kept_ref, spec_ref, taps_ref, first_ref, ahead_ref, behind_ref, last_ref,
    out_ref,
    grad_ref, mid_ref, back_ref, column_ref,
):
    back_ref[2 * HALF * 64 :, :] = jnp.zeros(((BACK - 2 * HALF) * 64, 4 * LANE), F32)
    column_ref[TOKENS:, :] = jnp.zeros((8, 4 * LANE), F32)
    for i in range(NEAR):
        total = share_ref[i].astype(F32)
        for far in range(1, FAR):
            total = total + share_ref[far * NEAR + i].astype(F32)
        for a in range(FAR):
            block = a * NEAR + i
            part = total[:, a * ROWS : (a + 1) * ROWS]
            grad_ref[block * ROWS : (block + 1) * ROWS, :] = jnp.concatenate([part] * 4, axis=0).T
    lane = lanes_of(32)

    def outer(n2):
        kept = kept_ref[pl.ds(n2, 32, stride=64), :]
        query = jnp.where(lane < 3 * LANE, pltpu.roll(kept, 2 * LANE, 1), pltpu.roll(kept, 3 * LANE, 1))
        data = grad_ref[pl.ds(n2, 32, stride=64), :] * query
        mid_ref[pl.ds(pl.multiple_of(n2 * MID, 8), MID), :] = matmul(first_ref[n2], pieces(data))

    every(64, 4, outer)

    wide = lanes_of(128)

    def inner(k1):
        grad = matmul(ahead_ref[...], pieces(ahead_rows(mid_ref, k1)))
        spec = spec_ref[k1]
        other = jnp.where(wide < 3 * LANE, pltpu.roll(spec, 3 * LANE, 1), pltpu.roll(spec, LANE, 1))
        re, im, other_re, other_im = grad[:64], grad[64:], other[:64], other[64:]
        both = jnp.concatenate(
            [other_re * re + other_im * im, other_re * im - other_im * re], axis=0
        )
        back_ref[pl.ds(pl.multiple_of(k1 * 128, 128), 128), :] = matmul(
            behind_ref[...], pieces(both)
        )

    every(HALF, 3, inner)

    def final(n2):
        found = matmul(last_ref[n2], pieces(back_ref[pl.ds(n2, BACK, stride=64), :]))
        kept = kept_ref[pl.ds(n2, 32, stride=64), :]
        grad = grad_ref[pl.ds(n2, 32, stride=64), :]
        up, down = pltpu.roll(kept, LANE, 1), pltpu.roll(kept, 3 * LANE, 1)
        mixed = jnp.where(
            lane < LANE,
            grad * up,
            jnp.where(
                lane < 2 * LANE,
                pltpu.roll(found, 3 * LANE, 1) * down,
                jnp.where(lane < 3 * LANE, found * up, found),
            ),
        )
        column_ref[pl.ds(n2, 32, stride=64), :] = mixed

    every(64, 4, final)

    tap0, tap1, tap2 = (
        jnp.broadcast_to(taps_ref[j : j + 1, :], (ROWS, 4 * LANE)) for j in range(3)
    )
    for block in range(SEQ):
        low = block * ROWS
        out_ref[block] = (
            tap0 * column_ref[low : low + ROWS, :]
            + tap1 * column_ref[low + 1 : low + 1 + ROWS, :]
            + tap2 * column_ref[low + 2 : low + 2 + ROWS, :]
        ).astype(BF16)


def whole(shape):
    return pl.BlockSpec(shape, lambda _: (0,) * len(shape))


def convolve(signals, taps, consts, interpret=False):
    shapes = (
        jax.ShapeDtypeStruct((NEAR, LANE, FAR * ROWS), BF16),
        jax.ShapeDtypeStruct((TOKENS, 4 * LANE), F32),
        jax.ShapeDtypeStruct((HALF, 128, 4 * LANE), F32),
    )
    return pl.pallas_call(
        forward_kernel,
        out_shape=shapes,
        scratch_shapes=[
            pltpu.VMEM((TOKENS + 8, 4 * LANE), F32),
            pltpu.VMEM((64 * MID, 4 * LANE), F32),
            pltpu.VMEM((64 * BACK, 4 * LANE), F32),
            pltpu.VMEM((TOKENS, 4 * LANE), F32),
        ],
        compiler_params=pltpu.CompilerParams(vmem_limit_bytes=VMEM_LIMIT),
        interpret=interpret,
        name="convolve",
    )(signals, taps, *consts)


def correlate(shares, kept, spec, taps, consts, interpret=False):
    inputs = (shares, kept, spec, taps) + tuple(consts)
    specs = [whole(x.shape) for x in inputs]
    specs[0] = pl.BlockSpec((SEQ, LANE, FAR * ROWS), lambda _: (0, 1, 0))
    return pl.pallas_call(
        backward_kernel,
        out_shape=jax.ShapeDtypeStruct((SEQ, ROWS, 4 * LANE), BF16),
        grid=(1,),
        in_specs=specs,
        out_specs=whole((SEQ, ROWS, 4 * LANE)),
        scratch_shapes=[
            pltpu.VMEM((TOKENS, 4 * LANE), F32),
            pltpu.VMEM((64 * MID, 4 * LANE), F32),
            pltpu.VMEM((64 * BACK, 4 * LANE), F32),
            pltpu.VMEM((TOKENS + 8, 4 * LANE), F32),
        ],
        compiler_params=pltpu.CompilerParams(vmem_limit_bytes=VMEM_LIMIT),
        interpret=interpret,
        name="correlate",
    )(*inputs)


def shards(projected, short_filter, long_filter, w_out, d_out):
    seq_at = lax.axis_index("seq")
    near_at = seq_at % NEAR
    consts = [jnp.asarray(table) for table in tables()]

    moved = swapped(d_out)

    streams = jnp.concatenate([projected, long_filter.astype(BF16)[:, None, :]], axis=1)
    packed = streams.reshape(ROWS, 4, SEQ, LANE).transpose(2, 0, 1, 3).reshape(SEQ, ROWS, 4 * LANE)
    signals = exchange(packed, "seq").reshape(TOKENS, 4 * LANE)

    cots = exchange(jnp.broadcast_to(moved[None], (CHAN, ROWS, COLS)), "chan")
    cots = cots.reshape(FAR, 2, ROWS, COLS).transpose(0, 2, 1, 3).reshape(FAR * ROWS, 2 * COLS)

    weights = jnp.zeros((NEAR,) + w_out.shape, BF16)
    for step in range(NEAR):
        piece = w_out if step == 0 else lax.ppermute(w_out, "seq", near_pairs(step))
        weights = lax.dynamic_update_slice(weights, piece[None], (near_at ^ step, 0, 0))
    weights = weights.transpose(1, 0, 2).reshape(COLS, NEAR * w_out.shape[1])

    own = lax.dynamic_slice_in_dim(short_filter, seq_at * LANE, LANE, axis=2).reshape(3, 3 * LANE)
    plain = jnp.zeros((3, LANE), F32).at[0].set(1.0)
    taps = jnp.concatenate([own, plain], axis=1)

    gated_send, kept, spec = convolve(signals, taps, consts)

    part = lax.dot_general(
        weights, cots, (((1,), (1,)), ((), ())), preferred_element_type=F32
    ).astype(BF16)
    gated_send = jnp.broadcast_to(
        gated_send[None], (FAR, NEAR, LANE, FAR * ROWS)
    ).reshape(SEQ, LANE, FAR * ROWS)
    sent = jnp.concatenate([gated_send, part.reshape(SEQ, LANE, FAR * ROWS)], axis=1)
    got = exchange(sent, "seq")
    gated_cols = got[:, :LANE].reshape(COLS, FAR * ROWS)

    partial_out = lax.dot_general(
        gated_cols, weights, (((0,), (0,)), ((), ())), preferred_element_type=F32
    ).astype(BF16)
    partial_out = partial_out.reshape(FAR, ROWS, 2, COLS).transpose(0, 2, 1, 3)
    shares = exchange(partial_out.reshape(CHAN, ROWS, COLS), "chan")
    output = swapped(jnp.sum(shares.astype(F32), axis=0).astype(BF16))

    grad = jnp.dot(gated_cols, cots, preferred_element_type=F32)
    grad = grad.reshape(COLS, NEAR, -1).transpose(1, 0, 2)
    d_wout = lax.dynamic_index_in_dim(grad, near_at, 0, keepdims=False)
    for step in range(1, NEAR):
        piece = lax.dynamic_index_in_dim(grad, near_at ^ step, 0, keepdims=False).astype(BF16)
        d_wout = d_wout + lax.ppermute(piece, "seq", near_pairs(step)).astype(F32)

    d_signals = correlate(got, kept, spec, taps, consts)
    returned = exchange(d_signals, "seq")
    returned = returned.reshape(SEQ, ROWS, 4, LANE).transpose(1, 2, 0, 3).reshape(ROWS, 4, COLS)
    return (output, returned[:, :3], d_wout, returned[:, 3].astype(F32))


def solution(mesh):
    in_specs = (
        P("seq", None, "chan"),
        P(None, None, "chan"),
        P("seq", "chan"),
        P("chan", "seq"),
        P("seq", "chan"),
    )
    out_specs = (P("seq", "chan"), P("seq", None, "chan"), P("chan", "seq"), P("seq", "chan"))
    return jax.shard_map(shards, mesh=mesh, in_specs=in_specs, out_specs=out_specs, check_vma=False)
```

profile of v0, /device:TPU:32, one launch (start us, length us, event | category | flops | bytes accessed | tf_op | source)
XLA Modules:
  0.0 175.5 jit_solution(13517514331595061449)
XLA Ops:
  0.7 1.1 copy.29
  1.8 1.2 copy.28
  3.1 0.8 copy.30
  3.9 7.0 %all-to-all-start = ((bf16[16,128,128]{1,2,0:T(8,128)(2,1)}), bf16[16,128,128]{1,2,0:T(8,128)(2,1)S(1)}, u32[]{:S(2)}, u32[]{:S(2)}) async-start(bf16[16,128,128]{1,2,0:T(8,128)(2,1)} %bitcast.3), calls=%async_computation | async-start | bytes 1048576 | tf_op jit(solution)/shard_map/all_to_all | solution.py:53
  11.1 1.8 collective-permute-start.2
  13.3 4.7 %collective-permute-start.3 = (bf16[128,512]{1,0:T(8,128)(2,1)S(1)}, bf16[128,512]{1,0:T(8,128)(2,1)S(1)}, u32[]{:S(2)}, u32[]{:S(2)}) collective-permute-start(bf16[128,512]{1,0:T(8,128)(2,1)S(1)} %copy-done.14), channel_id=1, source_target_pairs={{0,0},{1,1},{2,32},{3,33},{4,64},{5,65},{6,96},{7,97},{8,8},{9,9},... | collective-permute-start | bytes 393224 | tf_op jit(solution)/shard_map/ppermute | solution.py:45
  18.0 1.1 broadcast_in_dim.15
  19.8 17.8 %collective-permute-done.3 = bf16[128,512]{1,0:T(8,128)(2,1)S(1)} collective-permute-done((bf16[128,512]{1,0:T(8,128)(2,1)S(1)}, bf16[128,512]{1,0:T(8,128)(2,1)S(1)}, u32[]{:S(2)}, u32[]{:S(2)}) %collective-permute-start.3) | collective-permute-done | bytes 131104 | tf_op jit(solution)/shard_map/ppermute | solution.py:45
  38.4 1.1 broadcast_in_dim.36
  39.5 4.3 %all-to-all-start.1 = ((bf16[8,128,512]{2,1,0:T(8,128)(2,1)}), bf16[8,128,512]{2,1,0:T(8,128)(2,1)}, u32[]{:S(2)}, u32[]{:S(2)}) async-start(bf16[8,128,512]{2,1,0:T(8,128)(2,1)} %broadcast_in_dim.36), calls=%async_computation.1 | async-start | bytes 2097152 | tf_op jit(solution)/shard_map/all_to_all | solution.py:53
  46.3 1.3 copy.31
  47.7 22.9 %convolve.1 = (bf16[4,32,512]{2,1,0:T(8,128)(2,1)S(1)}, f32[2048,128]{1,0:T(8,128)S(1)}, f32[33,128,128]{2,1,0:T(8,128)}) custom-call(bf16[2048,128]{1,0:T(8,128)(2,1)S(1)} %bitcast.61, f32[3,128]{1,0:T(4,128)S(1)} %pad_maximum_fusion.1.taps_ref, bf16[64,72,96]{2,1,0:T(8,128)(2,1)S(1)} %copy-done.1, bf16[128,384]{1,0:T(8,128)(2,1)S(1)} %copy-done.7, ...), custom_call_target="tpu_custom_call" | custom-call | tf_op jit(solution)/shard_map/convolve/pallas_call | solution.py:246
  70.6 1.0 copy-done.4
  71.6 2.3 %copy.36 = bf16[4,128,2,512]{3,2,1,0:T(2,128)(2,1)S(1)} copy(bf16[4,128,2,512]{3,1,2,0:T(8,128)(2,1)} %bitcast.13) | data formatting | bytes 2097152 | tf_op jit(solution)/shard_map/transpose | solution.py:295
  74.2 2.4 %convolution_convert_fusion.1 = bf16[512,512]{1,0:T(8,128)(2,1)S(1)} fusion(bf16[512,1024]{0,1:T(8,128)(2,1)} %bitcast.11, bf16[512,1024]{1,0:T(8,128)(2,1)S(1)} %bitcast.63), kind=kOutput, calls=%fused_computation.1 | convolution fusion | flops 537133056 | bytes 2621440 | tf_op jit(solution)/shard_map/dot_general | solution.py:309
  76.7 26.1 %all_to_all.25.share_ref = bf16[16,64,512]{2,1,0:T(8,128)(2,1)S(1)} all-to-all(bf16[16,64,512]{2,1,0:T(8,128)(2,1)S(1)} %pad_maximum_fusion), channel_id=1, replica_groups=mesh['seq'=16,'chan'=8] {'seq'}, dimensions={0} | all-to-all | bytes 2097152 | tf_op jit(solution)/shard_map/all_to_all | solution.py:53
  102.8 20.4 %correlate.1 = bf16[16,128,128]{2,1,0:T(8,128)(2,1)S(1)} custom-call(bf16[16,64,512]{2,1,0:T(8,128)(2,1)S(1)} %all_to_all.25.share_ref, f32[2048,128]{1,0:T(8,128)S(1)} %copy-done.5, f32[33,128,128]{2,1,0:T(8,128)} %get-tuple-element.21.spec_ref, f32[3,128]{1,0:T(4,128)S(1)} %pad_maximum_fusion.1.taps_ref, bf16[64,72,96]{2,1,0:T(8,128)(2,1)S(1)} %copy-done.1, ...), custom_call_target="tpu_custom_call" | custom-call | tf_op jit(solution)/shard_map/correlate/pallas_call | solution.py:265
  124.0 4.2 %all-to-all-start.4 = ((bf16[16,128,128]{2,1,0:T(8,128)(2,1)}), bf16[16,128,128]{2,1,0:T(8,128)(2,1)}, u32[]{:S(2)}, u32[]{:S(2)}) async-start(bf16[16,128,128]{2,1,0:T(8,128)(2,1)} %copy-done.3), calls=%async_computation.4 | async-start | bytes 1048576 | tf_op jit(solution)/shard_map/all_to_all | solution.py:53
  128.2 1.5 copy.40
  130.6 2.0 %convolution_convert_fusion = bf16[512,1024]{1,0:T(8,128)(2,1)S(1)} fusion(bf16[512,512]{1,0:T(8,128)(2,1)S(1)} %bitcast.66, bf16[512,1024]{0,1:T(8,128)(2,1)} %bitcast.11), kind=kOutput, calls=%fused_computation | convolution fusion | flops 537395200 | bytes 2621440 | tf_op jit(solution)/shard_map/dot_general | solution.py:319
  133.4 1.2 copy.37
  134.5 6.0 %all-to-all-done.4 = bf16[16,128,128]{2,1,0:T(8,128)(2,1)} async-done(((bf16[16,128,128]{2,1,0:T(8,128)(2,1)}), bf16[16,128,128]{2,1,0:T(8,128)(2,1)}, u32[]{:S(2)}, u32[]{:S(2)}) %all-to-all-start.4) | async-done | bytes 524320 | tf_op jit(solution)/shard_map/all_to_all | solution.py:53
  140.6 5.1 %all-to-all-start.3 = ((bf16[8,128,512]{2,1,0:T(8,128)(2,1)}), bf16[8,128,512]{2,1,0:T(8,128)(2,1)S(1)}, u32[]{:S(2)}, u32[]{:S(2)}) async-start(bf16[8,128,512]{2,1,0:T(8,128)(2,1)} %bitcast.17), calls=%async_computation.3 | async-start | bytes 2097152 | tf_op jit(solution)/shard_map/all_to_all | solution.py:53
  146.7 2.0 %collective-permute-start.6 = (bf16[512,256]{1,0:T(8,128)(2,1)S(1)}, bf16[512,256]{1,0:T(8,128)(2,1)S(1)}, u32[]{:S(2)}, u32[]{:S(2)}) collective-permute-start(bf16[512,256]{1,0:T(8,128)(2,1)S(1)} %get-tuple-element.32), channel_id=1, source_target_pairs={{0,16},{8,24},{16,0},{24,8},{32,48},{40,56},{48,32},{56,40},{64,80... | collective-permute-start | bytes 786440 | tf_op jit(solution)/shard_map/ppermute | solution.py:331
  148.8 6.0 %collective-permute-done.7 = bf16[512,256]{1,0:T(8,128)(2,1)S(1)} collective-permute-done((bf16[512,256]{1,0:T(8,128)(2,1)S(1)}, bf16[512,256]{1,0:T(8,128)(2,1)S(1)}, u32[]{:S(2)}, u32[]{:S(2)}) %collective-permute-start.7) | collective-permute-done | bytes 262176 | tf_op jit(solution)/shard_map/ppermute | solution.py:331
  154.7 6.2 %collective-permute-done.6 = bf16[512,256]{1,0:T(8,128)(2,1)S(1)} collective-permute-done((bf16[512,256]{1,0:T(8,128)(2,1)S(1)}, bf16[512,256]{1,0:T(8,128)(2,1)S(1)}, u32[]{:S(2)}, u32[]{:S(2)}) %collective-permute-start.6) | collective-permute-done | bytes 262176 | tf_op jit(solution)/shard_map/ppermute | solution.py:331
  160.9 0.9 fusion.1
  161.8 1.3 copy.38
  163.2 0.9 copy.41
  164.3 2.0 %collective-permute-start.4 = (bf16[128,512]{1,0:T(8,128)(2,1)S(1)}, bf16[128,512]{1,0:T(8,128)(2,1)S(1)}, u32[]{:S(2)}, u32[]{:S(2)}) collective-permute-start(bf16[128,512]{1,0:T(8,128)(2,1)S(1)} %reduce_sum.12), channel_id=1, source_target_pairs={{0,0},{1,1},{2,32},{3,33},{4,64},{5,65},{6,96},{7,97},{8,8},{9,9},... | collective-permute-start | bytes 393224 | tf_op jit(solution)/shard_map/ppermute | solution.py:45
  166.4 0.8 copy.42
  167.2 7.7 %collective-permute-done.4 = bf16[128,512]{1,0:T(8,128)(2,1)S(1)} collective-permute-done((bf16[128,512]{1,0:T(8,128)(2,1)S(1)}, bf16[128,512]{1,0:T(8,128)(2,1)S(1)}, u32[]{:S(2)}, u32[]{:S(2)}) %collective-permute-start.4) | collective-permute-done | bytes 131104 | tf_op jit(solution)/shard_map/ppermute | solution.py:45
  (61 shorter events, 9.3 us)
Async XLA Ops:
  0.6 43.2 %copy-start = (f32[3,3,512]{2,1,0:T(4,128)S(1)}, f32[3,3,512]{2,1,0:T(4,128)}, u32[]{:S(2)}) copy-start(f32[3,3,512]{2,1,0:T(4,128)} %param.12) | copy-start | bytes 55300
  0.6 10.3 %copy-start.12 = (bf16[512,256]{1,0:T(8,128)(2,1)S(1)}, bf16[512,256]{1,0:T(8,128)(2,1)}, u32[]{:S(2)}) copy-start(bf16[512,256]{1,0:T(8,128)(2,1)} %param.14) | copy-start | bytes 786436
  1.8 11.5 %copy-start.14 = (bf16[128,512]{1,0:T(8,128)(2,1)S(1)}, bf16[128,512]{1,0:T(8,128)(2,1)}, u32[]{:S(2)}) copy-start(bf16[128,512]{1,0:T(8,128)(2,1)} %param.15) | copy-start | bytes 393220
  3.9 33.7 %all-to-all-start = ((bf16[16,128,128]{1,2,0:T(8,128)(2,1)}), bf16[16,128,128]{1,2,0:T(8,128)(2,1)S(1)}, u32[]{:S(2)}, u32[]{:S(2)}) async-start(bf16[16,128,128]{1,2,0:T(8,128)(2,1)} %bitcast.3), calls=%async_computation | async-start | bytes 1048576 | tf_op jit(solution)/shard_map/all_to_all | solution.py:53
  11.1 34.4 %collective-permute-start.2 = (bf16[512,256]{0,1:T(8,128)(2,1)S(1)}, bf16[512,256]{0,1:T(8,128)(2,1)S(1)}, u32[]{:S(2)}, u32[]{:S(2)}) collective-permute-start(bf16[512,256]{0,1:T(8,128)(2,1)S(1)} %copy.32), channel_id=1, source_target_pairs={{0,24},{8,16},{16,8},{24,0},{32,56},{40,48},{48,40},{56,32},{64,88... | collective-permute-start | bytes 786440 | tf_op jit(solution)/shard_map/ppermute | solution.py:299
  12.9 32.0 %collective-permute-start.1 = (bf16[512,256]{0,1:T(8,128)(2,1)S(1)}, bf16[512,256]{0,1:T(8,128)(2,1)S(1)}, u32[]{:S(2)}, u32[]{:S(2)}) collective-permute-start(bf16[512,256]{0,1:T(8,128)(2,1)S(1)} %copy.32), channel_id=1, source_target_pairs={{0,16},{8,24},{16,0},{24,8},{32,48},{40,56},{48,32},{56,40},{64,80... | collective-permute-start | bytes 786440 | tf_op jit(solution)/shard_map/ppermute | solution.py:299
  13.3 30.8 %collective-permute-start = (bf16[512,256]{0,1:T(8,128)(2,1)S(1)}, bf16[512,256]{0,1:T(8,128)(2,1)S(1)}, u32[]{:S(2)}, u32[]{:S(2)}) collective-permute-start(bf16[512,256]{0,1:T(8,128)(2,1)S(1)} %copy.32), channel_id=1, source_target_pairs={{0,8},{8,0},{16,24},{24,16},{32,40},{40,32},{48,56},{56,48},{64,72... | collective-permute-start | bytes 786440 | tf_op jit(solution)/shard_map/ppermute | solution.py:299
  13.3 24.3 %collective-permute-start.3 = (bf16[128,512]{1,0:T(8,128)(2,1)S(1)}, bf16[128,512]{1,0:T(8,128)(2,1)S(1)}, u32[]{:S(2)}, u32[]{:S(2)}) collective-permute-start(bf16[128,512]{1,0:T(8,128)(2,1)S(1)} %copy-done.14), channel_id=1, source_target_pairs={{0,0},{1,1},{2,32},{3,33},{4,64},{5,65},{6,96},{7,97},{8,8},{9,9},... | collective-permute-start | bytes 393224 | tf_op jit(solution)/shard_map/ppermute | solution.py:45
  19.1 25.0 %copy-start.13 = (f32[3,32]{1,0:T(4,128)S(1)}, f32[3,32]{1,0:T(4,128)}, u32[]{:S(2)}) copy-start(f32[3,32]{1,0:T(4,128)} %constant.76.clone.1) | copy-start | bytes 1156
  37.6 0.8 copy-start.11
  39.5 8.1 %copy-start.1 = (bf16[64,72,96]{2,1,0:T(8,128)(2,1)S(1)}, bf16[64,72,96]{2,1,0:T(8,128)(2,1)}, u32[]{:S(2)}) copy-start(bf16[64,72,96]{2,1,0:T(8,128)(2,1)} %constant.82.clone.first_ref) | copy-start | bytes 2654212
  39.5 8.2 %copy-start.2 = (bf16[64,32,240]{2,1,0:T(8,128)(2,1)S(1)}, bf16[64,32,240]{2,1,0:T(8,128)(2,1)}, u32[]{:S(2)}) copy-start(bf16[64,32,240]{2,1,0:T(8,128)(2,1)} %constant.85.clone.last_ref) | copy-start | bytes 2949124
  39.5 8.2 %copy-start.6 = (bf16[128,384]{1,0:T(8,128)(2,1)S(1)}, bf16[128,384]{1,0:T(8,128)(2,1)}, u32[]{:S(2)}) copy-start(bf16[128,384]{1,0:T(8,128)(2,1)} %constant.84.clone.behind_ref) | copy-start | bytes 294916
  39.5 8.2 %copy-start.7 = (bf16[128,384]{1,0:T(8,128)(2,1)S(1)}, bf16[128,384]{1,0:T(8,128)(2,1)}, u32[]{:S(2)}) copy-start(bf16[128,384]{1,0:T(8,128)(2,1)} %constant.83.clone.ahead_ref) | copy-start | bytes 294916
  39.5 32.1 %all-to-all-start.1 = ((bf16[8,128,512]{2,1,0:T(8,128)(2,1)}), bf16[8,128,512]{2,1,0:T(8,128)(2,1)}, u32[]{:S(2)}, u32[]{:S(2)}) async-start(bf16[8,128,512]{2,1,0:T(8,128)(2,1)} %broadcast_in_dim.36), calls=%async_computation.1 | async-start | bytes 2097152 | tf_op jit(solution)/shard_map/all_to_all | solution.py:53
  70.6 1.0 copy-start.4
  74.1 2.4 %copy-start.8 = (bf16[64,8,2,512]{3,1,2,0:T(8,128)(2,1)}, bf16[64,8,2,512]{3,1,2,0:T(8,128)(2,1)S(1)}, u32[]{:S(2)}) copy-start(bf16[64,8,2,512]{3,1,2,0:T(8,128)(2,1)S(1)} %copy.43) | copy-start | bytes 3145732
  76.6 26.2 %copy-start.5 = (f32[2048,128]{1,0:T(8,128)S(1)}, f32[2048,128]{1,0:T(8,128)}, u32[]{:S(2)}) copy-start(f32[2048,128]{1,0:T(8,128)} %copy-done.4) | copy-start | bytes 3145732
  123.2 0.8 copy-start.3
  124.0 16.6 %all-to-all-start.4 = ((bf16[16,128,128]{2,1,0:T(8,128)(2,1)}), bf16[16,128,128]{2,1,0:T(8,128)(2,1)}, u32[]{:S(2)}, u32[]{:S(2)}) async-start(bf16[16,128,128]{2,1,0:T(8,128)(2,1)} %copy-done.3), calls=%async_computation.4 | async-start | bytes 1048576 | tf_op jit(solution)/shard_map/all_to_all | solution.py:53
  129.8 0.8 copy-start.9
  133.4 12.3 %copy-start.10 = (bf16[16,32,512]{2,1,0:T(8,128)(2,1)S(1)}, bf16[16,32,512]{2,1,0:T(8,128)(2,1)}, u32[]{:S(2)}) copy-start(bf16[16,32,512]{2,1,0:T(8,128)(2,1)} %copy-done.9) | copy-start | bytes 1572868
  140.6 23.6 %all-to-all-start.3 = ((bf16[8,128,512]{2,1,0:T(8,128)(2,1)}), bf16[8,128,512]{2,1,0:T(8,128)(2,1)S(1)}, u32[]{:S(2)}, u32[]{:S(2)}) async-start(bf16[8,128,512]{2,1,0:T(8,128)(2,1)} %bitcast.17), calls=%async_computation.3 | async-start | bytes 2097152 | tf_op jit(solution)/shard_map/all_to_all | solution.py:53
  146.5 2.2 %collective-permute-start.5 = (bf16[512,256]{1,0:T(8,128)(2,1)S(1)}, bf16[512,256]{1,0:T(8,128)(2,1)S(1)}, u32[]{:S(2)}, u32[]{:S(2)}) collective-permute-start(bf16[512,256]{1,0:T(8,128)(2,1)S(1)} %get-tuple-element.30), channel_id=1, source_target_pairs={{0,8},{8,0},{16,24},{24,16},{32,40},{40,32},{48,56},{56,48},{64,72... | collective-permute-start | bytes 786440 | tf_op jit(solution)/shard_map/ppermute | solution.py:331
  146.6 8.1 %collective-permute-start.7 = (bf16[512,256]{1,0:T(8,128)(2,1)S(1)}, bf16[512,256]{1,0:T(8,128)(2,1)S(1)}, u32[]{:S(2)}, u32[]{:S(2)}) collective-permute-start(bf16[512,256]{1,0:T(8,128)(2,1)S(1)} %get-tuple-element.31), channel_id=1, source_target_pairs={{0,24},{8,16},{16,8},{24,0},{32,56},{40,48},{48,40},{56,32},{64,88... | collective-permute-start | bytes 786440 | tf_op jit(solution)/shard_map/ppermute | solution.py:331
  146.7 14.2 %collective-permute-start.6 = (bf16[512,256]{1,0:T(8,128)(2,1)S(1)}, bf16[512,256]{1,0:T(8,128)(2,1)S(1)}, u32[]{:S(2)}, u32[]{:S(2)}) collective-permute-start(bf16[512,256]{1,0:T(8,128)(2,1)S(1)} %get-tuple-element.32), channel_id=1, source_target_pairs={{0,16},{8,24},{16,0},{24,8},{32,48},{40,56},{48,32},{56,40},{64,80... | collective-permute-start | bytes 786440 | tf_op jit(solution)/shard_map/ppermute | solution.py:331
  164.3 10.6 %collective-permute-start.4 = (bf16[128,512]{1,0:T(8,128)(2,1)S(1)}, bf16[128,512]{1,0:T(8,128)(2,1)S(1)}, u32[]{:S(2)}, u32[]{:S(2)}) collective-permute-start(bf16[128,512]{1,0:T(8,128)(2,1)S(1)} %reduce_sum.12), channel_id=1, source_target_pairs={{0,0},{1,1},{2,32},{3,33},{4,64},{5,65},{6,96},{7,97},{8,8},{9,9},... | collective-permute-start | bytes 393224 | tf_op jit(solution)/shard_map/ppermute | solution.py:45
where the time goes:
time: 178 us; the launch traced here: 176 us
  waiting for transfers between devices  43.7 us (25%)
  Pallas kernels  43.3 us (24%)
  starting transfers between devices  31.8 us (18%)
  blocking collectives  26.1 us (15%)
  local copies, waits for them, and re-layouts  23.4 us (13%)
  matrix products  5.08 us (3%)
    all_to_all x1, blocking collectives, exchange(): return lax.all_to_all(array, axis, 0, 0, tiled=True)  26.1 us
    ppermute x2, waiting for transfers between devices, swapped(): return lax.ppermute(array, ('seq', 'chan'), swap_pairs())  25.5 us
    pallas_call x1, Pallas kernels, convolve(): pl.pallas_call(forward_kernel, out_shape=shapes, scratch_shapes=[pltpu.VM...  22.9 us
    all_to_all x4, starting transfers between devices, exchange(): return lax.all_to_all(array, axis, 0, 0, tiled=True)  20.7 us
    pallas_call x1, Pallas kernels, correlate(): pl.pallas_call(backward_kernel, out_shape=jax.ShapeDtypeStruct((SEQ, ROWS...  20.4 us
    ppermute x3, waiting for transfers between devices, shards(): d_wout = d_wout + lax.ppermute(piece, 'seq', near_pairs(step)).astype(F32)  12.2 us
    unnamed x37, local copies, waits for them, and re-layouts  8.63 us
    ppermute x2, starting transfers between devices, swapped(): return lax.ppermute(array, ('seq', 'chan'), swap_pairs())  6.71 us
  transfers between devices with their start and end apart: 12, of which 5 were waited for; matrix products, arithmetic and copies ran while one was open for 10% of the time, Pallas kernels for 13%

commit v1 on v0

--- a/solution.py
+++ b/solution.py
@@ -23,6 +23,8 @@
 MID = 72
 BACK = 80
 VMEM_LIMIT = 48 * 1024 * 1024
+WIDE = 16
+GROUP = 11
 
 
 def device(seq_at, chan_at):
@@ -102,11 +104,28 @@
     return lax.broadcasted_iota(jnp.int32, (rows, 4 * LANE), 1)
 
 
-def ahead_rows(mid_ref, k1):
+def ahead_rows(mid_ref, first):
     return jnp.concatenate(
-        [mid_ref[pl.ds(k1, 64, stride=MID), :], mid_ref[pl.ds(HALF + k1, 64, stride=MID), :]],
-        axis=0,
-    )
+        [
+            jnp.concatenate(
+                [
+                    mid_ref[pl.ds(first + at, 64, stride=MID), :],
+                    mid_ref[pl.ds(HALF + first + at, 64, stride=MID), :],
+                ],
+                axis=0,
+            )
+            for at in range(GROUP)
+        ],
+        axis=1,
+    )
+
+
+def behind_rows(back_ref, first, behind_ref, products):
+    found = matmul(behind_ref[...], pieces(jnp.concatenate(products, axis=1)))
+    for at in range(GROUP):
+        back_ref[pl.ds(pl.multiple_of((first + at) * 128, 128), 128), :] = found[
+            :, at * 128 : (at + 1) * 128
+        ]
 
 
 def forward_kernel(
@@ -130,21 +149,24 @@
         data = jnp.where((lane >= 2 * LANE) & (lane < 3 * LANE), carried, mixed)
         mid_ref[pl.ds(pl.multiple_of(n2 * MID, 8), MID), :] = matmul(first_ref[n2], pieces(data))
 
-    every(64, 4, outer)
-
-    def inner(k1):
-        spec = matmul(ahead_ref[...], pieces(ahead_rows(mid_ref, k1)))
-        spec_ref[k1] = spec
-        other = pltpu.roll(spec, 3 * LANE, 1)
-        re, im, other_re, other_im = spec[:64], spec[64:], other[:64], other[64:]
-        both = jnp.concatenate(
-            [re * other_re - im * other_im, re * other_im + im * other_re], axis=0
-        )
-        back_ref[pl.ds(pl.multiple_of(k1 * 128, 128), 128), :] = matmul(
-            behind_ref[...], pieces(both)
-        )
-
-    every(HALF, 3, inner)
+    every(64, WIDE, outer)
+
+    def inner(group):
+        spec = matmul(ahead_ref[...], pieces(ahead_rows(mid_ref, group * GROUP)))
+        products = []
+        for at in range(GROUP):
+            one = spec[:, at * 128 : (at + 1) * 128]
+            spec_ref[group * GROUP + at] = one
+            other = pltpu.roll(one, 3 * LANE, 1)
+            re, im, other_re, other_im = one[:64], one[64:], other[:64], other[64:]
+            products.append(
+                jnp.concatenate(
+                    [re * other_re - im * other_im, re * other_im + im * other_re], axis=0
+                )
+            )
+        behind_rows(back_ref, group * GROUP, behind_ref, products)
+
+    every(HALF // GROUP, 1, inner)
 
     def final(n2):
         conv = matmul(last_ref[n2], pieces(back_ref[pl.ds(n2, BACK, stride=64), :]))
@@ -154,7 +176,7 @@
             lane < 3 * LANE, mixed, pltpu.roll(conv, LANE, 1)
         )
 
-    every(64, 4, final)
+    every(64, WIDE, final)
 
     for block in range(SEQ):
         a, i = divmod(block, NEAR)
@@ -185,23 +207,28 @@
         data = grad_ref[pl.ds(n2, 32, stride=64), :] * query
         mid_ref[pl.ds(pl.multiple_of(n2 * MID, 8), MID), :] = matmul(first_ref[n2], pieces(data))
 
-    every(64, 4, outer)
+    every(64, WIDE, outer)
 
     wide = lanes_of(128)
 
-    def inner(k1):
-        grad = matmul(ahead_ref[...], pieces(ahead_rows(mid_ref, k1)))
-        spec = spec_ref[k1]
-        other = jnp.where(wide < 3 * LANE, pltpu.roll(spec, 3 * LANE, 1), pltpu.roll(spec, LANE, 1))
-        re, im, other_re, other_im = grad[:64], grad[64:], other[:64], other[64:]
-        both = jnp.concatenate(
-            [other_re * re + other_im * im, other_re * im - other_im * re], axis=0
-        )
-        back_ref[pl.ds(pl.multiple_of(k1 * 128, 128), 128), :] = matmul(
-            behind_ref[...], pieces(both)
-        )
-
-    every(HALF, 3, inner)
+    def inner(group):
+        grad = matmul(ahead_ref[...], pieces(ahead_rows(mid_ref, group * GROUP)))
+        products = []
+        for at in range(GROUP):
+            one = grad[:, at * 128 : (at + 1) * 128]
+            spec = spec_ref[group * GROUP + at]
+            other = jnp.where(
+                wide < 3 * LANE, pltpu.roll(spec, 3 * LANE, 1), pltpu.roll(spec, LANE, 1)
+            )
+            re, im, other_re, other_im = one[:64], one[64:], other[:64], other[64:]
+            products.append(
+                jnp.concatenate(
+                    [other_re * re + other_im * im, other_re * im - other_im * re], axis=0
+                )
+            )
+        behind_rows(back_ref, group * GROUP, behind_ref, products)
+
+    every(HALF // GROUP, 1, inner)
 
     def final(n2):
         found = matmul(last_ref[n2], pieces(back_ref[pl.ds(n2, BACK, stride=64), :]))
@@ -219,7 +246,7 @@
         )
         column_ref[pl.ds(n2, 32, stride=64), :] = mixed
 
-    every(64, 4, final)
+    every(64, WIDE, final)
 
     tap0, tap1, tap2 = (
         jnp.broadcast_to(taps_ref[j : j + 1, :], (ROWS, 4 * LANE)) for j in range(3)
@@ -231,6 +258,9 @@
             + tap1 * column_ref[low + 1 : low + 1 + ROWS, :]
             + tap2 * column_ref[low + 2 : low + 2 + ROWS, :]
         ).astype(BF16)
+
+
+LONG = pl.CostEstimate(flops=8_000_000_000, transcendentals=0, bytes_accessed=6_000_000)
 
 
 def whole(shape):
@@ -253,6 +283,7 @@
             pltpu.VMEM((TOKENS, 4 * LANE), F32),
         ],
         compiler_params=pltpu.CompilerParams(vmem_limit_bytes=VMEM_LIMIT),
+        cost_estimate=LONG,
         interpret=interpret,
         name="convolve",
     )(signals, taps, *consts)
@@ -275,65 +306,160 @@
             pltpu.VMEM((TOKENS + 8, 4 * LANE), F32),
         ],
         compiler_params=pltpu.CompilerParams(vmem_limit_bytes=VMEM_LIMIT),
+        cost_estimate=LONG,
         interpret=interpret,
         name="correlate",
     )(*inputs)
 
 
+def pack_kernel(streams_ref, filter_ref, out_ref):
+    lane = lanes_of(ROWS)
+    for column in range(COLS // 128):
+        at = slice(column * 128, (column + 1) * 128)
+        blocks = [streams_ref[j, :, at].astype(F32) for j in range(3)] + [filter_ref[:, at]]
+        for part in range(4):
+            placed = [pltpu.roll(b, ((j - part) % 4) * LANE, 1) if j != part else b
+                      for j, b in enumerate(blocks)]
+            joined = placed[3]
+            for j in range(2, -1, -1):
+                joined = jnp.where(lane < (j + 1) * LANE, placed[j], joined)
+            out_ref[column * 4 + part] = joined.astype(BF16)
+
+
+def unpack_kernel(got_ref, streams_ref, filter_ref):
+    lane = lanes_of(ROWS)
+    for column in range(COLS // 128):
+        at = slice(column * 128, (column + 1) * 128)
+        blocks = [got_ref[column * 4 + part].astype(F32) for part in range(4)]
+        for j in range(4):
+            placed = [pltpu.roll(b, ((part - j) % 4) * LANE, 1) if j != part else b
+                      for part, b in enumerate(blocks)]
+            joined = placed[3]
+            for part in range(2, -1, -1):
+                joined = jnp.where(lane < (part + 1) * LANE, placed[part], joined)
+            if j < 3:
+                streams_ref[j, :, at] = joined.astype(BF16)
+            else:
+                filter_ref[:, at] = joined
+
+
+def cot_columns(cots_ref, block):
+    low = pl.multiple_of((block % 2) * 256, 256)
+    return jnp.concatenate(
+        [cots_ref[2 * a + block // 2, :, pl.ds(low, 256)] for a in range(FAR)], axis=0
+    )
+
+
+def contract(left, right, left_dim, right_dim):
+    return lax.dot_general(
+        left, right, (((left_dim,), (right_dim,)), ((), ())), preferred_element_type=F32
+    )
+
+
+def send_kernel(near_ref, gated_ref, cots_ref, *refs):
+    weight_refs, sent_ref = refs[:NEAR], refs[NEAR]
+    total = None
+    for step in range(NEAR):
+        term = contract(weight_refs[step][...], cot_columns(cots_ref, near_ref[0] ^ step), 1, 1)
+        total = term if total is None else total + term
+    total = total.astype(BF16)
+    for s in range(SEQ):
+        sent_ref[s, :LANE, :] = gated_ref[s % NEAR]
+        sent_ref[s, LANE:, :] = total[s * LANE : (s + 1) * LANE]
+
+
+def product_kernel(near_ref, got_ref, cots_ref, *refs):
+    weight_refs, out_ref, grad_refs = refs[:NEAR], refs[NEAR], refs[NEAR + 1 :]
+    gated = got_ref[...].reshape(COLS, FAR * ROWS)
+    for step in range(NEAR):
+        block = near_ref[0] ^ step
+        low = pl.multiple_of((block % 2) * 256, 256)
+        part = contract(gated, weight_refs[step][...], 0, 0).astype(BF16)
+        for a in range(FAR):
+            out_ref[2 * a + block // 2, :, pl.ds(low, 256)] = part[a * ROWS : (a + 1) * ROWS]
+        grad = contract(gated, cot_columns(cots_ref, block), 1, 0)
+        grad_refs[step][...] = grad.astype(grad_refs[step].dtype)
+
+
+def call(kernel, name, out_shape, interpret, *inputs, specs=None):
+    many = isinstance(out_shape, tuple)
+    outs = out_shape if many else (out_shape,)
+    in_specs = [whole(x.shape) for x in inputs]
+    for at, spec in (specs or {}).items():
+        in_specs[at] = spec
+    out_specs = tuple(whole(x.shape) for x in outs)
+    return pl.pallas_call(
+        kernel,
+        out_shape=out_shape,
+        grid=(1,),
+        in_specs=in_specs,
+        out_specs=out_specs if many else out_specs[0],
+        compiler_params=pltpu.CompilerParams(vmem_limit_bytes=VMEM_LIMIT),
+        cost_estimate=pl.CostEstimate(flops=1_000_000_000, transcendentals=0, bytes_accessed=2_000_000),
+        interpret=interpret,
+        name=name,
+    )(*inputs)
+
+
+SCALAR = pl.BlockSpec(memory_space=pltpu.SMEM)
+
+
+def pack(streams, long_filter, interpret=False):
+    shape = jax.ShapeDtypeStruct((SEQ, ROWS, 4 * LANE), BF16)
+    return call(pack_kernel, "pack", shape, interpret, streams, long_filter)
+
+
+def unpack(got, interpret=False):
+    shapes = (
+        jax.ShapeDtypeStruct((3, ROWS, COLS), BF16),
+        jax.ShapeDtypeStruct((ROWS, COLS), F32),
+    )
+    return call(unpack_kernel, "unpack", shapes, interpret, got)
+
+
+def to_send(near, gated, cots, weights, interpret=False):
+    shape = jax.ShapeDtypeStruct((SEQ, 2 * LANE, FAR * ROWS), BF16)
+    return call(send_kernel, "send", shape, interpret, near, gated, cots, *weights, specs={0: SCALAR})
+
+
+def products(near, got, cots, weights, interpret=False):
+    width = weights[0].shape[1]
+    shapes = (jax.ShapeDtypeStruct((CHAN, ROWS, COLS), BF16),) + tuple(
+        jax.ShapeDtypeStruct((COLS, width), BF16 if step else F32) for step in range(NEAR)
+    )
+    half = pl.BlockSpec((SEQ, LANE, FAR * ROWS), lambda _: (0, 0, 0))
+    return call(
+        product_kernel, "products", shapes, interpret, near, got, cots, *weights,
+        specs={0: SCALAR, 1: half},
+    )
+
+
 def shards(projected, short_filter, long_filter, w_out, d_out):
     seq_at = lax.axis_index("seq")
-    near_at = seq_at % NEAR
+    near = (seq_at % NEAR).astype(jnp.int32).reshape(1)
     consts = [jnp.asarray(table) for table in tables()]
 
     moved = swapped(d_out)
-
-    streams = jnp.concatenate([projected, long_filter.astype(BF16)[:, None, :]], axis=1)
-    packed = streams.reshape(ROWS, 4, SEQ, LANE).transpose(2, 0, 1, 3).reshape(SEQ, ROWS, 4 * LANE)
-    signals = exchange(packed, "seq").reshape(TOKENS, 4 * LANE)
-
+    signals = exchange(pack(projected.transpose(1, 0, 2), long_filter), "seq")
     cots = exchange(jnp.broadcast_to(moved[None], (CHAN, ROWS, COLS)), "chan")
-    cots = cots.reshape(FAR, 2, ROWS, COLS).transpose(0, 2, 1, 3).reshape(FAR * ROWS, 2 * COLS)
-
-    weights = jnp.zeros((NEAR,) + w_out.shape, BF16)
-    for step in range(NEAR):
-        piece = w_out if step == 0 else lax.ppermute(w_out, "seq", near_pairs(step))
-        weights = lax.dynamic_update_slice(weights, piece[None], (near_at ^ step, 0, 0))
-    weights = weights.transpose(1, 0, 2).reshape(COLS, NEAR * w_out.shape[1])
+    weights = [w_out] + [lax.ppermute(w_out, "seq", near_pairs(step)) for step in range(1, NEAR)]
 
     own = lax.dynamic_slice_in_dim(short_filter, seq_at * LANE, LANE, axis=2).reshape(3, 3 * LANE)
     plain = jnp.zeros((3, LANE), F32).at[0].set(1.0)
     taps = jnp.concatenate([own, plain], axis=1)
 
-    gated_send, kept, spec = convolve(signals, taps, consts)
-
-    part = lax.dot_general(
-        weights, cots, (((1,), (1,)), ((), ())), preferred_element_type=F32
-    ).astype(BF16)
-    gated_send = jnp.broadcast_to(
-        gated_send[None], (FAR, NEAR, LANE, FAR * ROWS)
-    ).reshape(SEQ, LANE, FAR * ROWS)
-    sent = jnp.concatenate([gated_send, part.reshape(SEQ, LANE, FAR * ROWS)], axis=1)
-    got = exchange(sent, "seq")
-    gated_cols = got[:, :LANE].reshape(COLS, FAR * ROWS)
-
-    partial_out = lax.dot_general(
-        gated_cols, weights, (((0,), (0,)), ((), ())), preferred_element_type=F32
-    ).astype(BF16)
-    partial_out = partial_out.reshape(FAR, ROWS, 2, COLS).transpose(0, 2, 1, 3)
-    shares = exchange(partial_out.reshape(CHAN, ROWS, COLS), "chan")
+    gated, kept, spec = convolve(signals.reshape(TOKENS, 4 * LANE), taps, consts)
+    got = exchange(to_send(near, gated, cots, weights), "seq")
+
+    partial_out, d_wout, *others = products(near, got, cots, weights)
+    shares = exchange(partial_out, "chan")
     output = swapped(jnp.sum(shares.astype(F32), axis=0).astype(BF16))
-
-    grad = jnp.dot(gated_cols, cots, preferred_element_type=F32)
-    grad = grad.reshape(COLS, NEAR, -1).transpose(1, 0, 2)
-    d_wout = lax.dynamic_index_in_dim(grad, near_at, 0, keepdims=False)
-    for step in range(1, NEAR):
-        piece = lax.dynamic_index_in_dim(grad, near_at ^ step, 0, keepdims=False).astype(BF16)
+    for step, piece in enumerate(others, 1):
         d_wout = d_wout + lax.ppermute(piece, "seq", near_pairs(step)).astype(F32)
 
-    d_signals = correlate(got, kept, spec, taps, consts)
-    returned = exchange(d_signals, "seq")
-    returned = returned.reshape(SEQ, ROWS, 4, LANE).transpose(1, 2, 0, 3).reshape(ROWS, 4, COLS)
-    return (output, returned[:, :3], d_wout, returned[:, 3].astype(F32))
+    returned = exchange(correlate(got, kept, spec, taps, consts), "seq")
+    d_projected, d_filter = unpack(returned)
+    return (output, d_projected.transpose(1, 0, 2), d_wout, d_filter)
 
 
 def solution(mesh):

time: 178 us -> 124 us (0.70)
  waiting for transfers between devices: 43.7 us -> 16.4 us
  Pallas kernels: 43.3 us -> 26.8 us
  local copies, waits for them, and re-layouts: 23.4 us -> 15.7 us
  matrix products: 5.08 us -> 0 us
  starting transfers between devices: 31.8 us -> 34 us
    ppermute x2, waiting for transfers between devices: 25.5 us -> 10.8 us  [swapped(): return lax.ppermute(array, ('seq', 'chan'), swap_pairs())]
    pallas_call x1, Pallas kernels: 22.9 us -> 10.3 us  [convolve(): pl.pallas_call(forward_kernel, out_shape=shapes, scratch_shapes=[pltpu.VM...]
    ppermute x3, waiting for transfers between devices: 12.2 us -> 0.01 us  [shards(): d_wout = d_wout + lax.ppermute(piece, 'seq', near_pairs(step)).astype(F32)]
    pallas_call x1, Pallas kernels: 20.4 us -> 10.9 us  [correlate(): pl.pallas_call(backward_kernel, out_shape=jax.ShapeDtypeStruct((SEQ, ROWS...]
    unnamed x37 -> x41, local copies, waits for them, and re-layouts: 8.63 us -> 14.5 us
    pallas_call x0 -> x4, Pallas kernels: none -> 5.63 us  [call(): pl.pallas_call(kernel, out_shape=out_shape, grid=(1,), in_specs=in_specs,...]
    dot_general x3 -> x0, matrix products: 5.08 us -> none  [the longest x1 2.36 us: shards(): lax.dot_general(weights, cots, (((1,), (1,)), ((), ())), preferred_elemen...]
    transpose x3 -> x0, local copies, waits for them, and re-layouts: 3.19 us -> none  [the longest x1 2.3 us: shards(): cots.reshape(FAR, 2, ROWS, COLS).transpose(0, 2, 1, 3)]
  transfers between devices with their start and end apart: 12 -> 12, of which waited for: 5 -> 3; matrix products, arithmetic and copies ran while one was open for 10% -> 3% of each run, Pallas kernels for 13% -> 18%
where the time goes in v1:
time: 124 us; the launch traced here: 122 us
  starting transfers between devices  34 us (27%)
  Pallas kernels  26.8 us (22%)
  blocking collectives  26.1 us (21%)
  waiting for transfers between devices  16.4 us (13%)
  local copies, waits for them, and re-layouts  15.7 us (13%)
  other arithmetic  2.37 us (2%)
    all_to_all x1, blocking collectives, exchange(): return lax.all_to_all(array, axis, 0, 0, tiled=True)  26.1 us
    all_to_all x4, starting transfers between devices, exchange(): return lax.all_to_all(array, axis, 0, 0, tiled=True)  20.5 us
    unnamed x41, local copies, waits for them, and re-layouts  14.5 us
    pallas_call x1, Pallas kernels, correlate(): pl.pallas_call(backward_kernel, out_shape=jax.ShapeDtypeStruct((SEQ, ROWS...  10.9 us
    ppermute x2, waiting for transfers between devices, swapped(): return lax.ppermute(array, ('seq', 'chan'), swap_pairs())  10.8 us
    pallas_call x1, Pallas kernels, convolve(): pl.pallas_call(forward_kernel, out_shape=shapes, scratch_shapes=[pltpu.VM...  10.3 us
    ppermute x2, starting transfers between devices, swapped(): return lax.ppermute(array, ('seq', 'chan'), swap_pairs())  9.76 us
    pallas_call x4, Pallas kernels, call(): pl.pallas_call(kernel, out_shape=out_shape, grid=(1,), in_specs=in_specs,...  5.63 us
  transfers between devices with their start and end apart: 12, of which 3 were waited for; matrix products, arithmetic and copies ran while one was open for 3% of the time, Pallas kernels for 18%

profile of v1, /device:TPU:32, one launch (start us, length us, event | category | flops | bytes accessed | tf_op | source)
XLA Modules:
  0.0 122.2 jit_solution(17246276267780469744)
XLA Ops:
  0.7 1.0 copy-done.1
  1.7 0.9 copy-done.2
  2.6 1.3 %pack.1 = bf16[16,128,128]{2,1,0:T(8,128)(2,1)} custom-call(bf16[3,128,512]{2,1,0:T(8,128)(2,1)S(1)} %bitcast.5, f32[128,512]{1,0:T(8,128)S(1)} %copy-done.2), custom_call_target="tpu_custom_call" | custom-call | flops 1000000000 | bytes 2000000 | tf_op jit(solution)/shard_map/pack/pallas_call | solution.py:391
  3.9 7.2 %all-to-all-start = ((bf16[16,128,128]{2,1,0:T(8,128)(2,1)}), bf16[16,128,128]{2,1,0:T(8,128)(2,1)S(1)}, u32[]{:S(2)}, u32[]{:S(2)}) async-start(bf16[16,128,128]{2,1,0:T(8,128)(2,1)} %pack.1), calls=%async_computation | async-start | bytes 1048576 | tf_op jit(solution)/shard_map/all_to_all | solution.py:55
  11.1 4.9 %collective-permute-start = (bf16[128,512]{1,0:T(8,128)(2,1)S(1)}, bf16[128,512]{1,0:T(8,128)(2,1)S(1)}, u32[]{:S(2)}, u32[]{:S(2)}) collective-permute-start(bf16[128,512]{1,0:T(8,128)(2,1)S(1)} %copy-done.19), channel_id=1, source_target_pairs={{0,0},{1,1},{2,32},{3,33},{4,64},{5,65},{6,96},{7,97},{8,8},{9,9},... | collective-permute-start | bytes 393224 | tf_op jit(solution)/shard_map/ppermute | solution.py:47
  16.1 1.5 %collective-permute-start.2 = (bf16[512,256]{1,0:T(8,128)(2,1)S(1)}, bf16[512,256]{1,0:T(8,128)(2,1)S(1)}, u32[]{:S(2)}, u32[]{:S(2)}) collective-permute-start(bf16[512,256]{1,0:T(8,128)(2,1)S(1)} %copy-done.3), channel_id=1, source_target_pairs={{0,16},{8,24},{16,0},{24,8},{32,48},{40,56},{48,32},{56,40},{64,80... | collective-permute-start | bytes 786440 | tf_op jit(solution)/shard_map/ppermute | solution.py:445
  17.9 8.7 %collective-permute-done = bf16[128,512]{1,0:T(8,128)(2,1)S(1)} collective-permute-done((bf16[128,512]{1,0:T(8,128)(2,1)S(1)}, bf16[128,512]{1,0:T(8,128)(2,1)S(1)}, u32[]{:S(2)}, u32[]{:S(2)}) %collective-permute-start) | collective-permute-done | bytes 131104 | tf_op jit(solution)/shard_map/ppermute | solution.py:47
  26.7 1.1 broadcast_in_dim.2
  27.7 4.1 %all-to-all-start.1 = ((bf16[8,128,512]{2,1,0:T(8,128)(2,1)}), bf16[8,128,512]{2,1,0:T(8,128)(2,1)S(1)}, u32[]{:S(2)}, u32[]{:S(2)}) async-start(bf16[8,128,512]{2,1,0:T(8,128)(2,1)} %broadcast_in_dim.2), calls=%async_computation.1 | async-start | bytes 2097152 | tf_op jit(solution)/shard_map/all_to_all | solution.py:55
  32.0 1.3 %copy-done.9 = bf16[64,72,96]{2,1,0:T(8,128)(2,1)S(1)} copy-done((bf16[64,72,96]{2,1,0:T(8,128)(2,1)S(1)}, bf16[64,72,96]{2,1,0:T(8,128)(2,1)}, u32[]{:S(2)}) %copy-start.9) | copy-done | bytes 884760
  33.3 1.2 %copy-done.11 = bf16[64,32,240]{2,1,0:T(8,128)(2,1)S(1)} copy-done((bf16[64,32,240]{2,1,0:T(8,128)(2,1)S(1)}, bf16[64,32,240]{2,1,0:T(8,128)(2,1)}, u32[]{:S(2)}) %copy-start.11) | copy-done | bytes 983064
  34.5 10.3 %convolve.1 = (bf16[4,32,512]{2,1,0:T(8,128)(2,1)S(1)}, f32[2048,128]{1,0:T(8,128)S(1)}, f32[33,128,128]{2,1,0:T(8,128)}) custom-call(bf16[2048,128]{1,0:T(8,128)(2,1)S(1)} %bitcast.4, f32[3,128]{1,0:T(4,128)S(1)} %pad_maximum_fusion.taps_ref, bf16[64,72,96]{2,1,0:T(8,128)(2,1)S(1)} %copy-done.9, bf16[128,384]{1,0:T(8,128)(2,1)S(1)} %copy-done.14, ...), custom_call_target="tpu_custom_call" | custom-call | flops 8000000000 | bytes 6000000 | tf_op jit(solution)/shard_map/convolve/pallas_call | solution.py:276
  44.8 1.0 copy-done.16
  45.8 0.8 send.1
  47.3 26.1 %all_to_all.25.got_ref.share_ref = bf16[16,64,512]{2,1,0:T(8,128)(2,1)S(1)} all-to-all(bf16[16,64,512]{2,1,0:T(8,128)(2,1)S(1)} %send.1), channel_id=1, replica_groups=mesh['seq'=16,'chan'=8] {'seq'}, dimensions={0} | all-to-all | bytes 2097152 | tf_op jit(solution)/shard_map/all_to_all | solution.py:55
  73.4 0.9 copy-done.5
  74.3 2.3 %products.1 = (bf16[8,128,512]{2,1,0:T(8,128)(2,1)}, f32[512,256]{1,0:T(8,128)S(1)}, bf16[512,256]{1,0:T(8,128)(2,1)S(1)}, bf16[512,256]{1,0:T(8,128)(2,1)S(1)}, bf16[512,256]{1,0:T(8,128)(2,1)S(1)}) custom-call(s32[1]{0:T(128)} %bitcast.near_ref, bf16[16,64,512]{2,1,0:T(8,128)(2,1)S(1)} %all_to_all.25.got_ref.share_ref, ...), custom_call_target="tpu_custom_call" | custom-call | flops 1000000000 | bytes 2000000 | tf_op jit(solution)/shard_map/products/pallas_call | solution.py:391
  76.6 0.7 copy-done.6
  78.7 5.7 %all-to-all-start.3 = ((bf16[8,128,512]{2,1,0:T(8,128)(2,1)}), bf16[8,128,512]{2,1,0:T(8,128)(2,1)}, u32[]{:S(2)}, u32[]{:S(2)}) async-start(bf16[8,128,512]{2,1,0:T(8,128)(2,1)} %get-tuple-element.27), calls=%async_computation.3 | async-start | bytes 2097152 | tf_op jit(solution)/shard_map/all_to_all | solution.py:55
  84.4 1.9 %collective-permute-start.7 = (bf16[512,256]{1,0:T(8,128)(2,1)}, bf16[512,256]{1,0:T(8,128)(2,1)S(1)}, u32[]{:S(2)}, u32[]{:S(2)}) collective-permute-start(bf16[512,256]{1,0:T(8,128)(2,1)} %copy-done.6), channel_id=1, source_target_pairs={{0,24},{8,16},{16,8},{24,0},{32,56},{40,48},{48,40},{56,32},{64,88... | collective-permute-start | bytes 786440 | tf_op jit(solution)/shard_map/ppermute | solution.py:458
  86.3 1.3 %copy-done.10 = bf16[64,72,96]{2,1,0:T(8,128)(2,1)S(1)} copy-done((bf16[64,72,96]{2,1,0:T(8,128)(2,1)S(1)}, bf16[64,72,96]{2,1,0:T(8,128)(2,1)}, u32[]{:S(2)}) %copy-start.10) | copy-done | bytes 884760
  87.5 1.2 %copy-done.12 = bf16[64,32,240]{2,1,0:T(8,128)(2,1)S(1)} copy-done((bf16[64,32,240]{2,1,0:T(8,128)(2,1)S(1)}, bf16[64,32,240]{2,1,0:T(8,128)(2,1)}, u32[]{:S(2)}) %copy-start.12) | copy-done | bytes 983064
  88.8 0.9 copy-done.15
  89.7 1.2 %copy-done.17 = f32[2048,128]{1,0:T(8,128)S(1)} copy-done((f32[2048,128]{1,0:T(8,128)S(1)}, f32[2048,128]{1,0:T(8,128)}, u32[]{:S(2)}) %copy-start.17) | copy-done | bytes 1048600
  90.9 10.9 %correlate.1 = bf16[16,128,128]{2,1,0:T(8,128)(2,1)} custom-call(bf16[16,64,512]{2,1,0:T(8,128)(2,1)S(1)} %all_to_all.25.got_ref.share_ref, f32[2048,128]{1,0:T(8,128)S(1)} %copy-done.17, f32[33,128,128]{2,1,0:T(8,128)} %get-tuple-element.29.spec_ref, f32[3,128]{1,0:T(4,128)S(1)} %pad_maximum_fusion.taps_ref, bf16[64,72,96]{2,1,0:T(8,128)(2,1)S(1)} %copy-done.10, ...), custom_call_target="tpu_custom_call" | custom-call | flops 8000000000 | bytes 6000000 | tf_op jit(solution)/shard_map/correlate/pallas_call | solution.py:296
  101.8 3.6 %all-to-all-start.4 = ((bf16[16,128,128]{2,1,0:T(8,128)(2,1)}), bf16[16,128,128]{2,1,0:T(8,128)(2,1)S(1)}, u32[]{:S(2)}, u32[]{:S(2)}) async-start(bf16[16,128,128]{2,1,0:T(8,128)(2,1)} %correlate.1), calls=%async_computation.4 | async-start | bytes 1048576 | tf_op jit(solution)/shard_map/all_to_all | solution.py:55
  105.4 1.4 %reduce_sum.12 = bf16[128,512]{1,0:T(8,128)(2,1)S(1)} reduce(bf16[8,128,512]{2,1,0:T(8,128)(2,1)} %all-to-all-done.3, bf16[]{:T(256)} %constant.65.clone.1), dimensions={0}, to_apply=%region_0.1 | reduce | flops 458752 | bytes 1179650 | tf_op jit(solution)/shard_map/reduce_sum | solution.py:456
  106.8 4.9 %collective-permute-start.4 = (bf16[128,512]{1,0:T(8,128)(2,1)S(1)}, bf16[128,512]{1,0:T(8,128)(2,1)S(1)}, u32[]{:S(2)}, u32[]{:S(2)}) collective-permute-start(bf16[128,512]{1,0:T(8,128)(2,1)S(1)} %reduce_sum.12), channel_id=1, source_target_pairs={{0,0},{1,1},{2,32},{3,33},{4,64},{5,65},{6,96},{7,97},{8,8},{9,9},... | collective-permute-start | bytes 393224 | tf_op jit(solution)/shard_map/ppermute | solution.py:47
  111.7 0.9 convert_add_fusion
  112.6 5.6 %all-to-all-done.4.got_ref = bf16[16,128,128]{2,1,0:T(8,128)(2,1)S(1)} async-done(((bf16[16,128,128]{2,1,0:T(8,128)(2,1)}), bf16[16,128,128]{2,1,0:T(8,128)(2,1)S(1)}, u32[]{:S(2)}, u32[]{:S(2)}) %all-to-all-start.4) | async-done | bytes 524320 | tf_op jit(solution)/shard_map/all_to_all | solution.py:55
  118.2 1.3 %unpack.1 = (bf16[3,128,512]{2,1,0:T(8,128)(2,1)}, f32[128,512]{1,0:T(8,128)}) custom-call(bf16[16,128,128]{2,1,0:T(8,128)(2,1)S(1)} %all-to-all-done.4.got_ref), custom_call_target="tpu_custom_call" | custom-call | flops 1000000000 | bytes 2000000 | tf_op jit(solution)/shard_map/unpack/pallas_call | solution.py:391
  119.5 2.0 %collective-permute-done.4 = bf16[128,512]{1,0:T(8,128)(2,1)S(1)} collective-permute-done((bf16[128,512]{1,0:T(8,128)(2,1)S(1)}, bf16[128,512]{1,0:T(8,128)(2,1)S(1)}, u32[]{:S(2)}, u32[]{:S(2)}) %collective-permute-start.4) | collective-permute-done | bytes 131104 | tf_op jit(solution)/shard_map/ppermute | solution.py:47
  (46 shorter events, 3.5 us)
Async XLA Ops:
  0.6 31.2 %copy-start = (f32[3,3,512]{2,1,0:T(4,128)S(1)}, f32[3,3,512]{2,1,0:T(4,128)}, u32[]{:S(2)}) copy-start(f32[3,3,512]{2,1,0:T(4,128)} %param.12) | copy-start | bytes 55300
  0.6 1.0 copy-start.1
  1.6 0.9 copy-start.2
  2.6 8.5 %copy-start.19 = (bf16[128,512]{1,0:T(8,128)(2,1)S(1)}, bf16[128,512]{1,0:T(8,128)(2,1)}, u32[]{:S(2)}) copy-start(bf16[128,512]{1,0:T(8,128)(2,1)} %param.15) | copy-start | bytes 393220
  2.6 13.4 %copy-start.3 = (bf16[512,256]{1,0:T(8,128)(2,1)S(1)}, bf16[512,256]{1,0:T(8,128)(2,1)}, u32[]{:S(2)}) copy-start(bf16[512,256]{1,0:T(8,128)(2,1)} %refs_0_.3) | copy-start | bytes 786436
  3.9 28.1 %copy-start.18 = (f32[3,32]{1,0:T(4,128)S(1)}, f32[3,32]{1,0:T(4,128)}, u32[]{:S(2)}) copy-start(f32[3,32]{1,0:T(4,128)} %constant.64.clone.1) | copy-start | bytes 1156
  3.9 28.1 %copy-start.13 = (bf16[128,384]{1,0:T(8,128)(2,1)S(1)}, bf16[128,384]{1,0:T(8,128)(2,1)}, u32[]{:S(2)}) copy-start(bf16[128,384]{1,0:T(8,128)(2,1)} %constant.68.clone.behind_ref) | copy-start | bytes 294916
  3.9 28.1 %copy-start.14 = (bf16[128,384]{1,0:T(8,128)(2,1)S(1)}, bf16[128,384]{1,0:T(8,128)(2,1)}, u32[]{:S(2)}) copy-start(bf16[128,384]{1,0:T(8,128)(2,1)} %constant.67.clone.ahead_ref) | copy-start | bytes 294916
  3.9 22.8 %all-to-all-start = ((bf16[16,128,128]{2,1,0:T(8,128)(2,1)}), bf16[16,128,128]{2,1,0:T(8,128)(2,1)S(1)}, u32[]{:S(2)}, u32[]{:S(2)}) async-start(bf16[16,128,128]{2,1,0:T(8,128)(2,1)} %pack.1), calls=%async_computation | async-start | bytes 1048576 | tf_op jit(solution)/shard_map/all_to_all | solution.py:55
  11.1 15.6 %collective-permute-start = (bf16[128,512]{1,0:T(8,128)(2,1)S(1)}, bf16[128,512]{1,0:T(8,128)(2,1)S(1)}, u32[]{:S(2)}, u32[]{:S(2)}) collective-permute-start(bf16[128,512]{1,0:T(8,128)(2,1)S(1)} %copy-done.19), channel_id=1, source_target_pairs={{0,0},{1,1},{2,32},{3,33},{4,64},{5,65},{6,96},{7,97},{8,8},{9,9},... | collective-permute-start | bytes 393224 | tf_op jit(solution)/shard_map/ppermute | solution.py:47
  16.0 29.8 %collective-permute-start.3 = (bf16[512,256]{1,0:T(8,128)(2,1)S(1)}, bf16[512,256]{1,0:T(8,128)(2,1)S(1)}, u32[]{:S(2)}, u32[]{:S(2)}) collective-permute-start(bf16[512,256]{1,0:T(8,128)(2,1)S(1)} %copy-done.3), channel_id=1, source_target_pairs={{0,24},{8,16},{16,8},{24,0},{32,56},{40,48},{48,40},{56,32},{64,88... | collective-permute-start | bytes 786440 | tf_op jit(solution)/shard_map/ppermute | solution.py:445
  16.1 29.7 %collective-permute-start.2 = (bf16[512,256]{1,0:T(8,128)(2,1)S(1)}, bf16[512,256]{1,0:T(8,128)(2,1)S(1)}, u32[]{:S(2)}, u32[]{:S(2)}) collective-permute-start(bf16[512,256]{1,0:T(8,128)(2,1)S(1)} %copy-done.3), channel_id=1, source_target_pairs={{0,16},{8,24},{16,0},{24,8},{32,48},{40,56},{48,32},{56,40},{64,80... | collective-permute-start | bytes 786440 | tf_op jit(solution)/shard_map/ppermute | solution.py:445
  17.6 28.3 %collective-permute-start.1 = (bf16[512,256]{1,0:T(8,128)(2,1)S(1)}, bf16[512,256]{1,0:T(8,128)(2,1)S(1)}, u32[]{:S(2)}, u32[]{:S(2)}) collective-permute-start(bf16[512,256]{1,0:T(8,128)(2,1)S(1)} %copy-done.3), channel_id=1, source_target_pairs={{0,8},{8,0},{16,24},{24,16},{32,40},{40,32},{48,56},{56,48},{64,72... | collective-permute-start | bytes 786440 | tf_op jit(solution)/shard_map/ppermute | solution.py:445
  27.7 18.1 %all-to-all-start.1 = ((bf16[8,128,512]{2,1,0:T(8,128)(2,1)}), bf16[8,128,512]{2,1,0:T(8,128)(2,1)S(1)}, u32[]{:S(2)}, u32[]{:S(2)}) async-start(bf16[8,128,512]{2,1,0:T(8,128)(2,1)} %broadcast_in_dim.2), calls=%async_computation.1 | async-start | bytes 2097152 | tf_op jit(solution)/shard_map/all_to_all | solution.py:55
  32.0 1.3 %copy-start.9 = (bf16[64,72,96]{2,1,0:T(8,128)(2,1)S(1)}, bf16[64,72,96]{2,1,0:T(8,128)(2,1)}, u32[]{:S(2)}) copy-start(bf16[64,72,96]{2,1,0:T(8,128)(2,1)} %constant.66.clone.first_ref) | copy-start | bytes 2654212
  33.3 1.2 %copy-start.11 = (bf16[64,32,240]{2,1,0:T(8,128)(2,1)S(1)}, bf16[64,32,240]{2,1,0:T(8,128)(2,1)}, u32[]{:S(2)}) copy-start(bf16[64,32,240]{2,1,0:T(8,128)(2,1)} %constant.69.clone.last_ref) | copy-start | bytes 2949124
  44.8 1.0 copy-start.16
  46.6 0.7 copy-start.4
  73.4 1.0 copy-start.5
  76.6 0.7 copy-start.6
  77.3 0.7 copy-start.7
  78.0 0.7 copy-start.8
  78.7 23.1 %all-to-all-start.3 = ((bf16[8,128,512]{2,1,0:T(8,128)(2,1)}), bf16[8,128,512]{2,1,0:T(8,128)(2,1)}, u32[]{:S(2)}, u32[]{:S(2)}) async-start(bf16[8,128,512]{2,1,0:T(8,128)(2,1)} %get-tuple-element.27), calls=%async_computation.3 | async-start | bytes 2097152 | tf_op jit(solution)/shard_map/all_to_all | solution.py:55
  84.4 27.3 %collective-permute-start.5 = (bf16[512,256]{1,0:T(8,128)(2,1)}, bf16[512,256]{1,0:T(8,128)(2,1)S(1)}, u32[]{:S(2)}, u32[]{:S(2)}) collective-permute-start(bf16[512,256]{1,0:T(8,128)(2,1)} %copy-done.8), channel_id=1, source_target_pairs={{0,8},{8,0},{16,24},{24,16},{32,40},{40,32},{48,56},{56,48},{64,72... | collective-permute-start | bytes 786440 | tf_op jit(solution)/shard_map/ppermute | solution.py:458
  84.4 27.3 %collective-permute-start.6 = (bf16[512,256]{1,0:T(8,128)(2,1)}, bf16[512,256]{1,0:T(8,128)(2,1)S(1)}, u32[]{:S(2)}, u32[]{:S(2)}) collective-permute-start(bf16[512,256]{1,0:T(8,128)(2,1)} %copy-done.7), channel_id=1, source_target_pairs={{0,16},{8,24},{16,0},{24,8},{32,48},{40,56},{48,32},{56,40},{64,80... | collective-permute-start | bytes 786440 | tf_op jit(solution)/shard_map/ppermute | solution.py:458
  84.4 27.3 %collective-permute-start.7 = (bf16[512,256]{1,0:T(8,128)(2,1)}, bf16[512,256]{1,0:T(8,128)(2,1)S(1)}, u32[]{:S(2)}, u32[]{:S(2)}) collective-permute-start(bf16[512,256]{1,0:T(8,128)(2,1)} %copy-done.6), channel_id=1, source_target_pairs={{0,24},{8,16},{16,8},{24,0},{32,56},{40,48},{48,40},{56,32},{64,88... | collective-permute-start | bytes 786440 | tf_op jit(solution)/shard_map/ppermute | solution.py:458
  86.3 1.3 %copy-start.10 = (bf16[64,72,96]{2,1,0:T(8,128)(2,1)S(1)}, bf16[64,72,96]{2,1,0:T(8,128)(2,1)}, u32[]{:S(2)}) copy-start(bf16[64,72,96]{2,1,0:T(8,128)(2,1)} %constant.66.clone.first_ref) | copy-start | bytes 2654212
  87.5 1.2 %copy-start.12 = (bf16[64,32,240]{2,1,0:T(8,128)(2,1)S(1)}, bf16[64,32,240]{2,1,0:T(8,128)(2,1)}, u32[]{:S(2)}) copy-start(bf16[64,32,240]{2,1,0:T(8,128)(2,1)} %constant.69.clone.last_ref) | copy-start | bytes 2949124
  88.8 0.9 copy-start.15
  89.7 1.2 %copy-start.17 = (f32[2048,128]{1,0:T(8,128)S(1)}, f32[2048,128]{1,0:T(8,128)}, u32[]{:S(2)}) copy-start(f32[2048,128]{1,0:T(8,128)} %copy-done.16) | copy-start | bytes 3145732
  101.8 16.4 %all-to-all-start.4 = ((bf16[16,128,128]{2,1,0:T(8,128)(2,1)}), bf16[16,128,128]{2,1,0:T(8,128)(2,1)S(1)}, u32[]{:S(2)}, u32[]{:S(2)}) async-start(bf16[16,128,128]{2,1,0:T(8,128)(2,1)} %correlate.1), calls=%async_computation.4 | async-start | bytes 1048576 | tf_op jit(solution)/shard_map/all_to_all | solution.py:55
  106.8 14.8 %collective-permute-start.4 = (bf16[128,512]{1,0:T(8,128)(2,1)S(1)}, bf16[128,512]{1,0:T(8,128)(2,1)S(1)}, u32[]{:S(2)}, u32[]{:S(2)}) collective-permute-start(bf16[128,512]{1,0:T(8,128)(2,1)S(1)} %reduce_sum.12), channel_id=1, source_target_pairs={{0,0},{1,1},{2,32},{3,33},{4,64},{5,65},{6,96},{7,97},{8,8},{9,9},... | collective-permute-start | bytes 393224 | tf_op jit(solution)/shard_map/ppermute | solution.py:47

commit v2 on v1

--- a/solution.py
+++ b/solution.py
@@ -49,6 +49,10 @@
 
 def near_pairs(step):
     return [(i, i ^ step) for i in range(SEQ)]
+
+
+def chan_pairs(step):
+    return [(i, i ^ step) for i in range(CHAN)]
 
 
 def exchange(array, axis):
@@ -128,11 +132,22 @@
         ]
 
 
+def started(source, target, sem):
+    copy = pltpu.make_async_copy(source, target, sem)
+    copy.start()
+    return copy
+
+
 def forward_kernel(
-    signal_ref, taps_ref, first_ref, ahead_ref, behind_ref, last_ref,
-    gated_ref, kept_ref, spec_ref,
+    signal_ref, taps_ref, first_hbm, ahead_hbm, behind_hbm, last_hbm,
+    gated_ref, kept_hbm, spec_hbm,
     wide_ref, mid_ref, back_ref, column_ref,
+    first_ref, ahead_ref, behind_ref, last_ref, kept_ref, spec_ref, sems,
 ):
+    first_copy = started(first_hbm, first_ref, sems.at[0])
+    ahead_copy = started(ahead_hbm, ahead_ref, sems.at[1])
+    behind_copy = started(behind_hbm, behind_ref, sems.at[2])
+    last_copy = started(last_hbm, last_ref, sems.at[3])
     wide_ref[0:8, :] = jnp.zeros((8, 4 * LANE), F32)
     wide_ref[8:, :] = signal_ref[...].astype(F32)
     back_ref[2 * HALF * 64 :, :] = jnp.zeros(((BACK - 2 * HALF) * 64, 4 * LANE), F32)
@@ -149,6 +164,7 @@
         data = jnp.where((lane >= 2 * LANE) & (lane < 3 * LANE), carried, mixed)
         mid_ref[pl.ds(pl.multiple_of(n2 * MID, 8), MID), :] = matmul(first_ref[n2], pieces(data))
 
+    first_copy.wait()
     every(64, WIDE, outer)
 
     def inner(group):
@@ -166,7 +182,10 @@
             )
         behind_rows(back_ref, group * GROUP, behind_ref, products)
 
+    ahead_copy.wait()
+    behind_copy.wait()
     every(HALF // GROUP, 1, inner)
+    spec_copy = started(spec_ref, spec_hbm, sems.at[4])
 
     def final(n2):
         conv = matmul(last_ref[n2], pieces(back_ref[pl.ds(n2, BACK, stride=64), :]))
@@ -176,19 +195,30 @@
             lane < 3 * LANE, mixed, pltpu.roll(conv, LANE, 1)
         )
 
+    last_copy.wait()
     every(64, WIDE, final)
+    kept_copy = started(kept_ref, kept_hbm, sems.at[5])
 
     for block in range(SEQ):
         a, i = divmod(block, NEAR)
         turned = column_ref[block * ROWS : (block + 1) * ROWS, :].T
         gated_ref[i, :, a * ROWS : (a + 1) * ROWS] = turned[:LANE].astype(BF16)
+    spec_copy.wait()
+    kept_copy.wait()
 
 
 def backward_kernel(
-    share_ref, kept_ref, spec_ref, taps_ref, first_ref, ahead_ref, behind_ref, last_ref,
+    share_ref, kept_hbm, spec_hbm, taps_ref, first_hbm, ahead_hbm, behind_hbm, last_hbm,
     out_ref,
     grad_ref, mid_ref, back_ref, column_ref,
+    first_ref, ahead_ref, behind_ref, last_ref, kept_ref, spec_ref, sems,
 ):
+    first_copy = started(first_hbm, first_ref, sems.at[0])
+    kept_copy = started(kept_hbm, kept_ref, sems.at[5])
+    ahead_copy = started(ahead_hbm, ahead_ref, sems.at[1])
+    behind_copy = started(behind_hbm, behind_ref, sems.at[2])
+    spec_copy = started(spec_hbm, spec_ref, sems.at[4])
+    last_copy = started(last_hbm, last_ref, sems.at[3])
     back_ref[2 * HALF * 64 :, :] = jnp.zeros(((BACK - 2 * HALF) * 64, 4 * LANE), F32)
     column_ref[TOKENS:, :] = jnp.zeros((8, 4 * LANE), F32)
     for i in range(NEAR):
@@ -207,6 +237,8 @@
         data = grad_ref[pl.ds(n2, 32, stride=64), :] * query
         mid_ref[pl.ds(pl.multiple_of(n2 * MID, 8), MID), :] = matmul(first_ref[n2], pieces(data))
 
+    first_copy.wait()
+    kept_copy.wait()
     every(64, WIDE, outer)
 
     wide = lanes_of(128)
@@ -228,6 +260,9 @@
             )
         behind_rows(back_ref, group * GROUP, behind_ref, products)
 
+    ahead_copy.wait()
+    behind_copy.wait()
+    spec_copy.wait()
     every(HALF // GROUP, 1, inner)
 
     def final(n2):
@@ -246,6 +281,7 @@
         )
         column_ref[pl.ds(n2, 32, stride=64), :] = mixed
 
+    last_copy.wait()
     every(64, WIDE, final)
 
     tap0, tap1, tap2 = (
@@ -267,49 +303,67 @@
     return pl.BlockSpec(shape, lambda _: (0,) * len(shape))
 
 
+HELD = (
+    pltpu.VMEM((64, MID, 96), BF16),
+    pltpu.VMEM((128, 384), BF16),
+    pltpu.VMEM((128, 384), BF16),
+    pltpu.VMEM((64, 32, 3 * BACK), BF16),
+    pltpu.VMEM((TOKENS, 4 * LANE), F32),
+    pltpu.VMEM((HALF, 128, 4 * LANE), F32),
+    pltpu.SemaphoreType.DMA((6,)),
+)
+FAR_OFF = pl.BlockSpec(memory_space=pltpu.HBM)
+
+
+def resident(array):
+    return pltpu.with_memory_space_constraint(array, pltpu.HBM)
+
+
 def convolve(signals, taps, consts, interpret=False):
-    shapes = (
-        jax.ShapeDtypeStruct((NEAR, LANE, FAR * ROWS), BF16),
-        jax.ShapeDtypeStruct((TOKENS, 4 * LANE), F32),
-        jax.ShapeDtypeStruct((HALF, 128, 4 * LANE), F32),
-    )
     return pl.pallas_call(
         forward_kernel,
-        out_shape=shapes,
+        out_shape=(
+            jax.ShapeDtypeStruct((NEAR, LANE, FAR * ROWS), BF16),
+            pltpu.HBM((TOKENS, 4 * LANE), F32),
+            pltpu.HBM((HALF, 128, 4 * LANE), F32),
+        ),
+        grid=(1,),
+        in_specs=[whole(signals.shape), whole(taps.shape)] + [FAR_OFF] * 4,
+        out_specs=(whole((NEAR, LANE, FAR * ROWS)), FAR_OFF, FAR_OFF),
         scratch_shapes=[
             pltpu.VMEM((TOKENS + 8, 4 * LANE), F32),
             pltpu.VMEM((64 * MID, 4 * LANE), F32),
             pltpu.VMEM((64 * BACK, 4 * LANE), F32),
             pltpu.VMEM((TOKENS, 4 * LANE), F32),
+            *HELD,
         ],
         compiler_params=pltpu.CompilerParams(vmem_limit_bytes=VMEM_LIMIT),
         cost_estimate=LONG,
         interpret=interpret,
         name="convolve",
-    )(signals, taps, *consts)
+    )(signals, taps, *(resident(x) for x in consts))
 
 
 def correlate(shares, kept, spec, taps, consts, interpret=False):
-    inputs = (shares, kept, spec, taps) + tuple(consts)
-    specs = [whole(x.shape) for x in inputs]
-    specs[0] = pl.BlockSpec((SEQ, LANE, FAR * ROWS), lambda _: (0, 1, 0))
+    half = pl.BlockSpec((SEQ, LANE, FAR * ROWS), lambda _: (0, 1, 0))
     return pl.pallas_call(
         backward_kernel,
         out_shape=jax.ShapeDtypeStruct((SEQ, ROWS, 4 * LANE), BF16),
         grid=(1,),
-        in_specs=specs,
+        in_specs=[half, FAR_OFF, FAR_OFF, whole(taps.shape)] + [FAR_OFF] * 4,
         out_specs=whole((SEQ, ROWS, 4 * LANE)),
         scratch_shapes=[
             pltpu.VMEM((TOKENS, 4 * LANE), F32),
             pltpu.VMEM((64 * MID, 4 * LANE), F32),
             pltpu.VMEM((64 * BACK, 4 * LANE), F32),
             pltpu.VMEM((TOKENS + 8, 4 * LANE), F32),
+            *HELD,
         ],
         compiler_params=pltpu.CompilerParams(vmem_limit_bytes=VMEM_LIMIT),
         cost_estimate=LONG,
         interpret=interpret,
         name="correlate",
-    )(*inputs)
+    )(shares, resident(kept), resident(spec), taps, *(resident(x) for x in consts))
 
 
 def pack_kernel(streams_ref, filter_ref, out_ref):
@@ -343,45 +397,62 @@
                 filter_ref[:, at] = joined
 
 
-def cot_columns(cots_ref, block):
-    low = pl.multiple_of((block % 2) * 256, 256)
-    return jnp.concatenate(
-        [cots_ref[2 * a + block // 2, :, pl.ds(low, 256)] for a in range(FAR)], axis=0
-    )
-
-
 def contract(left, right, left_dim, right_dim):
     return lax.dot_general(
         left, right, (((left_dim,), (right_dim,)), ((), ())), preferred_element_type=F32
     )
 
 
-def send_kernel(near_ref, gated_ref, cots_ref, *refs):
-    weight_refs, sent_ref = refs[:NEAR], refs[NEAR]
-    total = None
+def fetch(place_ref, refs, weights, cots, sems):
+    copies = []
     for step in range(NEAR):
-        term = contract(weight_refs[step][...], cot_columns(cots_ref, near_ref[0] ^ step), 1, 1)
-        total = term if total is None else total + term
-    total = total.astype(BF16)
+        low = pl.multiple_of((place_ref[0] ^ step) * 256, 256)
+        copies.append(started(refs[step], weights.at[:, pl.ds(low, 256)], sems.at[step]))
+    for far in range(FAR):
+        row = pl.multiple_of((place_ref[1] ^ far) * ROWS, ROWS)
+        for side in range(2):
+            low = pl.multiple_of((place_ref[2] ^ side) * COLS, COLS)
+            copies.append(
+                started(
+                    refs[NEAR + far].at[side],
+                    cots.at[pl.ds(row, ROWS), pl.ds(low, COLS)],
+                    sems.at[NEAR + 2 * far + side],
+                )
+            )
+    return copies
+
+
+def send_kernel(place_ref, gated_ref, *refs):
+    sent_ref, weights, cots, sems = refs[NEAR + FAR :]
+    copies = fetch(place_ref, refs, weights, cots, sems)
     for s in range(SEQ):
         sent_ref[s, :LANE, :] = gated_ref[s % NEAR]
+    for copy in copies:
+        copy.wait()
+    total = contract(weights[...], cots[...], 1, 1).astype(BF16)
+    for s in range(SEQ):
         sent_ref[s, LANE:, :] = total[s * LANE : (s + 1) * LANE]
 
 
-def product_kernel(near_ref, got_ref, cots_ref, *refs):
-    weight_refs, out_ref, grad_refs = refs[:NEAR], refs[NEAR], refs[NEAR + 1 :]
+def product_kernel(place_ref, got_ref, *refs):
+    out_ref, *grad_refs = refs[NEAR + FAR : NEAR + FAR + 1 + NEAR]
+    weights, cots, sems = refs[NEAR + FAR + 1 + NEAR :]
+    copies = fetch(place_ref, refs, weights, cots, sems)
+    turned = got_ref[...].reshape(COLS, FAR * ROWS).T
+    for copy in copies:
+        copy.wait()
+    for side in range(2):
+        part = contract(turned, weights[:, side * COLS : (side + 1) * COLS], 1, 0).astype(BF16)
+        for a in range(FAR):
+            out_ref[2 * a + side] = part[a * ROWS : (a + 1) * ROWS]
     gated = got_ref[...].reshape(COLS, FAR * ROWS)
     for step in range(NEAR):
-        block = near_ref[0] ^ step
-        low = pl.multiple_of((block % 2) * 256, 256)
-        part = contract(gated, weight_refs[step][...], 0, 0).astype(BF16)
-        for a in range(FAR):
-            out_ref[2 * a + block // 2, :, pl.ds(low, 256)] = part[a * ROWS : (a + 1) * ROWS]
-        grad = contract(gated, cot_columns(cots_ref, block), 1, 0)
+        low = pl.multiple_of((place_ref[0] ^ step) * 256, 256)
+        grad = contract(gated, cots[:, pl.ds(low, 256)], 1, 0)
         grad_refs[step][...] = grad.astype(grad_refs[step].dtype)
 
 
-def call(kernel, name, out_shape, interpret, *inputs, specs=None):
+def call(kernel, name, out_shape, interpret, *inputs, specs=None, scratch=()):
     many = isinstance(out_shape, tuple)
     outs = out_shape if many else (out_shape,)
     in_specs = [whole(x.shape) for x in inputs]
@@ -394,6 +465,7 @@
         grid=(1,),
         in_specs=in_specs,
         out_specs=out_specs if many else out_specs[0],
+        scratch_shapes=list(scratch),
         compiler_params=pltpu.CompilerParams(vmem_limit_bytes=VMEM_LIMIT),
         cost_estimate=pl.CostEstimate(flops=1_000_000_000, transcendentals=0, bytes_accessed=2_000_000),
         interpret=interpret,
@@ -406,7 +478,9 @@
 
 def pack(streams, long_filter, interpret=False):
     shape = jax.ShapeDtypeStruct((SEQ, ROWS, 4 * LANE), BF16)
-    return call(pack_kernel, "pack", shape, interpret, streams, long_filter)
+    return call(
+        pack_kernel, "pack", shape, interpret, resident(streams), resident(long_filter)
+    )
 
 
 def unpack(got, interpret=False):
@@ -417,31 +491,47 @@
     return call(unpack_kernel, "unpack", shapes, interpret, got)
 
 
-def to_send(near, gated, cots, weights, interpret=False):
+def far_off(low, high):
+    return {at: FAR_OFF for at in range(low, high)}
+
+
+GATHERED = (
+    pltpu.VMEM((COLS, 2 * COLS), BF16),
+    pltpu.VMEM((FAR * ROWS, 2 * COLS), BF16),
+    pltpu.SemaphoreType.DMA((NEAR + 2 * FAR,)),
+)
+
+
+def to_send(place, gated, weights, cots, interpret=False):
     shape = jax.ShapeDtypeStruct((SEQ, 2 * LANE, FAR * ROWS), BF16)
-    return call(send_kernel, "send", shape, interpret, near, gated, cots, *weights, specs={0: SCALAR})
-
-
-def products(near, got, cots, weights, interpret=False):
+    return call(
+        send_kernel, "send", shape, interpret, place, gated, *weights, *cots,
+        specs={0: SCALAR, **far_off(2, 2 + NEAR + FAR)}, scratch=GATHERED,
+    )
+
+
+def products(place, got, weights, cots, interpret=False):
     width = weights[0].shape[1]
-    shapes = (jax.ShapeDtypeStruct((CHAN, ROWS, COLS), BF16),) + tuple(
-        jax.ShapeDtypeStruct((COLS, width), BF16 if step else F32) for step in range(NEAR)
+    shapes = (pltpu.HBM((CHAN, ROWS, COLS), BF16),) + tuple(
+        pltpu.HBM((COLS, width), BF16 if step else F32) for step in range(NEAR)
     )
     half = pl.BlockSpec((SEQ, LANE, FAR * ROWS), lambda _: (0, 0, 0))
     return call(
-        product_kernel, "products", shapes, interpret, near, got, cots, *weights,
-        specs={0: SCALAR, 1: half},
+        product_kernel, "products", shapes, interpret, place, got, *weights, *cots,
+        specs={0: SCALAR, 1: half, **far_off(2, 2 + NEAR + FAR)}, scratch=GATHERED,
     )
 
 
 def shards(projected, short_filter, long_filter, w_out, d_out):
     seq_at = lax.axis_index("seq")
-    near = (seq_at % NEAR).astype(jnp.int32).reshape(1)
+    chan_at = lax.axis_index("chan")
+    place = jnp.stack([seq_at % NEAR, chan_at // 2, chan_at % 2]).astype(jnp.int32)
     consts = [jnp.asarray(table) for table in tables()]
 
     moved = swapped(d_out)
     signals = exchange(pack(projected.transpose(1, 0, 2), long_filter), "seq")
-    cots = exchange(jnp.broadcast_to(moved[None], (CHAN, ROWS, COLS)), "chan")
+    pair = jnp.stack([moved, lax.ppermute(moved, "chan", chan_pairs(1))])
+    cots = [pair] + [lax.ppermute(pair, "chan", chan_pairs(2 * far)) for far in range(1, FAR)]
     weights = [w_out] + [lax.ppermute(w_out, "seq", near_pairs(step)) for step in range(1, NEAR)]
 
     own = lax.dynamic_slice_in_dim(short_filter, seq_at * LANE, LANE, axis=2).reshape(3, 3 * LANE)
@@ -449,9 +539,9 @@
     taps = jnp.concatenate([own, plain], axis=1)
 
     gated, kept, spec = convolve(signals.reshape(TOKENS, 4 * LANE), taps, consts)
-    got = exchange(to_send(near, gated, cots, weights), "seq")
-
-    partial_out, d_wout, *others = products(near, got, cots, weights)
+    got = exchange(to_send(place, gated, weights, cots), "seq")
+
+    partial_out, d_wout, *others = products(place, got, weights, cots)
     shares = exchange(partial_out, "chan")
     output = swapped(jnp.sum(shares.astype(F32), axis=0).astype(BF16))
     for step, piece in enumerate(others, 1):

time: 124 us -> 116 us (0.935); the launches traced: 122 us -> 116 us
  local copies, waits for them, and re-layouts: 15.7 us -> 0.84 us
  waiting for transfers between devices: 16.4 us -> 21.5 us
  Pallas kernels: 26.8 us -> 30.5 us
  starting transfers between devices: 34 us -> 36.8 us
  blocking collectives: 26.1 us -> 24.2 us
    unnamed x41 -> x11, local copies, waits for them, and re-layouts: 14.5 us -> 0.69 us
    ppermute x0 -> x4, starting transfers between devices: none -> 4.76 us  [the longest x3 4.17 us: shards(): lax.ppermute(pair, 'chan', chan_pairs(2 * far))]
    ppermute x0 -> x4, waiting for transfers between devices: none -> 4.33 us  [the longest x1 4.32 us: shards(): pair = jnp.stack([moved, lax.ppermute(moved, 'chan', chan_pairs(1))])]
    all_to_all x4 -> x3, starting transfers between devices: 20.5 us -> 16.5 us  [exchange(): return lax.all_to_all(array, axis, 0, 0, tiled=True)]
    pallas_call x4, Pallas kernels: 5.63 us -> 8.68 us  [call(): pl.pallas_call(kernel, out_shape=out_shape, grid=(1,), in_specs=in_specs,...]
    ppermute x2, starting transfers between devices: 9.76 us -> 11.8 us  [swapped(): return lax.ppermute(array, ('seq', 'chan'), swap_pairs())]
    all_to_all x1, blocking collectives: 26.1 us -> 24.2 us  [exchange(): return lax.all_to_all(array, axis, 0, 0, tiled=True)]
    all_to_all x4 -> x3, waiting for transfers between devices: 5.59 us -> 5.19 us  [exchange(): return lax.all_to_all(array, axis, 0, 0, tiled=True)]
  transfers between devices with their start and end apart: 12 -> 15, of which waited for: 3 -> 5; matrix products, arithmetic and copies ran while one was open for 3% -> 1% of each run, Pallas kernels for 18% -> 20%
where the time goes in v2:
time: 116 us
  starting transfers between devices  36.8 us (32%)
  Pallas kernels  30.5 us (26%)
  blocking collectives  24.2 us (21%)
  waiting for transfers between devices  21.5 us (19%)
  other arithmetic  1.24 us (1%)
    all_to_all x1, blocking collectives, exchange(): return lax.all_to_all(array, axis, 0, 0, tiled=True)  24.2 us
    all_to_all x3, starting transfers between devices, exchange(): return lax.all_to_all(array, axis, 0, 0, tiled=True)  16.5 us
    ppermute x2, waiting for transfers between devices, swapped(): return lax.ppermute(array, ('seq', 'chan'), swap_pairs())  11.9 us
    ppermute x2, starting transfers between devices, swapped(): return lax.ppermute(array, ('seq', 'chan'), swap_pairs())  11.8 us
    pallas_call x1, Pallas kernels, convolve(): pl.pallas_call(forward_kernel, out_shape=(jax.ShapeDtypeStruct((NEAR, LAN...  10.9 us
    pallas_call x1, Pallas kernels, correlate(): pl.pallas_call(backward_kernel, out_shape=jax.ShapeDtypeStruct((SEQ, ROWS...  10.9 us
    pallas_call x4, Pallas kernels, call(): pl.pallas_call(kernel, out_shape=out_shape, grid=(1,), in_specs=in_specs,...  8.68 us
    all_to_all x3, waiting for transfers between devices, exchange(): return lax.all_to_all(array, axis, 0, 0, tiled=True)  5.19 us
  transfers between devices with their start and end apart: 15, of which 5 were waited for; matrix products, arithmetic and copies ran while one was open for 1% of the time, Pallas kernels for 20%

profile of v2, /device:TPU:32, one launch (start us, length us, event | category | flops | bytes accessed | tf_op | source)
XLA Modules:
  0.0 116.0 jit_solution(1199097266861501991)
XLA Ops:
  0.7 2.4 %pack.1 = bf16[16,128,128]{2,1,0:T(8,128)(2,1)} custom-call(bf16[3,128,512]{2,1,0:T(8,128)(2,1)} %bitcast.11, f32[128,512]{1,0:T(8,128)} %filter_ref.1), custom_call_target="tpu_custom_call" | custom-call | flops 1000000000 | bytes 2000000 | tf_op jit(solution)/shard_map/pack/pallas_call | solution.py:462
  3.1 7.0 %all-to-all-start = ((bf16[16,128,128]{2,1,0:T(8,128)(2,1)}), bf16[16,128,128]{2,1,0:T(8,128)(2,1)S(1)}, u32[]{:S(2)}, u32[]{:S(2)}) async-start(bf16[16,128,128]{2,1,0:T(8,128)(2,1)} %pack.1), calls=%async_computation | async-start | bytes 1048576 | tf_op jit(solution)/shard_map/all_to_all | solution.py:59
  10.1 4.9 %collective-permute-start.3 = (bf16[128,512]{1,0:T(8,128)(2,1)S(1)}, bf16[128,512]{1,0:T(8,128)(2,1)S(1)}, u32[]{:S(2)}, u32[]{:S(2)}) collective-permute-start(bf16[128,512]{1,0:T(8,128)(2,1)S(1)} %copy-done.4), channel_id=1, source_target_pairs={{0,0},{1,1},{2,32},{3,33},{4,64},{5,65},{6,96},{7,97},{8,8},{9,9},... | collective-permute-start | bytes 393224 | tf_op jit(solution)/shard_map/ppermute | solution.py:47
  15.0 0.1 collective-permute-start.2
  15.1 1.5 %collective-permute-start.1 = (bf16[512,256]{1,0:T(8,128)(2,1)S(1)}, bf16[512,256]{1,0:T(8,128)(2,1)S(1)}, u32[]{:S(2)}, u32[]{:S(2)}) collective-permute-start(bf16[512,256]{1,0:T(8,128)(2,1)S(1)} %copy-done.1), channel_id=1, source_target_pairs={{0,16},{8,24},{16,0},{24,8},{32,48},{40,56},{48,32},{56,40},{64,80... | collective-permute-start | bytes 786440 | tf_op jit(solution)/shard_map/ppermute | solution.py:535
  16.6 0.4 collective-permute-start
  17.0 0.1 constant_dynamic-slice_fusion
  17.0 8.7 %collective-permute-done.3 = bf16[128,512]{1,0:T(8,128)(2,1)S(1)} collective-permute-done((bf16[128,512]{1,0:T(8,128)(2,1)S(1)}, bf16[128,512]{1,0:T(8,128)(2,1)S(1)}, u32[]{:S(2)}, u32[]{:S(2)}) %collective-permute-start.3) | collective-permute-done | bytes 131104 | tf_op jit(solution)/shard_map/ppermute | solution.py:47
  25.7 0.6 collective-permute-start.4
  26.3 0.1 pad_add_fusion.place_ref
  26.4 0.1 reshape.37
  26.5 0.1 pad_maximum_fusion.1.taps_ref
  26.5 4.3 %collective-permute-done.4 = bf16[128,512]{1,0:T(8,128)(2,1)S(1)} collective-permute-done((bf16[128,512]{1,0:T(8,128)(2,1)S(1)}, bf16[128,512]{1,0:T(8,128)(2,1)S(1)}, u32[]{:S(2)}, u32[]{:S(2)}) %collective-permute-start.4) | collective-permute-done | bytes 131104 | tf_op jit(solution)/shard_map/ppermute | solution.py:533
  30.9 0.1 collective-permute-start.7
  31.0 1.6 %collective-permute-start.6 = (bf16[2,128,512]{2,1,0:T(8,128)(2,1)S(1)}, bf16[2,128,512]{2,1,0:T(8,128)(2,1)S(1)}, u32[]{:S(2)}, u32[]{:S(2)}) collective-permute-start(bf16[2,128,512]{2,1,0:T(8,128)(2,1)S(1)} %pad_maximum_fusion.refs_4_), channel_id=1, source_target_pairs={{0,4},{1,5},{2,6},{3,7},{4,0},{5,1},{6,2},{7,3},{8,12},{9,13},{10,... | collective-permute-start | bytes 786440 | tf_op jit(solution)/shard_map/ppermute | solution.py:534
  32.6 2.4 %collective-permute-start.5 = (bf16[2,128,512]{2,1,0:T(8,128)(2,1)S(1)}, bf16[2,128,512]{2,1,0:T(8,128)(2,1)S(1)}, u32[]{:S(2)}, u32[]{:S(2)}) collective-permute-start(bf16[2,128,512]{2,1,0:T(8,128)(2,1)S(1)} %pad_maximum_fusion.refs_4_), channel_id=1, source_target_pairs={{0,2},{1,3},{2,0},{3,1},{4,6},{5,7},{6,4},{7,5},{8,10},{9,11},{10,... | collective-permute-start | bytes 786440 | tf_op jit(solution)/shard_map/ppermute | solution.py:534
  35.1 10.9 %convolve.1 = (bf16[4,32,512]{2,1,0:T(8,128)(2,1)S(1)}, f32[2048,128]{1,0:T(8,128)}, f32[33,128,128]{2,1,0:T(8,128)}) custom-call(bf16[2048,128]{1,0:T(8,128)(2,1)S(1)} %bitcast.8, f32[3,128]{1,0:T(4,128)S(1)} %pad_maximum_fusion.1.taps_ref, bf16[64,72,96]{2,1,0:T(8,128)(2,1)} %constant.90.clone.first_hbm, bf16[128,384]{1,0:T(8,128)(2,1)} %constant.91.clone.ahead_hbm, ...), custom_call_target="tpu_custom_call" | custom-call | flops 8000000000 | bytes 6000000 | tf_op jit(solution)/shard_map/convolve/pallas_call | solution.py:323
  46.1 1.7 %send.1 = bf16[16,64,512]{2,1,0:T(8,128)(2,1)S(1)} custom-call(s32[3]{0:T(128)S(1)} %pad_add_fusion.place_ref, bf16[4,32,512]{2,1,0:T(8,128)(2,1)S(1)} %get-tuple-element.26.gated_ref, bf16[512,256]{1,0:T(8,128)(2,1)S(1)} %copy-done.1, bf16[512,256]{1,0:T(8,128)(2,1)S(1)} %collective-permute-done.refs_1_, ...), custom_call_target="tpu_custom_call" | custom-call | flops 1000000000 | bytes 2000000 | tf_op jit(solution)/shard_map/send/pallas_call | solution.py:462
  47.8 24.2 %all_to_all.20.got_ref.share_ref = bf16[16,64,512]{2,1,0:T(8,128)(2,1)S(1)} all-to-all(bf16[16,64,512]{2,1,0:T(8,128)(2,1)S(1)} %send.1), channel_id=1, replica_groups=mesh['seq'=16,'chan'=8] {'seq'}, dimensions={0} | all-to-all | bytes 2097152 | tf_op jit(solution)/shard_map/all_to_all | solution.py:59
  72.0 3.2 %products.1 = (bf16[8,128,512]{2,1,0:T(8,128)(2,1)}, f32[512,256]{1,0:T(8,128)}, bf16[512,256]{1,0:T(8,128)(2,1)}, bf16[512,256]{1,0:T(8,128)(2,1)}, bf16[512,256]{1,0:T(8,128)(2,1)}) custom-call(s32[3]{0:T(128)S(1)} %pad_add_fusion.place_ref, bf16[16,64,512]{2,1,0:T(8,128)(2,1)S(1)} %all_to_all.20.got_ref.share_ref, bf16[512,256]{1,0:T(8,128)(2,1)S(1)} %copy-done.1, ...), custom_call_target="tpu_custom_call" | custom-call | flops 1000000000 | bytes 2000000 | tf_op jit(solution)/shard_map/products/pallas_call | solution.py:462
  75.3 5.3 %all-to-all-start.2 = ((bf16[8,128,512]{2,1,0:T(8,128)(2,1)}), bf16[8,128,512]{2,1,0:T(8,128)(2,1)S(1)}, u32[]{:S(2)}, u32[]{:S(2)}) async-start(bf16[8,128,512]{2,1,0:T(8,128)(2,1)} %get-tuple-element.27), calls=%async_computation.2 | async-start | bytes 2097152 | tf_op jit(solution)/shard_map/all_to_all | solution.py:59
  80.6 1.9 %collective-permute-start.11 = (bf16[512,256]{1,0:T(8,128)(2,1)}, bf16[512,256]{1,0:T(8,128)(2,1)S(1)}, u32[]{:S(2)}, u32[]{:S(2)}) collective-permute-start(bf16[512,256]{1,0:T(8,128)(2,1)} %get-tuple-element.34), channel_id=1, source_target_pairs={{0,24},{8,16},{16,8},{24,0},{32,56},{40,48},{48,40},{56,32},{64,88... | collective-permute-start | bytes 786440 | tf_op jit(solution)/shard_map/ppermute | solution.py:548
  82.5 10.9 %correlate.1 = bf16[16,128,128]{2,1,0:T(8,128)(2,1)} custom-call(bf16[16,64,512]{2,1,0:T(8,128)(2,1)S(1)} %all_to_all.20.got_ref.share_ref, f32[2048,128]{1,0:T(8,128)} %get-tuple-element.28.kept_hbm, f32[33,128,128]{2,1,0:T(8,128)} %get-tuple-element.29.spec_hbm, f32[3,128]{1,0:T(4,128)S(1)} %pad_maximum_fusion.1.taps_ref, ...), custom_call_target="tpu_custom_call" | custom-call | flops 8000000000 | bytes 6000000 | tf_op jit(solution)/shard_map/correlate/pallas_call | solution.py:349
  93.4 0.4 all-to-all-done.2
  93.7 4.2 %all-to-all-start.3 = ((bf16[16,128,128]{2,1,0:T(8,128)(2,1)}), bf16[16,128,128]{2,1,0:T(8,128)(2,1)S(1)}, u32[]{:S(2)}, u32[]{:S(2)}) async-start(bf16[16,128,128]{2,1,0:T(8,128)(2,1)} %correlate.1), calls=%async_computation.3 | async-start | bytes 1048576 | tf_op jit(solution)/shard_map/all_to_all | solution.py:59
  97.9 0.1 reduce_sum.12
  98.0 6.9 %collective-permute-start.8 = (bf16[128,512]{1,0:T(8,128)(2,1)S(1)}, bf16[128,512]{1,0:T(8,128)(2,1)S(1)}, u32[]{:S(2)}, u32[]{:S(2)}) collective-permute-start(bf16[128,512]{1,0:T(8,128)(2,1)S(1)} %reduce_sum.12), channel_id=1, source_target_pairs={{0,0},{1,1},{2,32},{3,33},{4,64},{5,65},{6,96},{7,97},{8,8},{9,9},... | collective-permute-start | bytes 393224 | tf_op jit(solution)/shard_map/ppermute | solution.py:47
  105.0 0.9 convert_add_fusion
  105.9 4.8 %all-to-all-done.3.got_ref = bf16[16,128,128]{2,1,0:T(8,128)(2,1)S(1)} async-done(((bf16[16,128,128]{2,1,0:T(8,128)(2,1)}), bf16[16,128,128]{2,1,0:T(8,128)(2,1)S(1)}, u32[]{:S(2)}, u32[]{:S(2)}) %all-to-all-start.3) | async-done | bytes 524320 | tf_op jit(solution)/shard_map/all_to_all | solution.py:59
  110.7 1.3 %unpack.1 = (bf16[3,128,512]{2,1,0:T(8,128)(2,1)}, f32[128,512]{1,0:T(8,128)}) custom-call(bf16[16,128,128]{2,1,0:T(8,128)(2,1)S(1)} %all-to-all-done.3.got_ref), custom_call_target="tpu_custom_call" | custom-call | flops 1000000000 | bytes 2000000 | tf_op jit(solution)/shard_map/unpack/pallas_call | solution.py:462
  112.0 3.3 %collective-permute-done.8 = bf16[128,512]{1,0:T(8,128)(2,1)S(1)} collective-permute-done((bf16[128,512]{1,0:T(8,128)(2,1)S(1)}, bf16[128,512]{1,0:T(8,128)(2,1)S(1)}, u32[]{:S(2)}, u32[]{:S(2)}) %collective-permute-start.8) | collective-permute-done | bytes 131104 | tf_op jit(solution)/shard_map/ppermute | solution.py:47
  115.3 0.7 copy.14
  (23 shorter events, 0.1 us)
Async XLA Ops:
  0.6 16.3 %copy-start = (f32[3,3,512]{2,1,0:T(4,128)S(1)}, f32[3,3,512]{2,1,0:T(4,128)}, u32[]{:S(2)}) copy-start(f32[3,3,512]{2,1,0:T(4,128)} %param.12) | copy-start | bytes 55300
  0.6 9.5 %copy-start.4 = (bf16[128,512]{1,0:T(8,128)(2,1)S(1)}, bf16[128,512]{1,0:T(8,128)(2,1)}, u32[]{:S(2)}) copy-start(bf16[128,512]{1,0:T(8,128)(2,1)} %param.15) | copy-start | bytes 393220
  0.7 14.4 %copy-start.1 = (bf16[512,256]{1,0:T(8,128)(2,1)S(1)}, bf16[512,256]{1,0:T(8,128)(2,1)}, u32[]{:S(2)}) copy-start(bf16[512,256]{1,0:T(8,128)(2,1)} %refs_0_.3) | copy-start | bytes 786436
  0.7 25.8 %copy-start.3 = (f32[3,32]{1,0:T(4,128)S(1)}, f32[3,32]{1,0:T(4,128)}, u32[]{:S(2)}) copy-start(f32[3,32]{1,0:T(4,128)} %constant.88.clone.1) | copy-start | bytes 1156
  3.1 32.0 %all-to-all-start = ((bf16[16,128,128]{2,1,0:T(8,128)(2,1)}), bf16[16,128,128]{2,1,0:T(8,128)(2,1)S(1)}, u32[]{:S(2)}, u32[]{:S(2)}) async-start(bf16[16,128,128]{2,1,0:T(8,128)(2,1)} %pack.1), calls=%async_computation | async-start | bytes 1048576 | tf_op jit(solution)/shard_map/all_to_all | solution.py:59
  10.1 15.6 %collective-permute-start.3 = (bf16[128,512]{1,0:T(8,128)(2,1)S(1)}, bf16[128,512]{1,0:T(8,128)(2,1)S(1)}, u32[]{:S(2)}, u32[]{:S(2)}) collective-permute-start(bf16[128,512]{1,0:T(8,128)(2,1)S(1)} %copy-done.4), channel_id=1, source_target_pairs={{0,0},{1,1},{2,32},{3,33},{4,64},{5,65},{6,96},{7,97},{8,8},{9,9},... | collective-permute-start | bytes 393224 | tf_op jit(solution)/shard_map/ppermute | solution.py:47
  15.0 17.6 %collective-permute-start.2 = (bf16[512,256]{1,0:T(8,128)(2,1)S(1)}, bf16[512,256]{1,0:T(8,128)(2,1)S(1)}, u32[]{:S(2)}, u32[]{:S(2)}) collective-permute-start(bf16[512,256]{1,0:T(8,128)(2,1)S(1)} %copy-done.1), channel_id=1, source_target_pairs={{0,24},{8,16},{16,8},{24,0},{32,56},{40,48},{48,40},{56,32},{64,88... | collective-permute-start | bytes 786440 | tf_op jit(solution)/shard_map/ppermute | solution.py:535
  15.1 30.9 %collective-permute-start.1 = (bf16[512,256]{1,0:T(8,128)(2,1)S(1)}, bf16[512,256]{1,0:T(8,128)(2,1)S(1)}, u32[]{:S(2)}, u32[]{:S(2)}) collective-permute-start(bf16[512,256]{1,0:T(8,128)(2,1)S(1)} %copy-done.1), channel_id=1, source_target_pairs={{0,16},{8,24},{16,0},{24,8},{32,48},{40,56},{48,32},{56,40},{64,80... | collective-permute-start | bytes 786440 | tf_op jit(solution)/shard_map/ppermute | solution.py:535
  16.6 29.4 %collective-permute-start = (bf16[512,256]{1,0:T(8,128)(2,1)S(1)}, bf16[512,256]{1,0:T(8,128)(2,1)S(1)}, u32[]{:S(2)}, u32[]{:S(2)}) collective-permute-start(bf16[512,256]{1,0:T(8,128)(2,1)S(1)} %copy-done.1), channel_id=1, source_target_pairs={{0,8},{8,0},{16,24},{24,16},{32,40},{40,32},{48,56},{56,48},{64,72... | collective-permute-start | bytes 786440 | tf_op jit(solution)/shard_map/ppermute | solution.py:535
  25.7 5.1 %collective-permute-start.4 = (bf16[128,512]{1,0:T(8,128)(2,1)S(1)}, bf16[128,512]{1,0:T(8,128)(2,1)S(1)}, u32[]{:S(2)}, u32[]{:S(2)}) collective-permute-start(bf16[128,512]{1,0:T(8,128)(2,1)S(1)} %collective-permute-done.3), channel_id=1, source_target_pairs={{0,1},{1,0},{2,3},{3,2},{4,5},{5,4},{6,7},{7,6},{8,9},{9,8},{10,11... | collective-permute-start | bytes 393224 | tf_op jit(solution)/shard_map/ppermute | solution.py:533
  30.9 15.1 %collective-permute-start.7 = (bf16[2,128,512]{2,1,0:T(8,128)(2,1)S(1)}, bf16[2,128,512]{2,1,0:T(8,128)(2,1)S(1)}, u32[]{:S(2)}, u32[]{:S(2)}) collective-permute-start(bf16[2,128,512]{2,1,0:T(8,128)(2,1)S(1)} %pad_maximum_fusion.refs_4_), channel_id=1, source_target_pairs={{0,6},{1,7},{2,4},{3,5},{4,2},{5,3},{6,0},{7,1},{8,14},{9,15},{10,... | collective-permute-start | bytes 786440 | tf_op jit(solution)/shard_map/ppermute | solution.py:534
  31.0 15.0 %collective-permute-start.6 = (bf16[2,128,512]{2,1,0:T(8,128)(2,1)S(1)}, bf16[2,128,512]{2,1,0:T(8,128)(2,1)S(1)}, u32[]{:S(2)}, u32[]{:S(2)}) collective-permute-start(bf16[2,128,512]{2,1,0:T(8,128)(2,1)S(1)} %pad_maximum_fusion.refs_4_), channel_id=1, source_target_pairs={{0,4},{1,5},{2,6},{3,7},{4,0},{5,1},{6,2},{7,3},{8,12},{9,13},{10,... | collective-permute-start | bytes 786440 | tf_op jit(solution)/shard_map/ppermute | solution.py:534
  32.6 13.4 %collective-permute-start.5 = (bf16[2,128,512]{2,1,0:T(8,128)(2,1)S(1)}, bf16[2,128,512]{2,1,0:T(8,128)(2,1)S(1)}, u32[]{:S(2)}, u32[]{:S(2)}) collective-permute-start(bf16[2,128,512]{2,1,0:T(8,128)(2,1)S(1)} %pad_maximum_fusion.refs_4_), channel_id=1, source_target_pairs={{0,2},{1,3},{2,0},{3,1},{4,6},{5,7},{6,4},{7,5},{8,10},{9,11},{10,... | collective-permute-start | bytes 786440 | tf_op jit(solution)/shard_map/ppermute | solution.py:534
  75.3 18.5 %all-to-all-start.2 = ((bf16[8,128,512]{2,1,0:T(8,128)(2,1)}), bf16[8,128,512]{2,1,0:T(8,128)(2,1)S(1)}, u32[]{:S(2)}, u32[]{:S(2)}) async-start(bf16[8,128,512]{2,1,0:T(8,128)(2,1)} %get-tuple-element.27), calls=%async_computation.2 | async-start | bytes 2097152 | tf_op jit(solution)/shard_map/all_to_all | solution.py:59
  80.6 24.4 %collective-permute-start.9 = (bf16[512,256]{1,0:T(8,128)(2,1)}, bf16[512,256]{1,0:T(8,128)(2,1)S(1)}, u32[]{:S(2)}, u32[]{:S(2)}) collective-permute-start(bf16[512,256]{1,0:T(8,128)(2,1)} %get-tuple-element.32), channel_id=1, source_target_pairs={{0,8},{8,0},{16,24},{24,16},{32,40},{40,32},{48,56},{56,48},{64,72... | collective-permute-start | bytes 786440 | tf_op jit(solution)/shard_map/ppermute | solution.py:548
  80.6 24.4 %collective-permute-start.10 = (bf16[512,256]{1,0:T(8,128)(2,1)}, bf16[512,256]{1,0:T(8,128)(2,1)S(1)}, u32[]{:S(2)}, u32[]{:S(2)}) collective-permute-start(bf16[512,256]{1,0:T(8,128)(2,1)} %get-tuple-element.33), channel_id=1, source_target_pairs={{0,16},{8,24},{16,0},{24,8},{32,48},{40,56},{48,32},{56,40},{64,80... | collective-permute-start | bytes 786440 | tf_op jit(solution)/shard_map/ppermute | solution.py:548
  80.6 24.4 %collective-permute-start.11 = (bf16[512,256]{1,0:T(8,128)(2,1)}, bf16[512,256]{1,0:T(8,128)(2,1)S(1)}, u32[]{:S(2)}, u32[]{:S(2)}) collective-permute-start(bf16[512,256]{1,0:T(8,128)(2,1)} %get-tuple-element.34), channel_id=1, source_target_pairs={{0,24},{8,16},{16,8},{24,0},{32,56},{40,48},{48,40},{56,32},{64,88... | collective-permute-start | bytes 786440 | tf_op jit(solution)/shard_map/ppermute | solution.py:548
  93.4 11.6 %copy-start.2 = (f32[512,256]{1,0:T(8,128)S(1)}, f32[512,256]{1,0:T(8,128)}, u32[]{:S(2)}) copy-start(f32[512,256]{1,0:T(8,128)} %get-tuple-element.31) | copy-start | bytes 1572868
  93.7 17.0 %all-to-all-start.3 = ((bf16[16,128,128]{2,1,0:T(8,128)(2,1)}), bf16[16,128,128]{2,1,0:T(8,128)(2,1)S(1)}, u32[]{:S(2)}, u32[]{:S(2)}) async-start(bf16[16,128,128]{2,1,0:T(8,128)(2,1)} %correlate.1), calls=%async_computation.3 | async-start | bytes 1048576 | tf_op jit(solution)/shard_map/all_to_all | solution.py:59
  98.0 17.3 %collective-permute-start.8 = (bf16[128,512]{1,0:T(8,128)(2,1)S(1)}, bf16[128,512]{1,0:T(8,128)(2,1)S(1)}, u32[]{:S(2)}, u32[]{:S(2)}) collective-permute-start(bf16[128,512]{1,0:T(8,128)(2,1)S(1)} %reduce_sum.12), channel_id=1, source_target_pairs={{0,0},{1,1},{2,32},{3,33},{4,64},{5,65},{6,96},{7,97},{8,8},{9,9},... | collective-permute-start | bytes 393224 | tf_op jit(solution)/shard_map/ppermute | solution.py:47

commit v3 on v2

--- a/solution.py
+++ b/solution.py
@@ -202,7 +202,9 @@
     for block in range(SEQ):
         a, i = divmod(block, NEAR)
         turned = column_ref[block * ROWS : (block + 1) * ROWS, :].T
-        gated_ref[i, :, a * ROWS : (a + 1) * ROWS] = turned[:LANE].astype(BF16)
+        turned = turned[:LANE].astype(BF16)
+        for far in range(FAR):
+            gated_ref[far * NEAR + i, :, a * ROWS : (a + 1) * ROWS] = turned
     spec_copy.wait()
     kept_copy.wait()
 
@@ -323,13 +325,13 @@
     return pl.pallas_call(
         forward_kernel,
         out_shape=(
-            jax.ShapeDtypeStruct((NEAR, LANE, FAR * ROWS), BF16),
+            jax.ShapeDtypeStruct((SEQ, LANE, FAR * ROWS), BF16),
             pltpu.HBM((TOKENS, 4 * LANE), F32),
             pltpu.HBM((HALF, 128, 4 * LANE), F32),
         ),
         grid=(1,),
         in_specs=[whole(signals.shape), whole(taps.shape)] + [FAR_OFF] * 4,
-        out_specs=(whole((NEAR, LANE, FAR * ROWS)), FAR_OFF, FAR_OFF),
+        out_specs=(whole((SEQ, LANE, FAR * ROWS)), FAR_OFF, FAR_OFF),
         scratch_shapes=[
             pltpu.VMEM((TOKENS + 8, 4 * LANE), F32),
             pltpu.VMEM((64 * MID, 4 * LANE), F32),
@@ -345,12 +347,11 @@
 
 
 def correlate(shares, kept, spec, taps, consts, interpret=False):
-    half = pl.BlockSpec((SEQ, LANE, FAR * ROWS), lambda _: (0, 1, 0))
     return pl.pallas_call(
         backward_kernel,
         out_shape=jax.ShapeDtypeStruct((SEQ, ROWS, 4 * LANE), BF16),
         grid=(1,),
-        in_specs=[half, FAR_OFF, FAR_OFF, whole(taps.shape)] + [FAR_OFF] * 4,
+        in_specs=[whole(shares.shape), FAR_OFF, FAR_OFF, whole(taps.shape)] + [FAR_OFF] * 4,
         out_specs=whole((SEQ, ROWS, 4 * LANE)),
         scratch_shapes=[
             pltpu.VMEM((TOKENS, 4 * LANE), F32),
@@ -408,44 +409,38 @@
     for step in range(NEAR):
         low = pl.multiple_of((place_ref[0] ^ step) * 256, 256)
         copies.append(started(refs[step], weights.at[:, pl.ds(low, 256)], sems.at[step]))
-    for far in range(FAR):
-        row = pl.multiple_of((place_ref[1] ^ far) * ROWS, ROWS)
-        for side in range(2):
-            low = pl.multiple_of((place_ref[2] ^ side) * COLS, COLS)
-            copies.append(
-                started(
-                    refs[NEAR + far].at[side],
-                    cots.at[pl.ds(row, ROWS), pl.ds(low, COLS)],
-                    sems.at[NEAR + 2 * far + side],
-                )
+    for block in range(CHAN):
+        far, side = divmod(block, 2)
+        copies.append(
+            started(
+                refs[NEAR].at[block],
+                cots.at[far * ROWS : (far + 1) * ROWS, side * COLS : (side + 1) * COLS],
+                sems.at[NEAR + block],
             )
+        )
     return copies
 
 
-def send_kernel(place_ref, gated_ref, *refs):
-    sent_ref, weights, cots, sems = refs[NEAR + FAR :]
-    copies = fetch(place_ref, refs, weights, cots, sems)
-    for s in range(SEQ):
-        sent_ref[s, :LANE, :] = gated_ref[s % NEAR]
-    for copy in copies:
+def send_kernel(place_ref, *refs):
+    sent_ref, weights, cots, sems = refs[NEAR + 1 :]
+    for copy in fetch(place_ref, refs, weights, cots, sems):
         copy.wait()
     total = contract(weights[...], cots[...], 1, 1).astype(BF16)
-    for s in range(SEQ):
-        sent_ref[s, LANE:, :] = total[s * LANE : (s + 1) * LANE]
+    sent_ref[...] = total.reshape(SEQ, LANE, FAR * ROWS)
 
 
 def product_kernel(place_ref, got_ref, *refs):
-    out_ref, *grad_refs = refs[NEAR + FAR : NEAR + FAR + 1 + NEAR]
-    weights, cots, sems = refs[NEAR + FAR + 1 + NEAR :]
+    out_ref, *grad_refs = refs[NEAR + 1 : NEAR + 2 + NEAR]
+    weights, cots, sems = refs[NEAR + 2 + NEAR :]
     copies = fetch(place_ref, refs, weights, cots, sems)
-    turned = got_ref[...].reshape(COLS, FAR * ROWS).T
+    gated = got_ref[...].reshape(COLS, FAR * ROWS)
+    turned = gated.T
     for copy in copies:
         copy.wait()
     for side in range(2):
         part = contract(turned, weights[:, side * COLS : (side + 1) * COLS], 1, 0).astype(BF16)
         for a in range(FAR):
             out_ref[2 * a + side] = part[a * ROWS : (a + 1) * ROWS]
-    gated = got_ref[...].reshape(COLS, FAR * ROWS)
     for step in range(NEAR):
         low = pl.multiple_of((place_ref[0] ^ step) * 256, 256)
         grad = contract(gated, cots[:, pl.ds(low, 256)], 1, 0)
@@ -502,11 +497,11 @@
 )
 
 
-def to_send(place, gated, weights, cots, interpret=False):
-    shape = jax.ShapeDtypeStruct((SEQ, 2 * LANE, FAR * ROWS), BF16)
+def to_send(place, weights, cots, interpret=False):
+    shape = jax.ShapeDtypeStruct((SEQ, LANE, FAR * ROWS), BF16)
     return call(
-        send_kernel, "send", shape, interpret, place, gated, *weights, *cots,
-        specs={0: SCALAR, **far_off(2, 2 + NEAR + FAR)}, scratch=GATHERED,
+        send_kernel, "send", shape, interpret, place, *weights, cots,
+        specs={0: SCALAR, **far_off(1, 2 + NEAR)}, scratch=GATHERED,
     )
 
 
@@ -515,10 +510,9 @@
     shapes = (pltpu.HBM((CHAN, ROWS, COLS), BF16),) + tuple(
         pltpu.HBM((COLS, width), BF16 if step else F32) for step in range(NEAR)
     )
-    half = pl.BlockSpec((SEQ, LANE, FAR * ROWS), lambda _: (0, 0, 0))
     return call(
-        product_kernel, "products", shapes, interpret, place, got, *weights, *cots,
-        specs={0: SCALAR, 1: half, **far_off(2, 2 + NEAR + FAR)}, scratch=GATHERED,
+        product_kernel, "products", shapes, interpret, place, got, *weights, cots,
+        specs={0: SCALAR, **far_off(2, 3 + NEAR)}, scratch=GATHERED,
     )
 
 
@@ -528,10 +522,10 @@
     place = jnp.stack([seq_at % NEAR, chan_at // 2, chan_at % 2]).astype(jnp.int32)
     consts = [jnp.asarray(table) for table in tables()]
 
-    moved = swapped(d_out)
-    signals = exchange(pack(projected.transpose(1, 0, 2), long_filter), "seq")
-    pair = jnp.stack([moved, lax.ppermute(moved, "chan", chan_pairs(1))])
-    cots = [pair] + [lax.ppermute(pair, "chan", chan_pairs(2 * far)) for far in range(1, FAR)]
+    packed = pack(projected.transpose(1, 0, 2), long_filter)
+    moved, packed = lax.optimization_barrier((swapped(d_out), packed))
+    signals = exchange(packed, "seq")
+    cots = lax.all_gather(moved, "chan", axis=0)
     weights = [w_out] + [lax.ppermute(w_out, "seq", near_pairs(step)) for step in range(1, NEAR)]
 
     own = lax.dynamic_slice_in_dim(short_filter, seq_at * LANE, LANE, axis=2).reshape(3, 3 * LANE)
@@ -539,15 +533,17 @@
     taps = jnp.concatenate([own, plain], axis=1)
 
     gated, kept, spec = convolve(signals.reshape(TOKENS, 4 * LANE), taps, consts)
-    got = exchange(to_send(place, gated, weights, cots), "seq")
+    got = exchange(gated, "seq")
+    d_gated = exchange(to_send(place, weights, cots), "seq")
 
     partial_out, d_wout, *others = products(place, got, weights, cots)
+    partial_out, d_gated = lax.optimization_barrier((partial_out, d_gated))
     shares = exchange(partial_out, "chan")
     output = swapped(jnp.sum(shares.astype(F32), axis=0).astype(BF16))
     for step, piece in enumerate(others, 1):
         d_wout = d_wout + lax.ppermute(piece, "seq", near_pairs(step)).astype(F32)
 
-    returned = exchange(correlate(got, kept, spec, taps, consts), "seq")
+    returned = exchange(correlate(d_gated, kept, spec, taps, consts), "seq")
     d_projected, d_filter = unpack(returned)
     return (output, d_projected.transpose(1, 0, 2), d_wout, d_filter)
 

time: 116 us -> 150 us (1.29)
  waiting for transfers between devices: 21.5 us -> 53.9 us
  blocking collectives: 24.2 us -> 0 us
  between operations: 0.86 us -> 14.2 us
  starting transfers between devices: 36.8 us -> 45.3 us
  local copies, waits for them, and re-layouts: 0.84 us -> 2.73 us
    all_to_all x3 -> x5, waiting for transfers between devices: 5.19 us -> 29.8 us  [exchange(): return lax.all_to_all(array, axis, 0, 0, tiled=True)]
    all_to_all x1 -> x0, blocking collectives: 24.2 us -> none  [exchange(): return lax.all_to_all(array, axis, 0, 0, tiled=True)]
    ppermute x3, waiting for transfers between devices: 0.01 us -> 17.2 us  [shards(): lax.ppermute(w_out, 'seq', near_pairs(step))]
    all_to_all x3 -> x5, starting transfers between devices: 16.5 us -> 29.8 us  [exchange(): return lax.all_to_all(array, axis, 0, 0, tiled=True)]
    ppermute x2, waiting for transfers between devices: 11.9 us -> 6.83 us  [swapped(): return lax.ppermute(array, ('seq', 'chan'), swap_pairs())]
    ppermute x4 -> x0, starting transfers between devices: 4.76 us -> none  [the longest x3 4.17 us: shards(): lax.ppermute(pair, 'chan', chan_pairs(2 * far))]
    ppermute x4 -> x0, waiting for transfers between devices: 4.33 us -> none  [the longest x1 4.32 us: shards(): pair = jnp.stack([moved, lax.ppermute(moved, 'chan', chan_pairs(1))])]
    unnamed x11 -> x15, local copies, waits for them, and re-layouts: 0.69 us -> 2.57 us
  transfers between devices with their start and end apart: 15 -> 14, of which waited for: 5 -> 8; matrix products, arithmetic and copies ran while one was open for 1% -> 1% of each run, Pallas kernels for 20% -> 20%
where the time goes in v3:
time: 150 us; the launch traced here: 149 us
  waiting for transfers between devices  53.9 us (36%)
  starting transfers between devices  45.3 us (30%)
  Pallas kernels  31.9 us (21%)
  between operations  14.2 us (9%)
  local copies, waits for them, and re-layouts  2.73 us (2%)
    all_to_all x5, waiting for transfers between devices, exchange(): return lax.all_to_all(array, axis, 0, 0, tiled=True)  29.8 us
    all_to_all x5, starting transfers between devices, exchange(): return lax.all_to_all(array, axis, 0, 0, tiled=True)  29.8 us
    ppermute x3, waiting for transfers between devices, shards(): lax.ppermute(w_out, 'seq', near_pairs(step))  17.2 us
    pallas_call x1, Pallas kernels, convolve(): pl.pallas_call(forward_kernel, out_shape=(jax.ShapeDtypeStruct((SEQ, LANE...  11.7 us
    ppermute x2, starting transfers between devices, swapped(): return lax.ppermute(array, ('seq', 'chan'), swap_pairs())  11.5 us
    pallas_call x1, Pallas kernels, correlate(): pl.pallas_call(backward_kernel, out_shape=jax.ShapeDtypeStruct((SEQ, ROWS...  10.8 us
    pallas_call x4, Pallas kernels, call(): pl.pallas_call(kernel, out_shape=out_shape, grid=(1,), in_specs=in_specs,...  9.41 us
    ppermute x2, waiting for transfers between devices, swapped(): return lax.ppermute(array, ('seq', 'chan'), swap_pairs())  6.83 us
  transfers between devices with their start and end apart: 14, of which 8 were waited for; matrix products, arithmetic and copies ran while one was open for 1% of the time, Pallas kernels for 20%

profile of v3, /device:TPU:32, one launch (start us, length us, event | category | flops | bytes accessed | tf_op | source)
XLA Modules:
  0.0 149.3 jit_solution(7208467622927343245)
XLA Ops:
  7.2 4.6 %collective-permute-start = (bf16[128,512]{1,0:T(8,128)(2,1)}, bf16[128,512]{1,0:T(8,128)(2,1)S(1)}, u32[]{:S(2)}, u32[]{:S(2)}) collective-permute-start(bf16[128,512]{1,0:T(8,128)(2,1)} %param.15), channel_id=1, source_target_pairs={{0,0},{1,1},{2,32},{3,33},{4,64},{5,65},{6,96},{7,97},{8,8},{9,9},... | collective-permute-start | bytes 393224 | tf_op jit(solution)/shard_map/ppermute | solution.py:47
  11.9 2.4 %pack.1 = bf16[16,128,128]{2,1,0:T(8,128)(2,1)} custom-call(bf16[3,128,512]{2,1,0:T(8,128)(2,1)} %bitcast.10, f32[128,512]{1,0:T(8,128)} %filter_ref.1), custom_call_target="tpu_custom_call" | custom-call | flops 1000000000 | bytes 2000000 | tf_op jit(solution)/shard_map/pack/pallas_call | solution.py:457
  14.3 3.6 %collective-permute-done = bf16[128,512]{1,0:T(8,128)(2,1)S(1)} collective-permute-done((bf16[128,512]{1,0:T(8,128)(2,1)}, bf16[128,512]{1,0:T(8,128)(2,1)S(1)}, u32[]{:S(2)}, u32[]{:S(2)}) %collective-permute-start) | collective-permute-done | bytes 131104 | tf_op jit(solution)/shard_map/ppermute | solution.py:47
  17.8 0.7 copy-done.5
  18.5 8.9 %all-to-all-start = ((bf16[16,128,128]{2,1,0:T(8,128)(2,1)}), bf16[16,128,128]{2,1,0:T(8,128)(2,1)S(1)}, u32[]{:S(2)}, u32[]{:S(2)}) async-start(bf16[16,128,128]{2,1,0:T(8,128)(2,1)} %pack.1), calls=%async_computation | async-start | bytes 1048576 | tf_op jit(solution)/shard_map/all_to_all | solution.py:59
  27.4 0.1 constant_dynamic-slice_fusion
  27.5 0.1 reshape.37
  27.6 15.4 %all-to-all-done = bf16[16,128,128]{2,1,0:T(8,128)(2,1)S(1)} async-done(((bf16[16,128,128]{2,1,0:T(8,128)(2,1)}), bf16[16,128,128]{2,1,0:T(8,128)(2,1)S(1)}, u32[]{:S(2)}, u32[]{:S(2)}) %all-to-all-start) | async-done | bytes 524320 | tf_op jit(solution)/shard_map/all_to_all | solution.py:59
  43.1 11.7 %convolve.1 = (bf16[16,32,512]{2,1,0:T(8,128)(2,1)}, f32[2048,128]{1,0:T(8,128)}, f32[33,128,128]{2,1,0:T(8,128)}) custom-call(bf16[2048,128]{1,0:T(8,128)(2,1)S(1)} %bitcast.7, f32[3,128]{1,0:T(4,128)S(1)} %pad_maximum_fusion.taps_ref, bf16[64,72,96]{2,1,0:T(8,128)(2,1)} %constant.90.clone.first_hbm, bf16[128,384]{1,0:T(8,128)(2,1)} %constant.91.clone.ahead_hbm, ...), custom_call_target="tpu_custom_call" | custom-call | flops 8000000000 | bytes 6000000 | tf_op jit(solution)/shard_map/convolve/pallas_call | solution.py:325
  54.8 3.6 %all-to-all-start.1 = ((bf16[16,32,512]{2,1,0:T(8,128)(2,1)}), bf16[16,32,512]{2,1,0:T(8,128)(2,1)S(1)}, u32[]{:S(2)}, u32[]{:S(2)}) async-start(bf16[16,32,512]{2,1,0:T(8,128)(2,1)} %get-tuple-element.31), calls=%async_computation.1 | async-start | bytes 1048576 | tf_op jit(solution)/shard_map/all_to_all | solution.py:59
  58.4 0.4 collective-permute-start.1
  58.8 1.7 %collective-permute-start.2 = (bf16[512,256]{1,0:T(8,128)(2,1)S(1)}, bf16[512,256]{1,0:T(8,128)(2,1)S(1)}, u32[]{:S(2)}, u32[]{:S(2)}) collective-permute-start(bf16[512,256]{1,0:T(8,128)(2,1)S(1)} %copy-done.3), channel_id=1, source_target_pairs={{0,16},{8,24},{16,0},{24,8},{32,48},{40,56},{48,32},{56,40},{64,80... | collective-permute-start | bytes 786440 | tf_op jit(solution)/shard_map/ppermute | solution.py:529
  60.5 0.1 pad_add_fusion.place_ref
  60.5 12.6 %collective-permute-done.2.refs_2_ = bf16[512,256]{1,0:T(8,128)(2,1)S(1)} collective-permute-done((bf16[512,256]{1,0:T(8,128)(2,1)S(1)}, bf16[512,256]{1,0:T(8,128)(2,1)S(1)}, u32[]{:S(2)}, u32[]{:S(2)}) %collective-permute-start.2) | collective-permute-done | bytes 262176 | tf_op jit(solution)/shard_map/ppermute | solution.py:529
  73.1 4.7 %collective-permute-done.3.refs_3_ = bf16[512,256]{1,0:T(8,128)(2,1)S(1)} collective-permute-done((bf16[512,256]{1,0:T(8,128)(2,1)S(1)}, bf16[512,256]{1,0:T(8,128)(2,1)S(1)}, u32[]{:S(2)}, u32[]{:S(2)}) %collective-permute-start.3) | collective-permute-done | bytes 262176 | tf_op jit(solution)/shard_map/ppermute | solution.py:529
  77.8 1.2 copy-done.1
  79.0 2.5 %send.1 = bf16[16,32,512]{2,1,0:T(8,128)(2,1)} custom-call(s32[3]{0:T(128)S(1)} %pad_add_fusion.place_ref, bf16[512,256]{1,0:T(8,128)(2,1)S(1)} %copy-done.3, bf16[512,256]{1,0:T(8,128)(2,1)S(1)} %collective-permute-done.1.refs_1_, bf16[512,256]{1,0:T(8,128)(2,1)S(1)} %collective-permute-done.2.refs_2_, bf16[512,256]{1,0:T(8,128)(2,1)S(1)} %collective-permute-done.3.refs_3_, ...), custom_call_target="tpu_custom_call" | custom-call | flops 1000000000 | bytes 2000000 | tf_op jit(solution)/shard_map/send/pallas_call | solution.py:457
  81.5 6.9 %all-to-all-start.2 = ((bf16[16,32,512]{2,1,0:T(8,128)(2,1)}), bf16[16,32,512]{2,1,0:T(8,128)(2,1)S(1)}, u32[]{:S(2)}, u32[]{:S(2)}) async-start(bf16[16,32,512]{2,1,0:T(8,128)(2,1)} %send.1), calls=%async_computation.2 | async-start | bytes 1048576 | tf_op jit(solution)/shard_map/all_to_all | solution.py:59
  88.5 3.3 %products.1 = (bf16[8,128,512]{2,1,0:T(8,128)(2,1)}, f32[512,256]{1,0:T(8,128)}, bf16[512,256]{1,0:T(8,128)(2,1)}, bf16[512,256]{1,0:T(8,128)(2,1)}, bf16[512,256]{1,0:T(8,128)(2,1)}) custom-call(s32[3]{0:T(128)S(1)} %pad_add_fusion.place_ref, bf16[16,32,512]{2,1,0:T(8,128)(2,1)S(1)} %all-to-all-done.1.got_ref, bf16[512,256]{1,0:T(8,128)(2,1)S(1)} %copy-done.3, ...), custom_call_target="tpu_custom_call" | custom-call | flops 1000000000 | bytes 2000000 | tf_op jit(solution)/shard_map/products/pallas_call | solution.py:457
  91.7 9.1 %all-to-all-done.2.share_ref = bf16[16,32,512]{2,1,0:T(8,128)(2,1)S(1)} async-done(((bf16[16,32,512]{2,1,0:T(8,128)(2,1)}), bf16[16,32,512]{2,1,0:T(8,128)(2,1)S(1)}, u32[]{:S(2)}, u32[]{:S(2)}) %all-to-all-start.2) | async-done | bytes 524320 | tf_op jit(solution)/shard_map/all_to_all | solution.py:59
  100.8 6.3 %all-to-all-start.3 = ((bf16[8,128,512]{2,1,0:T(8,128)(2,1)}), bf16[8,128,512]{2,1,0:T(8,128)(2,1)S(1)}, u32[]{:S(2)}, u32[]{:S(2)}) async-start(bf16[8,128,512]{2,1,0:T(8,128)(2,1)} %get-tuple-element.34), calls=%async_computation.3 | async-start | bytes 2097152 | tf_op jit(solution)/shard_map/all_to_all | solution.py:59
  107.1 1.9 %collective-permute-start.7 = (bf16[512,256]{1,0:T(8,128)(2,1)}, bf16[512,256]{1,0:T(8,128)(2,1)S(1)}, u32[]{:S(2)}, u32[]{:S(2)}) collective-permute-start(bf16[512,256]{1,0:T(8,128)(2,1)} %get-tuple-element.42), channel_id=1, source_target_pairs={{0,24},{8,16},{16,8},{24,0},{32,56},{40,48},{48,40},{56,32},{64,88... | collective-permute-start | bytes 786440 | tf_op jit(solution)/shard_map/ppermute | solution.py:544
  108.9 10.8 %correlate.1 = bf16[16,128,128]{2,1,0:T(8,128)(2,1)} custom-call(bf16[16,32,512]{2,1,0:T(8,128)(2,1)S(1)} %all-to-all-done.2.share_ref, f32[2048,128]{1,0:T(8,128)} %get-tuple-element.36.kept_hbm, f32[33,128,128]{2,1,0:T(8,128)} %get-tuple-element.37.spec_hbm, f32[3,128]{1,0:T(4,128)S(1)} %pad_maximum_fusion.taps_ref, ...), custom_call_target="tpu_custom_call" | custom-call | flops 8000000000 | bytes 6000000 | tf_op jit(solution)/shard_map/correlate/pallas_call | solution.py:350
  119.8 0.4 all-to-all-done.3
  120.2 4.2 %all-to-all-start.4 = ((bf16[16,128,128]{2,1,0:T(8,128)(2,1)}), bf16[16,128,128]{2,1,0:T(8,128)(2,1)S(1)}, u32[]{:S(2)}, u32[]{:S(2)}) async-start(bf16[16,128,128]{2,1,0:T(8,128)(2,1)} %correlate.1), calls=%async_computation.4 | async-start | bytes 1048576 | tf_op jit(solution)/shard_map/all_to_all | solution.py:59
  124.4 0.1 reduce_sum.12
  124.5 6.9 %collective-permute-start.4 = (bf16[128,512]{1,0:T(8,128)(2,1)S(1)}, bf16[128,512]{1,0:T(8,128)(2,1)S(1)}, u32[]{:S(2)}, u32[]{:S(2)}) collective-permute-start(bf16[128,512]{1,0:T(8,128)(2,1)S(1)} %reduce_sum.12), channel_id=1, source_target_pairs={{0,0},{1,1},{2,32},{3,33},{4,64},{5,65},{6,96},{7,97},{8,8},{9,9},... | collective-permute-start | bytes 393224 | tf_op jit(solution)/shard_map/ppermute | solution.py:47
  131.5 0.9 convert_add_fusion
  132.4 4.8 %all-to-all-done.4.got_ref = bf16[16,128,128]{2,1,0:T(8,128)(2,1)S(1)} async-done(((bf16[16,128,128]{2,1,0:T(8,128)(2,1)}), bf16[16,128,128]{2,1,0:T(8,128)(2,1)S(1)}, u32[]{:S(2)}, u32[]{:S(2)}) %all-to-all-start.4) | async-done | bytes 524320 | tf_op jit(solution)/shard_map/all_to_all | solution.py:59
  137.2 1.3 unpack.1
  138.5 3.3 %collective-permute-done.4 = bf16[128,512]{1,0:T(8,128)(2,1)S(1)} collective-permute-done((bf16[128,512]{1,0:T(8,128)(2,1)S(1)}, bf16[128,512]{1,0:T(8,128)(2,1)S(1)}, u32[]{:S(2)}, u32[]{:S(2)}) %collective-permute-start.4) | collective-permute-done | bytes 131104 | tf_op jit(solution)/shard_map/ppermute | solution.py:47
  141.8 0.7 copy.14
  (24 shorter events, 0.2 us)
Async XLA Ops:
  7.2 20.2 %copy-start = (f32[3,3,512]{2,1,0:T(4,128)S(1)}, f32[3,3,512]{2,1,0:T(4,128)}, u32[]{:S(2)}) copy-start(f32[3,3,512]{2,1,0:T(4,128)} %param.12) | copy-start | bytes 55300
  7.2 70.6 %all-gather.3.cloned.1.call-start = ((), (), s32[]{:S(2)}) async-start(), calls=%async_computation.5 | async-start | bytes 1179648 | tf_op jit(solution)/shard_map/all_gather | solution.py:528
  7.2 10.6 %collective-permute-start = (bf16[128,512]{1,0:T(8,128)(2,1)}, bf16[128,512]{1,0:T(8,128)(2,1)S(1)}, u32[]{:S(2)}, u32[]{:S(2)}) collective-permute-start(bf16[128,512]{1,0:T(8,128)(2,1)} %param.15), channel_id=1, source_target_pairs={{0,0},{1,1},{2,32},{3,33},{4,64},{5,65},{6,96},{7,97},{8,8},{9,9},... | collective-permute-start | bytes 393224 | tf_op jit(solution)/shard_map/ppermute | solution.py:47
  11.9 15.7 %copy-start.6 = (f32[3,32]{1,0:T(4,128)S(1)}, f32[3,32]{1,0:T(4,128)}, u32[]{:S(2)}) copy-start(f32[3,32]{1,0:T(4,128)} %constant.88.clone.1) | copy-start | bytes 1156
  17.8 0.7 copy-start.5
  18.5 24.6 %all-to-all-start = ((bf16[16,128,128]{2,1,0:T(8,128)(2,1)}), bf16[16,128,128]{2,1,0:T(8,128)(2,1)S(1)}, u32[]{:S(2)}, u32[]{:S(2)}) async-start(bf16[16,128,128]{2,1,0:T(8,128)(2,1)} %pack.1), calls=%async_computation | async-start | bytes 1048576 | tf_op jit(solution)/shard_map/all_to_all | solution.py:59
  43.1 15.3 %copy-start.3 = (bf16[512,256]{1,0:T(8,128)(2,1)S(1)}, bf16[512,256]{1,0:T(8,128)(2,1)}, u32[]{:S(2)}) copy-start(bf16[512,256]{1,0:T(8,128)(2,1)} %refs_0_.3) | copy-start | bytes 786436
  54.8 26.7 %all-to-all-start.1 = ((bf16[16,32,512]{2,1,0:T(8,128)(2,1)}), bf16[16,32,512]{2,1,0:T(8,128)(2,1)S(1)}, u32[]{:S(2)}, u32[]{:S(2)}) async-start(bf16[16,32,512]{2,1,0:T(8,128)(2,1)} %get-tuple-element.31), calls=%async_computation.1 | async-start | bytes 1048576 | tf_op jit(solution)/shard_map/all_to_all | solution.py:59
  58.4 2.1 %collective-permute-start.1 = (bf16[512,256]{1,0:T(8,128)(2,1)S(1)}, bf16[512,256]{1,0:T(8,128)(2,1)S(1)}, u32[]{:S(2)}, u32[]{:S(2)}) collective-permute-start(bf16[512,256]{1,0:T(8,128)(2,1)S(1)} %copy-done.3), channel_id=1, source_target_pairs={{0,8},{8,0},{16,24},{24,16},{32,40},{40,32},{48,56},{56,48},{64,72... | collective-permute-start | bytes 786440 | tf_op jit(solution)/shard_map/ppermute | solution.py:529
  58.8 14.3 %collective-permute-start.2 = (bf16[512,256]{1,0:T(8,128)(2,1)S(1)}, bf16[512,256]{1,0:T(8,128)(2,1)S(1)}, u32[]{:S(2)}, u32[]{:S(2)}) collective-permute-start(bf16[512,256]{1,0:T(8,128)(2,1)S(1)} %copy-done.3), channel_id=1, source_target_pairs={{0,16},{8,24},{16,0},{24,8},{32,48},{40,56},{48,32},{56,40},{64,80... | collective-permute-start | bytes 786440 | tf_op jit(solution)/shard_map/ppermute | solution.py:529
  60.5 17.3 %collective-permute-start.3 = (bf16[512,256]{1,0:T(8,128)(2,1)S(1)}, bf16[512,256]{1,0:T(8,128)(2,1)S(1)}, u32[]{:S(2)}, u32[]{:S(2)}) collective-permute-start(bf16[512,256]{1,0:T(8,128)(2,1)S(1)} %copy-done.3), channel_id=1, source_target_pairs={{0,24},{8,16},{16,8},{24,0},{32,56},{40,48},{48,40},{56,32},{64,88... | collective-permute-start | bytes 786440 | tf_op jit(solution)/shard_map/ppermute | solution.py:529
  77.8 1.2 copy-start.1
  79.0 9.4 %copy-start.2 = (bf16[1024,512]{1,0:T(8,128)(2,1)S(1)}, bf16[1024,512]{1,0:T(8,128)(2,1)}, u32[]{:S(2)}) copy-start(bf16[1024,512]{1,0:T(8,128)(2,1)} %all-gather.3.cloned.1.call-done) | copy-start | bytes 3145732
  81.5 19.3 %all-to-all-start.2 = ((bf16[16,32,512]{2,1,0:T(8,128)(2,1)}), bf16[16,32,512]{2,1,0:T(8,128)(2,1)S(1)}, u32[]{:S(2)}, u32[]{:S(2)}) async-start(bf16[16,32,512]{2,1,0:T(8,128)(2,1)} %send.1), calls=%async_computation.2 | async-start | bytes 1048576 | tf_op jit(solution)/shard_map/all_to_all | solution.py:59
  100.8 19.4 %all-to-all-start.3 = ((bf16[8,128,512]{2,1,0:T(8,128)(2,1)}), bf16[8,128,512]{2,1,0:T(8,128)(2,1)S(1)}, u32[]{:S(2)}, u32[]{:S(2)}) async-start(bf16[8,128,512]{2,1,0:T(8,128)(2,1)} %get-tuple-element.34), calls=%async_computation.3 | async-start | bytes 2097152 | tf_op jit(solution)/shard_map/all_to_all | solution.py:59
  107.1 24.4 %collective-permute-start.5 = (bf16[512,256]{1,0:T(8,128)(2,1)}, bf16[512,256]{1,0:T(8,128)(2,1)S(1)}, u32[]{:S(2)}, u32[]{:S(2)}) collective-permute-start(bf16[512,256]{1,0:T(8,128)(2,1)} %get-tuple-element.40), channel_id=1, source_target_pairs={{0,8},{8,0},{16,24},{24,16},{32,40},{40,32},{48,56},{56,48},{64,72... | collective-permute-start | bytes 786440 | tf_op jit(solution)/shard_map/ppermute | solution.py:544
  107.1 24.4 %collective-permute-start.6 = (bf16[512,256]{1,0:T(8,128)(2,1)}, bf16[512,256]{1,0:T(8,128)(2,1)S(1)}, u32[]{:S(2)}, u32[]{:S(2)}) collective-permute-start(bf16[512,256]{1,0:T(8,128)(2,1)} %get-tuple-element.41), channel_id=1, source_target_pairs={{0,16},{8,24},{16,0},{24,8},{32,48},{40,56},{48,32},{56,40},{64,80... | collective-permute-start | bytes 786440 | tf_op jit(solution)/shard_map/ppermute | solution.py:544
  107.1 24.4 %collective-permute-start.7 = (bf16[512,256]{1,0:T(8,128)(2,1)}, bf16[512,256]{1,0:T(8,128)(2,1)S(1)}, u32[]{:S(2)}, u32[]{:S(2)}) collective-permute-start(bf16[512,256]{1,0:T(8,128)(2,1)} %get-tuple-element.42), channel_id=1, source_target_pairs={{0,24},{8,16},{16,8},{24,0},{32,56},{40,48},{48,40},{56,32},{64,88... | collective-permute-start | bytes 786440 | tf_op jit(solution)/shard_map/ppermute | solution.py:544
  119.7 11.7 %copy-start.4 = (f32[512,256]{1,0:T(8,128)S(1)}, f32[512,256]{1,0:T(8,128)}, u32[]{:S(2)}) copy-start(f32[512,256]{1,0:T(8,128)} %get-tuple-element.39) | copy-start | bytes 1572868
  120.2 17.0 %all-to-all-start.4 = ((bf16[16,128,128]{2,1,0:T(8,128)(2,1)}), bf16[16,128,128]{2,1,0:T(8,128)(2,1)S(1)}, u32[]{:S(2)}, u32[]{:S(2)}) async-start(bf16[16,128,128]{2,1,0:T(8,128)(2,1)} %correlate.1), calls=%async_computation.4 | async-start | bytes 1048576 | tf_op jit(solution)/shard_map/all_to_all | solution.py:59
  124.5 17.3 %collective-permute-start.4 = (bf16[128,512]{1,0:T(8,128)(2,1)S(1)}, bf16[128,512]{1,0:T(8,128)(2,1)S(1)}, u32[]{:S(2)}, u32[]{:S(2)}) collective-permute-start(bf16[128,512]{1,0:T(8,128)(2,1)S(1)} %reduce_sum.12), channel_id=1, source_target_pairs={{0,0},{1,1},{2,32},{3,33},{4,64},{5,65},{6,96},{7,97},{8,8},{9,9},... | collective-permute-start | bytes 393224 | tf_op jit(solution)/shard_map/ppermute | solution.py:47
Sparse Core Ops, SparseCore 0:
  18.6 43.4 all-gather.2

commit v4 on v2

--- a/solution.py
+++ b/solution.py
@@ -528,11 +528,15 @@
     place = jnp.stack([seq_at % NEAR, chan_at // 2, chan_at % 2]).astype(jnp.int32)
     consts = [jnp.asarray(table) for table in tables()]
 
-    moved = swapped(d_out)
-    signals = exchange(pack(projected.transpose(1, 0, 2), long_filter), "seq")
+    packed = pack(projected.transpose(1, 0, 2), long_filter)
+    moved, packed = lax.optimization_barrier((swapped(d_out), packed))
+    signals = exchange(packed, "seq")
     pair = jnp.stack([moved, lax.ppermute(moved, "chan", chan_pairs(1))])
+    pair, late = lax.optimization_barrier((pair, w_out))
     cots = [pair] + [lax.ppermute(pair, "chan", chan_pairs(2 * far)) for far in range(1, FAR)]
-    weights = [w_out] + [lax.ppermute(w_out, "seq", near_pairs(step)) for step in range(1, NEAR)]
+    across = lax.ppermute(late, "seq", near_pairs(2))
+    weights = [late, lax.ppermute(late, "seq", near_pairs(1)), across,
+               lax.ppermute(across, "seq", near_pairs(1))]
 
     own = lax.dynamic_slice_in_dim(short_filter, seq_at * LANE, LANE, axis=2).reshape(3, 3 * LANE)
     plain = jnp.zeros((3, LANE), F32).at[0].set(1.0)

time: 116 us -> 117 us (level)
  starting transfers between devices: 36.8 us -> 39.3 us
  waiting for transfers between devices: 21.5 us -> 19.5 us
    ppermute x3, waiting for transfers between devices: 0.01 us -> 7.52 us  [the longest x1 7.52 us: shards(): across = lax.ppermute(late, 'seq', near_pairs(2))]
    ppermute x2, waiting for transfers between devices: 11.9 us -> 6.79 us  [swapped(): return lax.ppermute(array, ('seq', 'chan'), swap_pairs())]
    ppermute x1, waiting for transfers between devices: 4.32 us -> 0.01 us  [shards(): pair = jnp.stack([moved, lax.ppermute(moved, 'chan', chan_pairs(1))])]
    all_to_all x3, starting transfers between devices: 16.5 us -> 17.9 us  [exchange(): return lax.all_to_all(array, axis, 0, 0, tiled=True)]
  transfers between devices with their start and end apart: 15 -> 15, of which waited for: 5 -> 5; matrix products, arithmetic and copies ran while one was open for 1% -> 1% of each run, Pallas kernels for 20% -> 22%
where the time goes in v4:
time: 117 us
  starting transfers between devices  39.3 us (34%)
  Pallas kernels  30.5 us (26%)
  blocking collectives  24.4 us (21%)
  waiting for transfers between devices  19.5 us (17%)
  other arithmetic  1.25 us (1%)
    all_to_all x1, blocking collectives, exchange(): return lax.all_to_all(array, axis, 0, 0, tiled=True)  24.4 us
    all_to_all x3, starting transfers between devices, exchange(): return lax.all_to_all(array, axis, 0, 0, tiled=True)  17.9 us
    ppermute x2, starting transfers between devices, swapped(): return lax.ppermute(array, ('seq', 'chan'), swap_pairs())  11.5 us
    pallas_call x1, Pallas kernels, correlate(): pl.pallas_call(backward_kernel, out_shape=jax.ShapeDtypeStruct((SEQ, ROWS...  10.9 us
    pallas_call x1, Pallas kernels, convolve(): pl.pallas_call(forward_kernel, out_shape=(jax.ShapeDtypeStruct((NEAR, LAN...  10.9 us
    pallas_call x4, Pallas kernels, call(): pl.pallas_call(kernel, out_shape=out_shape, grid=(1,), in_specs=in_specs,...  8.68 us
    ppermute x1, waiting for transfers between devices, shards(): across = lax.ppermute(late, 'seq', near_pairs(2))  7.52 us
    ppermute x2, waiting for transfers between devices, swapped(): return lax.ppermute(array, ('seq', 'chan'), swap_pairs())  6.79 us
  transfers between devices with their start and end apart: 15, of which 5 were waited for; matrix products, arithmetic and copies ran while one was open for 1% of the time, Pallas kernels for 22%

profile of v4, /device:TPU:32, one launch (start us, length us, event | category | flops | bytes accessed | tf_op | source)
XLA Modules:
  0.0 116.6 jit_solution(3964465846971721613)
XLA Ops:
  0.6 0.0 copy-start
  0.6 4.6 %collective-permute-start = (bf16[128,512]{1,0:T(8,128)(2,1)}, bf16[128,512]{1,0:T(8,128)(2,1)S(1)}, u32[]{:S(2)}, u32[]{:S(2)}) collective-permute-start(bf16[128,512]{1,0:T(8,128)(2,1)} %param.15), channel_id=1, source_target_pairs={{0,0},{1,1},{2,32},{3,33},{4,64},{5,65},{6,96},{7,97},{8,8},{9,9},... | collective-permute-start | bytes 393224 | tf_op jit(solution)/shard_map/ppermute | solution.py:47
  5.3 2.4 %pack.1 = bf16[16,128,128]{2,1,0:T(8,128)(2,1)} custom-call(bf16[3,128,512]{2,1,0:T(8,128)(2,1)} %bitcast.11, f32[128,512]{1,0:T(8,128)} %filter_ref.1), custom_call_target="tpu_custom_call" | custom-call | flops 1000000000 | bytes 2000000 | tf_op jit(solution)/shard_map/pack/pallas_call | solution.py:462
  7.7 3.5 %collective-permute-done = bf16[128,512]{1,0:T(8,128)(2,1)S(1)} collective-permute-done((bf16[128,512]{1,0:T(8,128)(2,1)}, bf16[128,512]{1,0:T(8,128)(2,1)S(1)}, u32[]{:S(2)}, u32[]{:S(2)}) %collective-permute-start) | collective-permute-done | bytes 131104 | tf_op jit(solution)/shard_map/ppermute | solution.py:47
  11.2 1.5 %collective-permute-start.1 = (bf16[128,512]{1,0:T(8,128)(2,1)S(1)}, bf16[128,512]{1,0:T(8,128)(2,1)S(1)}, u32[]{:S(2)}, u32[]{:S(2)}) collective-permute-start(bf16[128,512]{1,0:T(8,128)(2,1)S(1)} %collective-permute-done), channel_id=1, source_target_pairs={{0,1},{1,0},{2,3},{3,2},{4,5},{5,4},{6,7},{7,6},{8,9},{9,8},{10,11... | collective-permute-start | bytes 393224 | tf_op jit(solution)/shard_map/ppermute | solution.py:534
  12.7 8.6 %all-to-all-start = ((bf16[16,128,128]{2,1,0:T(8,128)(2,1)}), bf16[16,128,128]{2,1,0:T(8,128)(2,1)S(1)}, u32[]{:S(2)}, u32[]{:S(2)}) async-start(bf16[16,128,128]{2,1,0:T(8,128)(2,1)} %pack.1), calls=%async_computation | async-start | bytes 1048576 | tf_op jit(solution)/shard_map/all_to_all | solution.py:59
  21.3 2.0 %collective-permute-start.3 = (bf16[512,256]{1,0:T(8,128)(2,1)S(1)}, bf16[512,256]{1,0:T(8,128)(2,1)S(1)}, u32[]{:S(2)}, u32[]{:S(2)}) collective-permute-start(bf16[512,256]{1,0:T(8,128)(2,1)S(1)} %copy-done.1), channel_id=1, source_target_pairs={{0,16},{8,24},{16,0},{24,8},{32,48},{40,56},{48,32},{56,40},{64,80... | collective-permute-start | bytes 786440 | tf_op jit(solution)/shard_map/ppermute | solution.py:537
  23.3 0.1 constant_dynamic-slice_fusion
  23.4 0.1 reshape.37
  23.5 0.1 pad_add_fusion.place_ref
  23.6 0.1 pad_maximum_fusion.1.taps_ref
  23.7 0.0 collective-permute-start.2
  23.7 2.3 %collective-permute-start.7 = (bf16[2,128,512]{2,1,0:T(8,128)(2,1)S(1)}, bf16[2,128,512]{2,1,0:T(8,128)(2,1)S(1)}, u32[]{:S(2)}, u32[]{:S(2)}) collective-permute-start(bf16[2,128,512]{2,1,0:T(8,128)(2,1)S(1)} %pad_maximum_fusion.refs_4_), channel_id=1, source_target_pairs={{0,6},{1,7},{2,4},{3,5},{4,2},{5,3},{6,0},{7,1},{8,14},{9,15},{10,... | collective-permute-start | bytes 786440 | tf_op jit(solution)/shard_map/ppermute | solution.py:536
  26.0 1.2 collective-permute-start.6
  27.1 1.0 collective-permute-start.5
  28.1 7.5 %collective-permute-done.3.refs_2_ = bf16[512,256]{1,0:T(8,128)(2,1)S(1)} collective-permute-done((bf16[512,256]{1,0:T(8,128)(2,1)S(1)}, bf16[512,256]{1,0:T(8,128)(2,1)S(1)}, u32[]{:S(2)}, u32[]{:S(2)}) %collective-permute-start.3) | collective-permute-done | bytes 262176 | tf_op jit(solution)/shard_map/ppermute | solution.py:537
  35.7 10.9 %convolve.1 = (bf16[4,32,512]{2,1,0:T(8,128)(2,1)S(1)}, f32[2048,128]{1,0:T(8,128)}, f32[33,128,128]{2,1,0:T(8,128)}) custom-call(bf16[2048,128]{1,0:T(8,128)(2,1)S(1)} %bitcast.8, f32[3,128]{1,0:T(4,128)S(1)} %pad_maximum_fusion.1.taps_ref, bf16[64,72,96]{2,1,0:T(8,128)(2,1)} %constant.90.clone.first_hbm, bf16[128,384]{1,0:T(8,128)(2,1)} %constant.91.clone.ahead_hbm, ...), custom_call_target="tpu_custom_call" | custom-call | flops 8000000000 | bytes 6000000 | tf_op jit(solution)/shard_map/convolve/pallas_call | solution.py:323
  46.6 1.7 %send.1 = bf16[16,64,512]{2,1,0:T(8,128)(2,1)S(1)} custom-call(s32[3]{0:T(128)S(1)} %pad_add_fusion.place_ref, bf16[4,32,512]{2,1,0:T(8,128)(2,1)S(1)} %get-tuple-element.31.gated_ref, bf16[512,256]{1,0:T(8,128)(2,1)S(1)} %copy-done.1, bf16[512,256]{1,0:T(8,128)(2,1)S(1)} %collective-permute-done.2.refs_1_, ...), custom_call_target="tpu_custom_call" | custom-call | flops 1000000000 | bytes 2000000 | tf_op jit(solution)/shard_map/send/pallas_call | solution.py:462
  48.3 24.4 %all_to_all.20.got_ref.share_ref = bf16[16,64,512]{2,1,0:T(8,128)(2,1)S(1)} all-to-all(bf16[16,64,512]{2,1,0:T(8,128)(2,1)S(1)} %send.1), channel_id=1, replica_groups=mesh['seq'=16,'chan'=8] {'seq'}, dimensions={0} | all-to-all | bytes 2097152 | tf_op jit(solution)/shard_map/all_to_all | solution.py:59
  72.7 3.2 %products.1 = (bf16[8,128,512]{2,1,0:T(8,128)(2,1)}, f32[512,256]{1,0:T(8,128)}, bf16[512,256]{1,0:T(8,128)(2,1)}, bf16[512,256]{1,0:T(8,128)(2,1)}, bf16[512,256]{1,0:T(8,128)(2,1)}) custom-call(s32[3]{0:T(128)S(1)} %pad_add_fusion.place_ref, bf16[16,64,512]{2,1,0:T(8,128)(2,1)S(1)} %all_to_all.20.got_ref.share_ref, bf16[512,256]{1,0:T(8,128)(2,1)S(1)} %copy-done.1, ...), custom_call_target="tpu_custom_call" | custom-call | flops 1000000000 | bytes 2000000 | tf_op jit(solution)/shard_map/products/pallas_call | solution.py:462
  76.0 5.6 %all-to-all-start.2 = ((bf16[8,128,512]{2,1,0:T(8,128)(2,1)}), bf16[8,128,512]{2,1,0:T(8,128)(2,1)S(1)}, u32[]{:S(2)}, u32[]{:S(2)}) async-start(bf16[8,128,512]{2,1,0:T(8,128)(2,1)} %get-tuple-element.35), calls=%async_computation.2 | async-start | bytes 2097152 | tf_op jit(solution)/shard_map/all_to_all | solution.py:59
  81.5 1.9 %collective-permute-start.11 = (bf16[512,256]{1,0:T(8,128)(2,1)}, bf16[512,256]{1,0:T(8,128)(2,1)S(1)}, u32[]{:S(2)}, u32[]{:S(2)}) collective-permute-start(bf16[512,256]{1,0:T(8,128)(2,1)} %get-tuple-element.42), channel_id=1, source_target_pairs={{0,24},{8,16},{16,8},{24,0},{32,56},{40,48},{48,40},{56,32},{64,88... | collective-permute-start | bytes 786440 | tf_op jit(solution)/shard_map/ppermute | solution.py:552
  83.4 10.9 %correlate.1 = bf16[16,128,128]{2,1,0:T(8,128)(2,1)} custom-call(bf16[16,64,512]{2,1,0:T(8,128)(2,1)S(1)} %all_to_all.20.got_ref.share_ref, f32[2048,128]{1,0:T(8,128)} %get-tuple-element.36.kept_hbm, f32[33,128,128]{2,1,0:T(8,128)} %get-tuple-element.37.spec_hbm, f32[3,128]{1,0:T(4,128)S(1)} %pad_maximum_fusion.1.taps_ref, ...), custom_call_target="tpu_custom_call" | custom-call | flops 8000000000 | bytes 6000000 | tf_op jit(solution)/shard_map/correlate/pallas_call | solution.py:349
  94.3 0.4 all-to-all-done.2
  94.7 3.8 %all-to-all-start.3 = ((bf16[16,128,128]{2,1,0:T(8,128)(2,1)}), bf16[16,128,128]{2,1,0:T(8,128)(2,1)S(1)}, u32[]{:S(2)}, u32[]{:S(2)}) async-start(bf16[16,128,128]{2,1,0:T(8,128)(2,1)} %correlate.1), calls=%async_computation.3 | async-start | bytes 1048576 | tf_op jit(solution)/shard_map/all_to_all | solution.py:59
  98.5 0.1 reduce_sum.12
  98.6 6.9 %collective-permute-start.8 = (bf16[128,512]{1,0:T(8,128)(2,1)S(1)}, bf16[128,512]{1,0:T(8,128)(2,1)S(1)}, u32[]{:S(2)}, u32[]{:S(2)}) collective-permute-start(bf16[128,512]{1,0:T(8,128)(2,1)S(1)} %reduce_sum.12), channel_id=1, source_target_pairs={{0,0},{1,1},{2,32},{3,33},{4,64},{5,65},{6,96},{7,97},{8,8},{9,9},... | collective-permute-start | bytes 393224 | tf_op jit(solution)/shard_map/ppermute | solution.py:47
  105.6 0.9 convert_add_fusion
  106.5 4.8 %all-to-all-done.3.got_ref = bf16[16,128,128]{2,1,0:T(8,128)(2,1)S(1)} async-done(((bf16[16,128,128]{2,1,0:T(8,128)(2,1)}), bf16[16,128,128]{2,1,0:T(8,128)(2,1)S(1)}, u32[]{:S(2)}, u32[]{:S(2)}) %all-to-all-start.3) | async-done | bytes 524320 | tf_op jit(solution)/shard_map/all_to_all | solution.py:59
  111.3 1.3 %unpack.1 = (bf16[3,128,512]{2,1,0:T(8,128)(2,1)}, f32[128,512]{1,0:T(8,128)}) custom-call(bf16[16,128,128]{2,1,0:T(8,128)(2,1)S(1)} %all-to-all-done.3.got_ref), custom_call_target="tpu_custom_call" | custom-call | flops 1000000000 | bytes 2000000 | tf_op jit(solution)/shard_map/unpack/pallas_call | solution.py:462
  112.6 3.3 %collective-permute-done.8 = bf16[128,512]{1,0:T(8,128)(2,1)S(1)} collective-permute-done((bf16[128,512]{1,0:T(8,128)(2,1)S(1)}, bf16[128,512]{1,0:T(8,128)(2,1)S(1)}, u32[]{:S(2)}, u32[]{:S(2)}) %collective-permute-start.8) | collective-permute-done | bytes 131104 | tf_op jit(solution)/shard_map/ppermute | solution.py:47
  115.9 0.7 copy.14
  (21 shorter events, 0.1 us)
Async XLA Ops:
  0.6 22.7 %copy-start = (f32[3,3,512]{2,1,0:T(4,128)S(1)}, f32[3,3,512]{2,1,0:T(4,128)}, u32[]{:S(2)}) copy-start(f32[3,3,512]{2,1,0:T(4,128)} %param.12) | copy-start | bytes 55300
  0.6 10.6 %collective-permute-start = (bf16[128,512]{1,0:T(8,128)(2,1)}, bf16[128,512]{1,0:T(8,128)(2,1)S(1)}, u32[]{:S(2)}, u32[]{:S(2)}) collective-permute-start(bf16[128,512]{1,0:T(8,128)(2,1)} %param.15), channel_id=1, source_target_pairs={{0,0},{1,1},{2,32},{3,33},{4,64},{5,65},{6,96},{7,97},{8,8},{9,9},... | collective-permute-start | bytes 393224 | tf_op jit(solution)/shard_map/ppermute | solution.py:47
  5.3 16.0 %copy-start.1 = (bf16[512,256]{1,0:T(8,128)(2,1)S(1)}, bf16[512,256]{1,0:T(8,128)(2,1)}, u32[]{:S(2)}) copy-start(bf16[512,256]{1,0:T(8,128)(2,1)} %refs_0_.1) | copy-start | bytes 786436
  5.3 18.3 %copy-start.3 = (f32[3,32]{1,0:T(4,128)S(1)}, f32[3,32]{1,0:T(4,128)}, u32[]{:S(2)}) copy-start(f32[3,32]{1,0:T(4,128)} %constant.88.clone.1) | copy-start | bytes 1156
  11.2 10.1 %collective-permute-start.1 = (bf16[128,512]{1,0:T(8,128)(2,1)S(1)}, bf16[128,512]{1,0:T(8,128)(2,1)S(1)}, u32[]{:S(2)}, u32[]{:S(2)}) collective-permute-start(bf16[128,512]{1,0:T(8,128)(2,1)S(1)} %collective-permute-done), channel_id=1, source_target_pairs={{0,1},{1,0},{2,3},{3,2},{4,5},{5,4},{6,7},{7,6},{8,9},{9,8},{10,11... | collective-permute-start | bytes 393224 | tf_op jit(solution)/shard_map/ppermute | solution.py:534
  12.7 22.9 %all-to-all-start = ((bf16[16,128,128]{2,1,0:T(8,128)(2,1)}), bf16[16,128,128]{2,1,0:T(8,128)(2,1)S(1)}, u32[]{:S(2)}, u32[]{:S(2)}) async-start(bf16[16,128,128]{2,1,0:T(8,128)(2,1)} %pack.1), calls=%async_computation | async-start | bytes 1048576 | tf_op jit(solution)/shard_map/all_to_all | solution.py:59
  21.3 14.3 %collective-permute-start.3 = (bf16[512,256]{1,0:T(8,128)(2,1)S(1)}, bf16[512,256]{1,0:T(8,128)(2,1)S(1)}, u32[]{:S(2)}, u32[]{:S(2)}) collective-permute-start(bf16[512,256]{1,0:T(8,128)(2,1)S(1)} %copy-done.1), channel_id=1, source_target_pairs={{0,16},{8,24},{16,0},{24,8},{32,48},{40,56},{48,32},{56,40},{64,80... | collective-permute-start | bytes 786440 | tf_op jit(solution)/shard_map/ppermute | solution.py:537
  23.7 22.9 %collective-permute-start.2 = (bf16[512,256]{1,0:T(8,128)(2,1)S(1)}, bf16[512,256]{1,0:T(8,128)(2,1)S(1)}, u32[]{:S(2)}, u32[]{:S(2)}) collective-permute-start(bf16[512,256]{1,0:T(8,128)(2,1)S(1)} %copy-done.1), channel_id=1, source_target_pairs={{0,8},{8,0},{16,24},{24,16},{32,40},{40,32},{48,56},{56,48},{64,72... | collective-permute-start | bytes 786440 | tf_op jit(solution)/shard_map/ppermute | solution.py:538
  23.7 22.9 %collective-permute-start.7 = (bf16[2,128,512]{2,1,0:T(8,128)(2,1)S(1)}, bf16[2,128,512]{2,1,0:T(8,128)(2,1)S(1)}, u32[]{:S(2)}, u32[]{:S(2)}) collective-permute-start(bf16[2,128,512]{2,1,0:T(8,128)(2,1)S(1)} %pad_maximum_fusion.refs_4_), channel_id=1, source_target_pairs={{0,6},{1,7},{2,4},{3,5},{4,2},{5,3},{6,0},{7,1},{8,14},{9,15},{10,... | collective-permute-start | bytes 786440 | tf_op jit(solution)/shard_map/ppermute | solution.py:536
  26.0 20.6 %collective-permute-start.6 = (bf16[2,128,512]{2,1,0:T(8,128)(2,1)S(1)}, bf16[2,128,512]{2,1,0:T(8,128)(2,1)S(1)}, u32[]{:S(2)}, u32[]{:S(2)}) collective-permute-start(bf16[2,128,512]{2,1,0:T(8,128)(2,1)S(1)} %pad_maximum_fusion.refs_4_), channel_id=1, source_target_pairs={{0,4},{1,5},{2,6},{3,7},{4,0},{5,1},{6,2},{7,3},{8,12},{9,13},{10,... | collective-permute-start | bytes 786440 | tf_op jit(solution)/shard_map/ppermute | solution.py:536
  27.1 19.5 %collective-permute-start.5 = (bf16[2,128,512]{2,1,0:T(8,128)(2,1)S(1)}, bf16[2,128,512]{2,1,0:T(8,128)(2,1)S(1)}, u32[]{:S(2)}, u32[]{:S(2)}) collective-permute-start(bf16[2,128,512]{2,1,0:T(8,128)(2,1)S(1)} %pad_maximum_fusion.refs_4_), channel_id=1, source_target_pairs={{0,2},{1,3},{2,0},{3,1},{4,6},{5,7},{6,4},{7,5},{8,10},{9,11},{10,... | collective-permute-start | bytes 786440 | tf_op jit(solution)/shard_map/ppermute | solution.py:536
  35.6 11.0 %collective-permute-start.4 = (bf16[512,256]{1,0:T(8,128)(2,1)S(1)}, bf16[512,256]{1,0:T(8,128)(2,1)S(1)}, u32[]{:S(2)}, u32[]{:S(2)}) collective-permute-start(bf16[512,256]{1,0:T(8,128)(2,1)S(1)} %collective-permute-done.3.refs_2_), channel_id=1, source_target_pairs={{0,8},{8,0},{16,24},{24,16},{32,40},{40,32},{48,56},{56,48},{64,72... | collective-permute-start | bytes 786440 | tf_op jit(solution)/shard_map/ppermute | solution.py:539
  76.0 18.7 %all-to-all-start.2 = ((bf16[8,128,512]{2,1,0:T(8,128)(2,1)}), bf16[8,128,512]{2,1,0:T(8,128)(2,1)S(1)}, u32[]{:S(2)}, u32[]{:S(2)}) async-start(bf16[8,128,512]{2,1,0:T(8,128)(2,1)} %get-tuple-element.35), calls=%async_computation.2 | async-start | bytes 2097152 | tf_op jit(solution)/shard_map/all_to_all | solution.py:59
  81.5 24.0 %collective-permute-start.9 = (bf16[512,256]{1,0:T(8,128)(2,1)}, bf16[512,256]{1,0:T(8,128)(2,1)S(1)}, u32[]{:S(2)}, u32[]{:S(2)}) collective-permute-start(bf16[512,256]{1,0:T(8,128)(2,1)} %get-tuple-element.40), channel_id=1, source_target_pairs={{0,8},{8,0},{16,24},{24,16},{32,40},{40,32},{48,56},{56,48},{64,72... | collective-permute-start | bytes 786440 | tf_op jit(solution)/shard_map/ppermute | solution.py:552
  81.5 24.0 %collective-permute-start.10 = (bf16[512,256]{1,0:T(8,128)(2,1)}, bf16[512,256]{1,0:T(8,128)(2,1)S(1)}, u32[]{:S(2)}, u32[]{:S(2)}) collective-permute-start(bf16[512,256]{1,0:T(8,128)(2,1)} %get-tuple-element.41), channel_id=1, source_target_pairs={{0,16},{8,24},{16,0},{24,8},{32,48},{40,56},{48,32},{56,40},{64,80... | collective-permute-start | bytes 786440 | tf_op jit(solution)/shard_map/ppermute | solution.py:552
  81.5 24.0 %collective-permute-start.11 = (bf16[512,256]{1,0:T(8,128)(2,1)}, bf16[512,256]{1,0:T(8,128)(2,1)S(1)}, u32[]{:S(2)}, u32[]{:S(2)}) collective-permute-start(bf16[512,256]{1,0:T(8,128)(2,1)} %get-tuple-element.42), channel_id=1, source_target_pairs={{0,24},{8,16},{16,8},{24,0},{32,56},{40,48},{48,40},{56,32},{64,88... | collective-permute-start | bytes 786440 | tf_op jit(solution)/shard_map/ppermute | solution.py:552
  94.3 11.3 %copy-start.2 = (f32[512,256]{1,0:T(8,128)S(1)}, f32[512,256]{1,0:T(8,128)}, u32[]{:S(2)}) copy-start(f32[512,256]{1,0:T(8,128)} %get-tuple-element.39) | copy-start | bytes 1572868
  94.7 16.7 %all-to-all-start.3 = ((bf16[16,128,128]{2,1,0:T(8,128)(2,1)}), bf16[16,128,128]{2,1,0:T(8,128)(2,1)S(1)}, u32[]{:S(2)}, u32[]{:S(2)}) async-start(bf16[16,128,128]{2,1,0:T(8,128)(2,1)} %correlate.1), calls=%async_computation.3 | async-start | bytes 1048576 | tf_op jit(solution)/shard_map/all_to_all | solution.py:59
  98.6 17.3 %collective-permute-start.8 = (bf16[128,512]{1,0:T(8,128)(2,1)S(1)}, bf16[128,512]{1,0:T(8,128)(2,1)S(1)}, u32[]{:S(2)}, u32[]{:S(2)}) collective-permute-start(bf16[128,512]{1,0:T(8,128)(2,1)S(1)} %reduce_sum.12), channel_id=1, source_target_pairs={{0,0},{1,1},{2,32},{3,33},{4,64},{5,65},{6,96},{7,97},{8,8},{9,9},... | collective-permute-start | bytes 393224 | tf_op jit(solution)/shard_map/ppermute | solution.py:47

commit v5 on v4

--- a/solution.py
+++ b/solution.py
@@ -529,14 +529,12 @@
     consts = [jnp.asarray(table) for table in tables()]
 
     packed = pack(projected.transpose(1, 0, 2), long_filter)
-    moved, packed = lax.optimization_barrier((swapped(d_out), packed))
+    moved = swapped(d_out)
     signals = exchange(packed, "seq")
     pair = jnp.stack([moved, lax.ppermute(moved, "chan", chan_pairs(1))])
     pair, late = lax.optimization_barrier((pair, w_out))
     cots = [pair] + [lax.ppermute(pair, "chan", chan_pairs(2 * far)) for far in range(1, FAR)]
-    across = lax.ppermute(late, "seq", near_pairs(2))
-    weights = [late, lax.ppermute(late, "seq", near_pairs(1)), across,
-               lax.ppermute(across, "seq", near_pairs(1))]
+    weights = [late] + [lax.ppermute(late, "seq", near_pairs(step)) for step in range(1, NEAR)]
 
     own = lax.dynamic_slice_in_dim(short_filter, seq_at * LANE, LANE, axis=2).reshape(3, 3 * LANE)
     plain = jnp.zeros((3, LANE), F32).at[0].set(1.0)

time: 117 us -> 120 us (1.026)
  waiting for transfers between devices: 19.5 us -> 22.3 us
    ppermute x2, waiting for transfers between devices: 6.79 us -> 9.2 us  [swapped(): return lax.ppermute(array, ('seq', 'chan'), swap_pairs())]
  transfers between devices with their start and end apart: 15 -> 15, of which waited for: 5 -> 5; matrix products, arithmetic and copies ran while one was open for 1% -> 1% of each run, Pallas kernels for 22% -> 21%
where the time goes in v5:
time: 120 us; the launch traced here: 119 us
  starting transfers between devices  39 us (32%)
  Pallas kernels  30.5 us (25%)
  blocking collectives  24.7 us (21%)
  waiting for transfers between devices  22.3 us (19%)
  other arithmetic  1.25 us (1%)
    all_to_all x1, blocking collectives, exchange(): return lax.all_to_all(array, axis, 0, 0, tiled=True)  24.7 us
    all_to_all x3, starting transfers between devices, exchange(): return lax.all_to_all(array, axis, 0, 0, tiled=True)  17.2 us
    ppermute x2, starting transfers between devices, swapped(): return lax.ppermute(array, ('seq', 'chan'), swap_pairs())  11.5 us
    pallas_call x1, Pallas kernels, correlate(): pl.pallas_call(backward_kernel, out_shape=jax.ShapeDtypeStruct((SEQ, ROWS...  10.9 us
    pallas_call x1, Pallas kernels, convolve(): pl.pallas_call(forward_kernel, out_shape=(jax.ShapeDtypeStruct((NEAR, LAN...  10.9 us
    ppermute x2, waiting for transfers between devices, swapped(): return lax.ppermute(array, ('seq', 'chan'), swap_pairs())  9.2 us
    pallas_call x4, Pallas kernels, call(): pl.pallas_call(kernel, out_shape=out_shape, grid=(1,), in_specs=in_specs,...  8.68 us
    ppermute x3, waiting for transfers between devices, shards(): lax.ppermute(late, 'seq', near_pairs(step))  7.93 us
  transfers between devices with their start and end apart: 15, of which 5 were waited for; matrix products, arithmetic and copies ran while one was open for 1% of the time, Pallas kernels for 21%

profile of v5, /device:TPU:32, one launch (start us, length us, event | category | flops | bytes accessed | tf_op | source)
XLA Modules:
  0.0 119.3 jit_solution(14688068389550737614)
XLA Ops:
  0.6 4.6 %collective-permute-start = (bf16[128,512]{1,0:T(8,128)(2,1)}, bf16[128,512]{1,0:T(8,128)(2,1)S(1)}, u32[]{:S(2)}, u32[]{:S(2)}) collective-permute-start(bf16[128,512]{1,0:T(8,128)(2,1)} %param.15), channel_id=1, source_target_pairs={{0,0},{1,1},{2,32},{3,33},{4,64},{5,65},{6,96},{7,97},{8,8},{9,9},... | collective-permute-start | bytes 393224 | tf_op jit(solution)/shard_map/ppermute | solution.py:47
  5.3 5.9 %collective-permute-done = bf16[128,512]{1,0:T(8,128)(2,1)S(1)} collective-permute-done((bf16[128,512]{1,0:T(8,128)(2,1)}, bf16[128,512]{1,0:T(8,128)(2,1)S(1)}, u32[]{:S(2)}, u32[]{:S(2)}) %collective-permute-start) | collective-permute-done | bytes 131104 | tf_op jit(solution)/shard_map/ppermute | solution.py:47
  11.2 1.5 %collective-permute-start.1 = (bf16[128,512]{1,0:T(8,128)(2,1)S(1)}, bf16[128,512]{1,0:T(8,128)(2,1)S(1)}, u32[]{:S(2)}, u32[]{:S(2)}) collective-permute-start(bf16[128,512]{1,0:T(8,128)(2,1)S(1)} %collective-permute-done), channel_id=1, source_target_pairs={{0,1},{1,0},{2,3},{3,2},{4,5},{5,4},{6,7},{7,6},{8,9},{9,8},{10,11... | collective-permute-start | bytes 393224 | tf_op jit(solution)/shard_map/ppermute | solution.py:534
  12.7 2.4 %pack.1 = bf16[16,128,128]{2,1,0:T(8,128)(2,1)} custom-call(bf16[3,128,512]{2,1,0:T(8,128)(2,1)} %bitcast.11, f32[128,512]{1,0:T(8,128)} %filter_ref.1), custom_call_target="tpu_custom_call" | custom-call | flops 1000000000 | bytes 2000000 | tf_op jit(solution)/shard_map/pack/pallas_call | solution.py:462
  15.1 8.6 %all-to-all-start = ((bf16[16,128,128]{2,1,0:T(8,128)(2,1)}), bf16[16,128,128]{2,1,0:T(8,128)(2,1)S(1)}, u32[]{:S(2)}, u32[]{:S(2)}) async-start(bf16[16,128,128]{2,1,0:T(8,128)(2,1)} %pack.1), calls=%async_computation | async-start | bytes 1048576 | tf_op jit(solution)/shard_map/all_to_all | solution.py:59
  23.7 1.7 %collective-permute-start.4 = (bf16[512,256]{1,0:T(8,128)(2,1)S(1)}, bf16[512,256]{1,0:T(8,128)(2,1)S(1)}, u32[]{:S(2)}, u32[]{:S(2)}) collective-permute-start(bf16[512,256]{1,0:T(8,128)(2,1)S(1)} %copy-done.1), channel_id=1, source_target_pairs={{0,24},{8,16},{16,8},{24,0},{32,56},{40,48},{48,40},{56,32},{64,88... | collective-permute-start | bytes 786440 | tf_op jit(solution)/shard_map/ppermute | solution.py:537
  25.5 0.1 constant_dynamic-slice_fusion
  25.6 0.1 reshape.37
  25.7 0.1 pad_add_fusion.place_ref
  25.7 0.1 pad_maximum_fusion.1.taps_ref
  25.8 0.4 collective-permute-start.3
  26.2 0.1 collective-permute-start.2
  26.3 2.2 %collective-permute-start.7 = (bf16[2,128,512]{2,1,0:T(8,128)(2,1)S(1)}, bf16[2,128,512]{2,1,0:T(8,128)(2,1)S(1)}, u32[]{:S(2)}, u32[]{:S(2)}) collective-permute-start(bf16[2,128,512]{2,1,0:T(8,128)(2,1)S(1)} %pad_maximum_fusion.refs_4_), channel_id=1, source_target_pairs={{0,6},{1,7},{2,4},{3,5},{4,2},{5,3},{6,0},{7,1},{8,14},{9,15},{10,... | collective-permute-start | bytes 786440 | tf_op jit(solution)/shard_map/ppermute | solution.py:536
  28.5 1.2 collective-permute-start.6
  29.6 7.9 %collective-permute-done.4.refs_3_ = bf16[512,256]{1,0:T(8,128)(2,1)S(1)} collective-permute-done((bf16[512,256]{1,0:T(8,128)(2,1)S(1)}, bf16[512,256]{1,0:T(8,128)(2,1)S(1)}, u32[]{:S(2)}, u32[]{:S(2)}) %collective-permute-start.4) | collective-permute-done | bytes 262176 | tf_op jit(solution)/shard_map/ppermute | solution.py:537
  37.6 1.3 %collective-permute-start.5 = (bf16[2,128,512]{2,1,0:T(8,128)(2,1)S(1)}, bf16[2,128,512]{2,1,0:T(8,128)(2,1)S(1)}, u32[]{:S(2)}, u32[]{:S(2)}) collective-permute-start(bf16[2,128,512]{2,1,0:T(8,128)(2,1)S(1)} %pad_maximum_fusion.refs_4_), channel_id=1, source_target_pairs={{0,2},{1,3},{2,0},{3,1},{4,6},{5,7},{6,4},{7,5},{8,10},{9,11},{10,... | collective-permute-start | bytes 786440 | tf_op jit(solution)/shard_map/ppermute | solution.py:536
  38.9 10.9 %convolve.1 = (bf16[4,32,512]{2,1,0:T(8,128)(2,1)S(1)}, f32[2048,128]{1,0:T(8,128)}, f32[33,128,128]{2,1,0:T(8,128)}) custom-call(bf16[2048,128]{1,0:T(8,128)(2,1)S(1)} %bitcast.8, f32[3,128]{1,0:T(4,128)S(1)} %pad_maximum_fusion.1.taps_ref, bf16[64,72,96]{2,1,0:T(8,128)(2,1)} %constant.90.clone.first_hbm, bf16[128,384]{1,0:T(8,128)(2,1)} %constant.91.clone.ahead_hbm, ...), custom_call_target="tpu_custom_call" | custom-call | flops 8000000000 | bytes 6000000 | tf_op jit(solution)/shard_map/convolve/pallas_call | solution.py:323
  49.8 1.7 %send.1 = bf16[16,64,512]{2,1,0:T(8,128)(2,1)S(1)} custom-call(s32[3]{0:T(128)S(1)} %pad_add_fusion.place_ref, bf16[4,32,512]{2,1,0:T(8,128)(2,1)S(1)} %get-tuple-element.28.gated_ref, bf16[512,256]{1,0:T(8,128)(2,1)S(1)} %copy-done.1, bf16[512,256]{1,0:T(8,128)(2,1)S(1)} %collective-permute-done.2.refs_1_, ...), custom_call_target="tpu_custom_call" | custom-call | flops 1000000000 | bytes 2000000 | tf_op jit(solution)/shard_map/send/pallas_call | solution.py:462
  51.6 24.7 %all_to_all.20.got_ref.share_ref = bf16[16,64,512]{2,1,0:T(8,128)(2,1)S(1)} all-to-all(bf16[16,64,512]{2,1,0:T(8,128)(2,1)S(1)} %send.1), channel_id=1, replica_groups=mesh['seq'=16,'chan'=8] {'seq'}, dimensions={0} | all-to-all | bytes 2097152 | tf_op jit(solution)/shard_map/all_to_all | solution.py:59
  76.2 3.2 %products.1 = (bf16[8,128,512]{2,1,0:T(8,128)(2,1)}, f32[512,256]{1,0:T(8,128)}, bf16[512,256]{1,0:T(8,128)(2,1)}, bf16[512,256]{1,0:T(8,128)(2,1)}, bf16[512,256]{1,0:T(8,128)(2,1)}) custom-call(s32[3]{0:T(128)S(1)} %pad_add_fusion.place_ref, bf16[16,64,512]{2,1,0:T(8,128)(2,1)S(1)} %all_to_all.20.got_ref.share_ref, bf16[512,256]{1,0:T(8,128)(2,1)S(1)} %copy-done.1, ...), custom_call_target="tpu_custom_call" | custom-call | flops 1000000000 | bytes 2000000 | tf_op jit(solution)/shard_map/products/pallas_call | solution.py:462
  79.5 4.8 %all-to-all-start.2 = ((bf16[8,128,512]{2,1,0:T(8,128)(2,1)}), bf16[8,128,512]{2,1,0:T(8,128)(2,1)S(1)}, u32[]{:S(2)}, u32[]{:S(2)}) async-start(bf16[8,128,512]{2,1,0:T(8,128)(2,1)} %get-tuple-element.31), calls=%async_computation.2 | async-start | bytes 2097152 | tf_op jit(solution)/shard_map/all_to_all | solution.py:59
  84.3 1.9 %collective-permute-start.11 = (bf16[512,256]{1,0:T(8,128)(2,1)}, bf16[512,256]{1,0:T(8,128)(2,1)S(1)}, u32[]{:S(2)}, u32[]{:S(2)}) collective-permute-start(bf16[512,256]{1,0:T(8,128)(2,1)} %get-tuple-element.38), channel_id=1, source_target_pairs={{0,24},{8,16},{16,8},{24,0},{32,56},{40,48},{48,40},{56,32},{64,88... | collective-permute-start | bytes 786440 | tf_op jit(solution)/shard_map/ppermute | solution.py:550
  86.2 10.9 %correlate.1 = bf16[16,128,128]{2,1,0:T(8,128)(2,1)} custom-call(bf16[16,64,512]{2,1,0:T(8,128)(2,1)S(1)} %all_to_all.20.got_ref.share_ref, f32[2048,128]{1,0:T(8,128)} %get-tuple-element.32.kept_hbm, f32[33,128,128]{2,1,0:T(8,128)} %get-tuple-element.33.spec_hbm, f32[3,128]{1,0:T(4,128)S(1)} %pad_maximum_fusion.1.taps_ref, ...), custom_call_target="tpu_custom_call" | custom-call | flops 8000000000 | bytes 6000000 | tf_op jit(solution)/shard_map/correlate/pallas_call | solution.py:349
  97.1 0.4 all-to-all-done.2
  97.5 3.8 %all-to-all-start.3 = ((bf16[16,128,128]{2,1,0:T(8,128)(2,1)}), bf16[16,128,128]{2,1,0:T(8,128)(2,1)S(1)}, u32[]{:S(2)}, u32[]{:S(2)}) async-start(bf16[16,128,128]{2,1,0:T(8,128)(2,1)} %correlate.1), calls=%async_computation.3 | async-start | bytes 1048576 | tf_op jit(solution)/shard_map/all_to_all | solution.py:59
  101.3 0.1 reduce_sum.12
  101.4 6.9 %collective-permute-start.8 = (bf16[128,512]{1,0:T(8,128)(2,1)S(1)}, bf16[128,512]{1,0:T(8,128)(2,1)S(1)}, u32[]{:S(2)}, u32[]{:S(2)}) collective-permute-start(bf16[128,512]{1,0:T(8,128)(2,1)S(1)} %reduce_sum.12), channel_id=1, source_target_pairs={{0,0},{1,1},{2,32},{3,33},{4,64},{5,65},{6,96},{7,97},{8,8},{9,9},... | collective-permute-start | bytes 393224 | tf_op jit(solution)/shard_map/ppermute | solution.py:47
  108.4 0.9 convert_add_fusion
  109.3 4.8 %all-to-all-done.3.got_ref = bf16[16,128,128]{2,1,0:T(8,128)(2,1)S(1)} async-done(((bf16[16,128,128]{2,1,0:T(8,128)(2,1)}), bf16[16,128,128]{2,1,0:T(8,128)(2,1)S(1)}, u32[]{:S(2)}, u32[]{:S(2)}) %all-to-all-start.3) | async-done | bytes 524320 | tf_op jit(solution)/shard_map/all_to_all | solution.py:59
  114.1 1.3 %unpack.1 = (bf16[3,128,512]{2,1,0:T(8,128)(2,1)}, f32[128,512]{1,0:T(8,128)}) custom-call(bf16[16,128,128]{2,1,0:T(8,128)(2,1)S(1)} %all-to-all-done.3.got_ref), custom_call_target="tpu_custom_call" | custom-call | flops 1000000000 | bytes 2000000 | tf_op jit(solution)/shard_map/unpack/pallas_call | solution.py:462
  115.4 3.3 %collective-permute-done.8 = bf16[128,512]{1,0:T(8,128)(2,1)S(1)} collective-permute-done((bf16[128,512]{1,0:T(8,128)(2,1)S(1)}, bf16[128,512]{1,0:T(8,128)(2,1)S(1)}, u32[]{:S(2)}, u32[]{:S(2)}) %collective-permute-start.8) | collective-permute-done | bytes 131104 | tf_op jit(solution)/shard_map/ppermute | solution.py:47
  118.7 0.7 copy.14
  (21 shorter events, 0.1 us)
Async XLA Ops:
  0.6 24.9 %copy-start = (f32[3,3,512]{2,1,0:T(4,128)S(1)}, f32[3,3,512]{2,1,0:T(4,128)}, u32[]{:S(2)}) copy-start(f32[3,3,512]{2,1,0:T(4,128)} %param.12) | copy-start | bytes 55300
  0.6 10.6 %collective-permute-start = (bf16[128,512]{1,0:T(8,128)(2,1)}, bf16[128,512]{1,0:T(8,128)(2,1)S(1)}, u32[]{:S(2)}, u32[]{:S(2)}) collective-permute-start(bf16[128,512]{1,0:T(8,128)(2,1)} %param.15), channel_id=1, source_target_pairs={{0,0},{1,1},{2,32},{3,33},{4,64},{5,65},{6,96},{7,97},{8,8},{9,9},... | collective-permute-start | bytes 393224 | tf_op jit(solution)/shard_map/ppermute | solution.py:47
  11.2 12.5 %collective-permute-start.1 = (bf16[128,512]{1,0:T(8,128)(2,1)S(1)}, bf16[128,512]{1,0:T(8,128)(2,1)S(1)}, u32[]{:S(2)}, u32[]{:S(2)}) collective-permute-start(bf16[128,512]{1,0:T(8,128)(2,1)S(1)} %collective-permute-done), channel_id=1, source_target_pairs={{0,1},{1,0},{2,3},{3,2},{4,5},{5,4},{6,7},{7,6},{8,9},{9,8},{10,11... | collective-permute-start | bytes 393224 | tf_op jit(solution)/shard_map/ppermute | solution.py:534
  12.7 11.0 %copy-start.1 = (bf16[512,256]{1,0:T(8,128)(2,1)S(1)}, bf16[512,256]{1,0:T(8,128)(2,1)}, u32[]{:S(2)}) copy-start(bf16[512,256]{1,0:T(8,128)(2,1)} %refs_0_.1) | copy-start | bytes 786436
  12.7 13.0 %copy-start.3 = (f32[3,32]{1,0:T(4,128)S(1)}, f32[3,32]{1,0:T(4,128)}, u32[]{:S(2)}) copy-start(f32[3,32]{1,0:T(4,128)} %constant.88.clone.1) | copy-start | bytes 1156
  15.1 23.7 %all-to-all-start = ((bf16[16,128,128]{2,1,0:T(8,128)(2,1)}), bf16[16,128,128]{2,1,0:T(8,128)(2,1)S(1)}, u32[]{:S(2)}, u32[]{:S(2)}) async-start(bf16[16,128,128]{2,1,0:T(8,128)(2,1)} %pack.1), calls=%async_computation | async-start | bytes 1048576 | tf_op jit(solution)/shard_map/all_to_all | solution.py:59
  23.7 13.8 %collective-permute-start.4 = (bf16[512,256]{1,0:T(8,128)(2,1)S(1)}, bf16[512,256]{1,0:T(8,128)(2,1)S(1)}, u32[]{:S(2)}, u32[]{:S(2)}) collective-permute-start(bf16[512,256]{1,0:T(8,128)(2,1)S(1)} %copy-done.1), channel_id=1, source_target_pairs={{0,24},{8,16},{16,8},{24,0},{32,56},{40,48},{48,40},{56,32},{64,88... | collective-permute-start | bytes 786440 | tf_op jit(solution)/shard_map/ppermute | solution.py:537
  25.8 24.0 %collective-permute-start.3 = (bf16[512,256]{1,0:T(8,128)(2,1)S(1)}, bf16[512,256]{1,0:T(8,128)(2,1)S(1)}, u32[]{:S(2)}, u32[]{:S(2)}) collective-permute-start(bf16[512,256]{1,0:T(8,128)(2,1)S(1)} %copy-done.1), channel_id=1, source_target_pairs={{0,16},{8,24},{16,0},{24,8},{32,48},{40,56},{48,32},{56,40},{64,80... | collective-permute-start | bytes 786440 | tf_op jit(solution)/shard_map/ppermute | solution.py:537
  26.2 23.6 %collective-permute-start.2 = (bf16[512,256]{1,0:T(8,128)(2,1)S(1)}, bf16[512,256]{1,0:T(8,128)(2,1)S(1)}, u32[]{:S(2)}, u32[]{:S(2)}) collective-permute-start(bf16[512,256]{1,0:T(8,128)(2,1)S(1)} %copy-done.1), channel_id=1, source_target_pairs={{0,8},{8,0},{16,24},{24,16},{32,40},{40,32},{48,56},{56,48},{64,72... | collective-permute-start | bytes 786440 | tf_op jit(solution)/shard_map/ppermute | solution.py:537
  26.3 23.5 %collective-permute-start.7 = (bf16[2,128,512]{2,1,0:T(8,128)(2,1)S(1)}, bf16[2,128,512]{2,1,0:T(8,128)(2,1)S(1)}, u32[]{:S(2)}, u32[]{:S(2)}) collective-permute-start(bf16[2,128,512]{2,1,0:T(8,128)(2,1)S(1)} %pad_maximum_fusion.refs_4_), channel_id=1, source_target_pairs={{0,6},{1,7},{2,4},{3,5},{4,2},{5,3},{6,0},{7,1},{8,14},{9,15},{10,... | collective-permute-start | bytes 786440 | tf_op jit(solution)/shard_map/ppermute | solution.py:536
  28.5 21.3 %collective-permute-start.6 = (bf16[2,128,512]{2,1,0:T(8,128)(2,1)S(1)}, bf16[2,128,512]{2,1,0:T(8,128)(2,1)S(1)}, u32[]{:S(2)}, u32[]{:S(2)}) collective-permute-start(bf16[2,128,512]{2,1,0:T(8,128)(2,1)S(1)} %pad_maximum_fusion.refs_4_), channel_id=1, source_target_pairs={{0,4},{1,5},{2,6},{3,7},{4,0},{5,1},{6,2},{7,3},{8,12},{9,13},{10,... | collective-permute-start | bytes 786440 | tf_op jit(solution)/shard_map/ppermute | solution.py:536
  37.6 12.2 %collective-permute-start.5 = (bf16[2,128,512]{2,1,0:T(8,128)(2,1)S(1)}, bf16[2,128,512]{2,1,0:T(8,128)(2,1)S(1)}, u32[]{:S(2)}, u32[]{:S(2)}) collective-permute-start(bf16[2,128,512]{2,1,0:T(8,128)(2,1)S(1)} %pad_maximum_fusion.refs_4_), channel_id=1, source_target_pairs={{0,2},{1,3},{2,0},{3,1},{4,6},{5,7},{6,4},{7,5},{8,10},{9,11},{10,... | collective-permute-start | bytes 786440 | tf_op jit(solution)/shard_map/ppermute | solution.py:536
  79.5 18.0 %all-to-all-start.2 = ((bf16[8,128,512]{2,1,0:T(8,128)(2,1)}), bf16[8,128,512]{2,1,0:T(8,128)(2,1)S(1)}, u32[]{:S(2)}, u32[]{:S(2)}) async-start(bf16[8,128,512]{2,1,0:T(8,128)(2,1)} %get-tuple-element.31), calls=%async_computation.2 | async-start | bytes 2097152 | tf_op jit(solution)/shard_map/all_to_all | solution.py:59
  84.3 24.0 %collective-permute-start.9 = (bf16[512,256]{1,0:T(8,128)(2,1)}, bf16[512,256]{1,0:T(8,128)(2,1)S(1)}, u32[]{:S(2)}, u32[]{:S(2)}) collective-permute-start(bf16[512,256]{1,0:T(8,128)(2,1)} %get-tuple-element.36), channel_id=1, source_target_pairs={{0,8},{8,0},{16,24},{24,16},{32,40},{40,32},{48,56},{56,48},{64,72... | collective-permute-start | bytes 786440 | tf_op jit(solution)/shard_map/ppermute | solution.py:550
  84.3 24.0 %collective-permute-start.10 = (bf16[512,256]{1,0:T(8,128)(2,1)}, bf16[512,256]{1,0:T(8,128)(2,1)S(1)}, u32[]{:S(2)}, u32[]{:S(2)}) collective-permute-start(bf16[512,256]{1,0:T(8,128)(2,1)} %get-tuple-element.37), channel_id=1, source_target_pairs={{0,16},{8,24},{16,0},{24,8},{32,48},{40,56},{48,32},{56,40},{64,80... | collective-permute-start | bytes 786440 | tf_op jit(solution)/shard_map/ppermute | solution.py:550
  84.3 24.0 %collective-permute-start.11 = (bf16[512,256]{1,0:T(8,128)(2,1)}, bf16[512,256]{1,0:T(8,128)(2,1)S(1)}, u32[]{:S(2)}, u32[]{:S(2)}) collective-permute-start(bf16[512,256]{1,0:T(8,128)(2,1)} %get-tuple-element.38), channel_id=1, source_target_pairs={{0,24},{8,16},{16,8},{24,0},{32,56},{40,48},{48,40},{56,32},{64,88... | collective-permute-start | bytes 786440 | tf_op jit(solution)/shard_map/ppermute | solution.py:550
  97.1 11.3 %copy-start.2 = (f32[512,256]{1,0:T(8,128)S(1)}, f32[512,256]{1,0:T(8,128)}, u32[]{:S(2)}) copy-start(f32[512,256]{1,0:T(8,128)} %get-tuple-element.35) | copy-start | bytes 1572868
  97.5 16.7 %all-to-all-start.3 = ((bf16[16,128,128]{2,1,0:T(8,128)(2,1)}), bf16[16,128,128]{2,1,0:T(8,128)(2,1)S(1)}, u32[]{:S(2)}, u32[]{:S(2)}) async-start(bf16[16,128,128]{2,1,0:T(8,128)(2,1)} %correlate.1), calls=%async_computation.3 | async-start | bytes 1048576 | tf_op jit(solution)/shard_map/all_to_all | solution.py:59
  101.4 17.3 %collective-permute-start.8 = (bf16[128,512]{1,0:T(8,128)(2,1)S(1)}, bf16[128,512]{1,0:T(8,128)(2,1)S(1)}, u32[]{:S(2)}, u32[]{:S(2)}) collective-permute-start(bf16[128,512]{1,0:T(8,128)(2,1)S(1)} %reduce_sum.12), channel_id=1, source_target_pairs={{0,0},{1,1},{2,32},{3,33},{4,64},{5,65},{6,96},{7,97},{8,8},{9,9},... | collective-permute-start | bytes 393224 | tf_op jit(solution)/shard_map/ppermute | solution.py:47

commit v6 on v2

--- a/solution.py
+++ b/solution.py
@@ -104,6 +104,10 @@
     lax.fori_loop(0, count // width, body, 0)
 
 
+def column_rows(n2):
+    return pl.ds(pl.multiple_of(n2 * 32, 32), 32)
+
+
 def lanes_of(rows):
     return lax.broadcasted_iota(jnp.int32, (rows, 4 * LANE), 1)
 
@@ -159,7 +163,7 @@
         before = wide_ref[pl.ds(n2 + 7, 32, stride=64), :]
         earlier = wide_ref[pl.ds(n2 + 6, 32, stride=64), :]
         mixed = tap0 * now + tap1 * before + tap2 * earlier
-        kept_ref[pl.ds(n2, 32, stride=64), :] = mixed
+        kept_ref[column_rows(n2), :] = mixed
         carried = mixed * pltpu.roll(mixed, LANE, 1)
         data = jnp.where((lane >= 2 * LANE) & (lane < 3 * LANE), carried, mixed)
         mid_ref[pl.ds(pl.multiple_of(n2 * MID, 8), MID), :] = matmul(first_ref[n2], pieces(data))
@@ -189,15 +193,23 @@
 
     def final(n2):
         conv = matmul(last_ref[n2], pieces(back_ref[pl.ds(n2, BACK, stride=64), :]))
-        mixed = kept_ref[pl.ds(n2, 32, stride=64), :]
+        mixed = kept_ref[column_rows(n2), :]
         column_ref[pl.ds(n2, 32, stride=64), :] = mixed * pltpu.roll(conv, 2 * LANE, 1)
-        kept_ref[pl.ds(n2, 32, stride=64), :] = jnp.where(
+        kept_ref[column_rows(n2), :] = jnp.where(
             lane < 3 * LANE, mixed, pltpu.roll(conv, LANE, 1)
         )
 
     last_copy.wait()
-    every(64, WIDE, final)
-    kept_copy = started(kept_ref, kept_hbm, sems.at[5])
+
+    def block_of(block, carry):
+        for at in range(WIDE):
+            final(block * WIDE + at)
+        rows = pl.ds(pl.multiple_of(block * WIDE * 32, 32), WIDE * 32)
+        started(kept_ref.at[rows], kept_hbm.at[rows], sems.at[5])
+        return carry
+
+    lax.fori_loop(0, 64 // WIDE, block_of, 0)
+    kept_copy = pltpu.make_async_copy(kept_ref, kept_hbm, sems.at[5])
 
     for block in range(SEQ):
         a, i = divmod(block, NEAR)
@@ -232,7 +244,7 @@
     lane = lanes_of(32)
 
     def outer(n2):
-        kept = kept_ref[pl.ds(n2, 32, stride=64), :]
+        kept = kept_ref[column_rows(n2), :]
         query = jnp.where(lane < 3 * LANE, pltpu.roll(kept, 2 * LANE, 1), pltpu.roll(kept, 3 * LANE, 1))
         data = grad_ref[pl.ds(n2, 32, stride=64), :] * query
         mid_ref[pl.ds(pl.multiple_of(n2 * MID, 8), MID), :] = matmul(first_ref[n2], pieces(data))
@@ -267,7 +279,7 @@
 
     def final(n2):
         found = matmul(last_ref[n2], pieces(back_ref[pl.ds(n2, BACK, stride=64), :]))
-        kept = kept_ref[pl.ds(n2, 32, stride=64), :]
+        kept = kept_ref[column_rows(n2), :]
         grad = grad_ref[pl.ds(n2, 32, stride=64), :]
         up, down = pltpu.roll(kept, LANE, 1), pltpu.roll(kept, 3 * LANE, 1)
         mixed = jnp.where(
@@ -366,11 +378,22 @@
     )(shares, resident(kept), resident(spec), taps, *(resident(x) for x in consts))
 
 
-def pack_kernel(streams_ref, filter_ref, out_ref):
+def pack_kernel(streams_hbm, filter_hbm, out_hbm, streams_ref, filter_ref, out_ref, sems):
     lane = lanes_of(ROWS)
-    for column in range(COLS // 128):
-        at = slice(column * 128, (column + 1) * 128)
-        blocks = [streams_ref[j, :, at].astype(F32) for j in range(3)] + [filter_ref[:, at]]
+    columns = range(COLS // 128)
+    spans = [slice(column * 128, (column + 1) * 128) for column in columns]
+    arrivals = [
+        (
+            started(streams_hbm.at[:, :, span], streams_ref.at[column], sems.at[column]),
+            started(filter_hbm.at[:, span], filter_ref.at[column], sems.at[4 + column]),
+        )
+        for column, span in zip(columns, spans)
+    ]
+    departures = []
+    for column in columns:
+        for copy in arrivals[column]:
+            copy.wait()
+        blocks = [streams_ref[column, j].astype(F32) for j in range(3)] + [filter_ref[column]]
         for part in range(4):
             placed = [pltpu.roll(b, ((j - part) % 4) * LANE, 1) if j != part else b
                       for j, b in enumerate(blocks)]
@@ -378,6 +401,10 @@
             for j in range(2, -1, -1):
                 joined = jnp.where(lane < (j + 1) * LANE, placed[j], joined)
             out_ref[column * 4 + part] = joined.astype(BF16)
+        part = slice(column * 4, column * 4 + 4)
+        departures.append(started(out_ref.at[part], out_hbm.at[part], sems.at[8 + column]))
+    for copy in departures:
+        copy.wait()
 
 
 def unpack_kernel(got_ref, streams_ref, filter_ref):
@@ -403,18 +430,23 @@
     )
 
 
-def fetch(place_ref, refs, weights, cots, sems):
+def fetch_weights(place_ref, refs, weights, sems):
     copies = []
     for step in range(NEAR):
         low = pl.multiple_of((place_ref[0] ^ step) * 256, 256)
         copies.append(started(refs[step], weights.at[:, pl.ds(low, 256)], sems.at[step]))
+    return copies
+
+
+def fetch_cots(place_ref, refs, cots, sems):
+    copies = []
     for far in range(FAR):
         row = pl.multiple_of((place_ref[1] ^ far) * ROWS, ROWS)
         for side in range(2):
             low = pl.multiple_of((place_ref[2] ^ side) * COLS, COLS)
             copies.append(
                 started(
-                    refs[NEAR + far].at[side],
+                    refs[far].at[side],
                     cots.at[pl.ds(row, ROWS), pl.ds(low, COLS)],
                     sems.at[NEAR + 2 * far + side],
                 )
@@ -424,7 +456,8 @@
 
 def send_kernel(place_ref, gated_ref, *refs):
     sent_ref, weights, cots, sems = refs[NEAR + FAR :]
-    copies = fetch(place_ref, refs, weights, cots, sems)
+    copies = fetch_weights(place_ref, refs[:NEAR], weights, sems)
+    copies += fetch_cots(place_ref, refs[NEAR : NEAR + FAR], cots, sems)
     for s in range(SEQ):
         sent_ref[s, :LANE, :] = gated_ref[s % NEAR]
     for copy in copies:
@@ -434,10 +467,9 @@
         sent_ref[s, LANE:, :] = total[s * LANE : (s + 1) * LANE]
 
 
-def product_kernel(place_ref, got_ref, *refs):
-    out_ref, *grad_refs = refs[NEAR + FAR : NEAR + FAR + 1 + NEAR]
-    weights, cots, sems = refs[NEAR + FAR + 1 + NEAR :]
-    copies = fetch(place_ref, refs, weights, cots, sems)
+def output_kernel(place_ref, got_ref, *refs):
+    out_ref, weights, sems = refs[NEAR:]
+    copies = fetch_weights(place_ref, refs[:NEAR], weights, sems)
     turned = got_ref[...].reshape(COLS, FAR * ROWS).T
     for copy in copies:
         copy.wait()
@@ -445,7 +477,14 @@
         part = contract(turned, weights[:, side * COLS : (side + 1) * COLS], 1, 0).astype(BF16)
         for a in range(FAR):
             out_ref[2 * a + side] = part[a * ROWS : (a + 1) * ROWS]
+
+
+def weight_kernel(place_ref, got_ref, *refs):
+    grad_refs, (cots, sems) = refs[FAR : FAR + NEAR], refs[FAR + NEAR :]
+    copies = fetch_cots(place_ref, refs[:FAR], cots, sems)
     gated = got_ref[...].reshape(COLS, FAR * ROWS)
+    for copy in copies:
+        copy.wait()
     for step in range(NEAR):
         low = pl.multiple_of((place_ref[0] ^ step) * 256, 256)
         grad = contract(gated, cots[:, pl.ds(low, 256)], 1, 0)
@@ -477,10 +516,21 @@
 
 
 def pack(streams, long_filter, interpret=False):
-    shape = jax.ShapeDtypeStruct((SEQ, ROWS, 4 * LANE), BF16)
-    return call(
-        pack_kernel, "pack", shape, interpret, resident(streams), resident(long_filter)
-    )
+    return pl.pallas_call(
+        pack_kernel,
+        out_shape=pltpu.HBM((SEQ, ROWS, 4 * LANE), BF16),
+        in_specs=[FAR_OFF, FAR_OFF],
+        out_specs=FAR_OFF,
+        scratch_shapes=[
+            pltpu.VMEM((4, 3, ROWS, 128), BF16),
+            pltpu.VMEM((4, ROWS, 128), F32),
+            pltpu.VMEM((SEQ, ROWS, 4 * LANE), BF16),
+            pltpu.SemaphoreType.DMA((12,)),
+        ],
+        compiler_params=pltpu.CompilerParams(vmem_limit_bytes=VMEM_LIMIT),
+        interpret=interpret,
+        name="pack",
+    )(resident(streams), resident(long_filter))
 
 
 def unpack(got, interpret=False):
@@ -510,15 +560,22 @@
     )
 
 
-def products(place, got, weights, cots, interpret=False):
-    width = weights[0].shape[1]
-    shapes = (pltpu.HBM((CHAN, ROWS, COLS), BF16),) + tuple(
-        pltpu.HBM((COLS, width), BF16 if step else F32) for step in range(NEAR)
-    )
-    half = pl.BlockSpec((SEQ, LANE, FAR * ROWS), lambda _: (0, 0, 0))
+GATED = pl.BlockSpec((SEQ, LANE, FAR * ROWS), lambda _: (0, 0, 0))
+
+
+def output_shares(place, got, weights, interpret=False):
     return call(
-        product_kernel, "products", shapes, interpret, place, got, *weights, *cots,
-        specs={0: SCALAR, 1: half, **far_off(2, 2 + NEAR + FAR)}, scratch=GATHERED,
+        output_kernel, "outputs", pltpu.HBM((CHAN, ROWS, COLS), BF16), interpret,
+        place, got, *weights, specs={0: SCALAR, 1: GATED, **far_off(2, 2 + NEAR)},
+        scratch=(GATHERED[0], GATHERED[2]),
+    )
+
+
+def weight_shares(place, got, cots, width, interpret=False):
+    shapes = tuple(pltpu.HBM((COLS, width), BF16 if step else F32) for step in range(NEAR))
+    return call(
+        weight_kernel, "weights", shapes, interpret, place, got, *cots,
+        specs={0: SCALAR, 1: GATED, **far_off(2, 2 + FAR)}, scratch=GATHERED[1:],
     )
 
 
@@ -541,8 +598,8 @@
     gated, kept, spec = convolve(signals.reshape(TOKENS, 4 * LANE), taps, consts)
     got = exchange(to_send(place, gated, weights, cots), "seq")
 
-    partial_out, d_wout, *others = products(place, got, weights, cots)
-    shares = exchange(partial_out, "chan")
+    shares = exchange(output_shares(place, got, weights), "chan")
+    d_wout, *others = weight_shares(place, got, cots, w_out.shape[1])
     output = swapped(jnp.sum(shares.astype(F32), axis=0).astype(BF16))
     for step, piece in enumerate(others, 1):
         d_wout = d_wout + lax.ppermute(piece, "seq", near_pairs(step)).astype(F32)

time: 116 us -> 115 us (level)
  starting transfers between devices: 36.8 us -> 35.1 us
    pallas_call x0 -> x1, Pallas kernels: none -> 2.41 us  [pack(): pl.pallas_call(pack_kernel, out_shape=pltpu.HBM((SEQ, ROWS, 4 * LANE), BF...]
    pallas_call x1, Pallas kernels: 10.9 us -> 8.95 us  [convolve(): pl.pallas_call(forward_kernel, out_shape=(jax.ShapeDtypeStruct((NEAR, LAN...]
    ppermute x3, waiting for transfers between devices: 0.01 us -> 1.44 us  [shards(): lax.ppermute(pair, 'chan', chan_pairs(2 * far))]
where the time goes in v6:
time: 115 us
  starting transfers between devices  35.1 us (31%)
  Pallas kernels  29.8 us (26%)
  blocking collectives  24.5 us (21%)
  waiting for transfers between devices  22.5 us (20%)
  other arithmetic  1.26 us (1%)
    all_to_all x1, blocking collectives, exchange(): return lax.all_to_all(array, axis, 0, 0, tiled=True)  24.5 us
    all_to_all x3, starting transfers between devices, exchange(): return lax.all_to_all(array, axis, 0, 0, tiled=True)  15.8 us
    ppermute x2, waiting for transfers between devices, swapped(): return lax.ppermute(array, ('seq', 'chan'), swap_pairs())  10.8 us
    ppermute x2, starting transfers between devices, swapped(): return lax.ppermute(array, ('seq', 'chan'), swap_pairs())  10.6 us
    pallas_call x1, Pallas kernels, correlate(): pl.pallas_call(backward_kernel, out_shape=jax.ShapeDtypeStruct((SEQ, ROWS...  10.4 us
    pallas_call x1, Pallas kernels, convolve(): pl.pallas_call(forward_kernel, out_shape=(jax.ShapeDtypeStruct((NEAR, LAN...  8.95 us
    pallas_call x4, Pallas kernels, call(): pl.pallas_call(kernel, out_shape=out_shape, grid=(1,), in_specs=in_specs,...  8.04 us
    all_to_all x3, waiting for transfers between devices, exchange(): return lax.all_to_all(array, axis, 0, 0, tiled=True)  5.92 us
  transfers between devices with their start and end apart: 15, of which 5 were waited for; matrix products, arithmetic and copies ran while one was open for 1% of the time, Pallas kernels for 20%

profile of v6, /device:TPU:32, one launch (start us, length us, event | category | flops | bytes accessed | tf_op | source)
XLA Modules:
  0.0 114.9 jit_solution(15193612582751008167)
XLA Ops:
  0.7 2.4 %pack.1 = bf16[16,128,128]{2,1,0:T(8,128)(2,1)} custom-call(bf16[3,128,512]{2,1,0:T(8,128)(2,1)} %bitcast.9, f32[128,512]{1,0:T(8,128)} %filter_hbm.1), custom_call_target="tpu_custom_call" | custom-call | tf_op jit(solution)/shard_map/pack/pallas_call | solution.py:519
  3.1 7.0 %all-to-all-start = ((bf16[16,128,128]{2,1,0:T(8,128)(2,1)}), bf16[16,128,128]{2,1,0:T(8,128)(2,1)S(1)}, u32[]{:S(2)}, u32[]{:S(2)}) async-start(bf16[16,128,128]{2,1,0:T(8,128)(2,1)} %pack.1), calls=%async_computation | async-start | bytes 1048576 | tf_op jit(solution)/shard_map/all_to_all | solution.py:59
  10.2 4.9 %collective-permute-start.3 = (bf16[128,512]{1,0:T(8,128)(2,1)S(1)}, bf16[128,512]{1,0:T(8,128)(2,1)S(1)}, u32[]{:S(2)}, u32[]{:S(2)}) collective-permute-start(bf16[128,512]{1,0:T(8,128)(2,1)S(1)} %copy-done.4), channel_id=1, source_target_pairs={{0,0},{1,1},{2,32},{3,33},{4,64},{5,65},{6,96},{7,97},{8,8},{9,9},... | collective-permute-start | bytes 393224 | tf_op jit(solution)/shard_map/ppermute | solution.py:47
  15.1 0.1 collective-permute-start.2
  15.2 1.5 %collective-permute-start.1 = (bf16[512,256]{1,0:T(8,128)(2,1)S(1)}, bf16[512,256]{1,0:T(8,128)(2,1)S(1)}, u32[]{:S(2)}, u32[]{:S(2)}) collective-permute-start(bf16[512,256]{1,0:T(8,128)(2,1)S(1)} %copy-done.1), channel_id=1, source_target_pairs={{0,16},{8,24},{16,0},{24,8},{32,48},{40,56},{48,32},{56,40},{64,80... | collective-permute-start | bytes 786440 | tf_op jit(solution)/shard_map/ppermute | solution.py:592
  16.6 0.4 collective-permute-start
  17.1 8.7 %collective-permute-done.3 = bf16[128,512]{1,0:T(8,128)(2,1)S(1)} collective-permute-done((bf16[128,512]{1,0:T(8,128)(2,1)S(1)}, bf16[128,512]{1,0:T(8,128)(2,1)S(1)}, u32[]{:S(2)}, u32[]{:S(2)}) %collective-permute-start.3) | collective-permute-done | bytes 131104 | tf_op jit(solution)/shard_map/ppermute | solution.py:47
  25.7 0.6 collective-permute-start.4
  26.4 0.1 reshape.37
  26.6 4.3 %collective-permute-done.4 = bf16[128,512]{1,0:T(8,128)(2,1)S(1)} collective-permute-done((bf16[128,512]{1,0:T(8,128)(2,1)S(1)}, bf16[128,512]{1,0:T(8,128)(2,1)S(1)}, u32[]{:S(2)}, u32[]{:S(2)}) %collective-permute-start.4) | collective-permute-done | bytes 131104 | tf_op jit(solution)/shard_map/ppermute | solution.py:590
  30.9 0.1 collective-permute-start.7
  31.0 1.6 %collective-permute-start.6 = (bf16[2,128,512]{2,1,0:T(8,128)(2,1)S(1)}, bf16[2,128,512]{2,1,0:T(8,128)(2,1)S(1)}, u32[]{:S(2)}, u32[]{:S(2)}) collective-permute-start(bf16[2,128,512]{2,1,0:T(8,128)(2,1)S(1)} %pad_maximum_fusion.refs_4_.refs_0_), channel_id=1, source_target_pairs={{0,4},{1,5},{2,6},{3,7},{4,0},{5,1},{6,2},{7,3},{8,12},{9,13},{10,... | collective-permute-start | bytes 786440 | tf_op jit(solution)/shard_map/ppermute | solution.py:591
  32.7 2.4 %collective-permute-start.5 = (bf16[2,128,512]{2,1,0:T(8,128)(2,1)S(1)}, bf16[2,128,512]{2,1,0:T(8,128)(2,1)S(1)}, u32[]{:S(2)}, u32[]{:S(2)}) collective-permute-start(bf16[2,128,512]{2,1,0:T(8,128)(2,1)S(1)} %pad_maximum_fusion.refs_4_.refs_0_), channel_id=1, source_target_pairs={{0,2},{1,3},{2,0},{3,1},{4,6},{5,7},{6,4},{7,5},{8,10},{9,11},{10,... | collective-permute-start | bytes 786440 | tf_op jit(solution)/shard_map/ppermute | solution.py:591
  35.1 8.9 %convolve.1 = (bf16[4,32,512]{2,1,0:T(8,128)(2,1)S(1)}, f32[2048,128]{1,0:T(8,128)}, f32[33,128,128]{2,1,0:T(8,128)}) custom-call(bf16[2048,128]{1,0:T(8,128)(2,1)S(1)} %bitcast.8, f32[3,128]{1,0:T(4,128)S(1)} %pad_maximum_fusion.1.taps_ref, bf16[64,72,96]{2,1,0:T(8,128)(2,1)} %constant.90.clone.first_hbm, bf16[128,384]{1,0:T(8,128)(2,1)} %constant.91.clone.ahead_hbm, ...), custom_call_target="tpu_custom_call" | custom-call | flops 8000000000 | bytes 6000000 | tf_op jit(solution)/shard_map/convolve/pallas_call | solution.py:335
  44.1 1.4 %collective-permute-done.5.refs_5_.refs_1_ = bf16[2,128,512]{2,1,0:T(8,128)(2,1)S(1)} collective-permute-done((bf16[2,128,512]{2,1,0:T(8,128)(2,1)S(1)}, bf16[2,128,512]{2,1,0:T(8,128)(2,1)S(1)}, u32[]{:S(2)}, u32[]{:S(2)}) %collective-permute-start.5) | collective-permute-done | bytes 262176 | tf_op jit(solution)/shard_map/ppermute | solution.py:591
  45.5 1.7 %send.1 = bf16[16,64,512]{2,1,0:T(8,128)(2,1)S(1)} custom-call(s32[3]{0:T(128)S(1)} %pad_add_fusion.place_ref, bf16[4,32,512]{2,1,0:T(8,128)(2,1)S(1)} %get-tuple-element.25.gated_ref, bf16[512,256]{1,0:T(8,128)(2,1)S(1)} %copy-done.1, bf16[512,256]{1,0:T(8,128)(2,1)S(1)} %collective-permute-done.refs_1_, ...), custom_call_target="tpu_custom_call" | custom-call | flops 1000000000 | bytes 2000000 | tf_op jit(solution)/shard_map/send/pallas_call | solution.py:501
  47.3 24.5 %all_to_all.20.got_ref.share_ref = bf16[16,64,512]{2,1,0:T(8,128)(2,1)S(1)} all-to-all(bf16[16,64,512]{2,1,0:T(8,128)(2,1)S(1)} %send.1), channel_id=1, replica_groups=mesh['seq'=16,'chan'=8] {'seq'}, dimensions={0} | all-to-all | bytes 2097152 | tf_op jit(solution)/shard_map/all_to_all | solution.py:59
  71.8 2.7 %outputs.1 = bf16[8,128,512]{2,1,0:T(8,128)(2,1)} custom-call(s32[3]{0:T(128)S(1)} %pad_add_fusion.place_ref, bf16[16,64,512]{2,1,0:T(8,128)(2,1)S(1)} %all_to_all.20.got_ref.share_ref, bf16[512,256]{1,0:T(8,128)(2,1)S(1)} %copy-done.1, bf16[512,256]{1,0:T(8,128)(2,1)S(1)} %collective-permute-done.refs_1_, ...), custom_call_target="tpu_custom_call" | custom-call | flops 1000000000 | bytes 2000000 | tf_op jit(solution)/shard_map/outputs/pallas_call | solution.py:501
  74.4 5.0 %all-to-all-start.2 = ((bf16[8,128,512]{2,1,0:T(8,128)(2,1)}), bf16[8,128,512]{2,1,0:T(8,128)(2,1)S(1)}, u32[]{:S(2)}, u32[]{:S(2)}) async-start(bf16[8,128,512]{2,1,0:T(8,128)(2,1)} %outputs.1), calls=%async_computation.2 | async-start | bytes 2097152 | tf_op jit(solution)/shard_map/all_to_all | solution.py:59
  79.5 2.3 %weights.1 = (f32[512,256]{1,0:T(8,128)}, bf16[512,256]{1,0:T(8,128)(2,1)}, bf16[512,256]{1,0:T(8,128)(2,1)}, bf16[512,256]{1,0:T(8,128)(2,1)}) custom-call(s32[3]{0:T(128)S(1)} %pad_add_fusion.place_ref, bf16[16,64,512]{2,1,0:T(8,128)(2,1)S(1)} %all_to_all.20.got_ref.share_ref, bf16[2,128,512]{2,1,0:T(8,128)(2,1)S(1)} %pad_maximum_fusion.refs_4_.refs_0_, ...), custom_call_target="tpu_custom_call" | custom-call | flops 1000000000 | bytes 2000000 | tf_op jit(solution)/shard_map/weights/pallas_call | solution.py:501
  81.8 0.1 collective-permute-start.9
  81.9 0.1 collective-permute-start.10
  82.0 1.8 %collective-permute-start.11 = (bf16[512,256]{1,0:T(8,128)(2,1)}, bf16[512,256]{1,0:T(8,128)(2,1)S(1)}, u32[]{:S(2)}, u32[]{:S(2)}) collective-permute-start(bf16[512,256]{1,0:T(8,128)(2,1)} %get-tuple-element.32), channel_id=1, source_target_pairs={{0,24},{8,16},{16,8},{24,0},{32,56},{40,48},{48,40},{56,32},{64,88... | collective-permute-start | bytes 786440 | tf_op jit(solution)/shard_map/ppermute | solution.py:605
  83.8 10.4 %correlate.1 = bf16[16,128,128]{2,1,0:T(8,128)(2,1)} custom-call(bf16[16,64,512]{2,1,0:T(8,128)(2,1)S(1)} %all_to_all.20.got_ref.share_ref, f32[2048,128]{1,0:T(8,128)} %get-tuple-element.26.kept_hbm, f32[33,128,128]{2,1,0:T(8,128)} %get-tuple-element.27.spec_hbm, f32[3,128]{1,0:T(4,128)S(1)} %pad_maximum_fusion.1.taps_ref, ...), custom_call_target="tpu_custom_call" | custom-call | flops 8000000000 | bytes 6000000 | tf_op jit(solution)/shard_map/correlate/pallas_call | solution.py:361
  94.2 3.7 %all-to-all-start.3 = ((bf16[16,128,128]{2,1,0:T(8,128)(2,1)}), bf16[16,128,128]{2,1,0:T(8,128)(2,1)S(1)}, u32[]{:S(2)}, u32[]{:S(2)}) async-start(bf16[16,128,128]{2,1,0:T(8,128)(2,1)} %correlate.1), calls=%async_computation.3 | async-start | bytes 1048576 | tf_op jit(solution)/shard_map/all_to_all | solution.py:59
  97.9 0.1 reduce_sum.12
  98.1 5.7 %collective-permute-start.8 = (bf16[128,512]{1,0:T(8,128)(2,1)S(1)}, bf16[128,512]{1,0:T(8,128)(2,1)S(1)}, u32[]{:S(2)}, u32[]{:S(2)}) collective-permute-start(bf16[128,512]{1,0:T(8,128)(2,1)S(1)} %reduce_sum.12), channel_id=1, source_target_pairs={{0,0},{1,1},{2,32},{3,33},{4,64},{5,65},{6,96},{7,97},{8,8},{9,9},... | collective-permute-start | bytes 393224 | tf_op jit(solution)/shard_map/ppermute | solution.py:47
  103.9 0.9 convert_add_fusion
  104.8 5.9 %all-to-all-done.3.got_ref = bf16[16,128,128]{2,1,0:T(8,128)(2,1)S(1)} async-done(((bf16[16,128,128]{2,1,0:T(8,128)(2,1)}), bf16[16,128,128]{2,1,0:T(8,128)(2,1)S(1)}, u32[]{:S(2)}, u32[]{:S(2)}) %all-to-all-start.3) | async-done | bytes 524320 | tf_op jit(solution)/shard_map/all_to_all | solution.py:59
  110.7 1.3 %unpack.1 = (bf16[3,128,512]{2,1,0:T(8,128)(2,1)}, f32[128,512]{1,0:T(8,128)}) custom-call(bf16[16,128,128]{2,1,0:T(8,128)(2,1)S(1)} %all-to-all-done.3.got_ref), custom_call_target="tpu_custom_call" | custom-call | flops 1000000000 | bytes 2000000 | tf_op jit(solution)/shard_map/unpack/pallas_call | solution.py:501
  112.0 2.2 %collective-permute-done.8 = bf16[128,512]{1,0:T(8,128)(2,1)S(1)} collective-permute-done((bf16[128,512]{1,0:T(8,128)(2,1)S(1)}, bf16[128,512]{1,0:T(8,128)(2,1)S(1)}, u32[]{:S(2)}, u32[]{:S(2)}) %collective-permute-start.8) | collective-permute-done | bytes 131104 | tf_op jit(solution)/shard_map/ppermute | solution.py:47
  114.2 0.7 copy.14
  (24 shorter events, 0.3 us)
Async XLA Ops:
  0.6 16.4 %copy-start = (f32[3,3,512]{2,1,0:T(4,128)S(1)}, f32[3,3,512]{2,1,0:T(4,128)}, u32[]{:S(2)}) copy-start(f32[3,3,512]{2,1,0:T(4,128)} %param.12) | copy-start | bytes 55300
  0.6 25.9 %copy-start.3 = (f32[3,32]{1,0:T(4,128)S(1)}, f32[3,32]{1,0:T(4,128)}, u32[]{:S(2)}) copy-start(f32[3,32]{1,0:T(4,128)} %constant.88.clone.1) | copy-start | bytes 1156
  0.7 9.5 %copy-start.4 = (bf16[128,512]{1,0:T(8,128)(2,1)S(1)}, bf16[128,512]{1,0:T(8,128)(2,1)}, u32[]{:S(2)}) copy-start(bf16[128,512]{1,0:T(8,128)(2,1)} %param.15) | copy-start | bytes 393220
  0.7 14.4 %copy-start.1 = (bf16[512,256]{1,0:T(8,128)(2,1)S(1)}, bf16[512,256]{1,0:T(8,128)(2,1)}, u32[]{:S(2)}) copy-start(bf16[512,256]{1,0:T(8,128)(2,1)} %refs_0_.3) | copy-start | bytes 786436
  3.1 32.0 %all-to-all-start = ((bf16[16,128,128]{2,1,0:T(8,128)(2,1)}), bf16[16,128,128]{2,1,0:T(8,128)(2,1)S(1)}, u32[]{:S(2)}, u32[]{:S(2)}) async-start(bf16[16,128,128]{2,1,0:T(8,128)(2,1)} %pack.1), calls=%async_computation | async-start | bytes 1048576 | tf_op jit(solution)/shard_map/all_to_all | solution.py:59
  10.2 15.6 %collective-permute-start.3 = (bf16[128,512]{1,0:T(8,128)(2,1)S(1)}, bf16[128,512]{1,0:T(8,128)(2,1)S(1)}, u32[]{:S(2)}, u32[]{:S(2)}) collective-permute-start(bf16[128,512]{1,0:T(8,128)(2,1)S(1)} %copy-done.4), channel_id=1, source_target_pairs={{0,0},{1,1},{2,32},{3,33},{4,64},{5,65},{6,96},{7,97},{8,8},{9,9},... | collective-permute-start | bytes 393224 | tf_op jit(solution)/shard_map/ppermute | solution.py:47
  15.1 17.6 %collective-permute-start.2 = (bf16[512,256]{1,0:T(8,128)(2,1)S(1)}, bf16[512,256]{1,0:T(8,128)(2,1)S(1)}, u32[]{:S(2)}, u32[]{:S(2)}) collective-permute-start(bf16[512,256]{1,0:T(8,128)(2,1)S(1)} %copy-done.1), channel_id=1, source_target_pairs={{0,24},{8,16},{16,8},{24,0},{32,56},{40,48},{48,40},{56,32},{64,88... | collective-permute-start | bytes 786440 | tf_op jit(solution)/shard_map/ppermute | solution.py:592
  15.2 28.9 %collective-permute-start.1 = (bf16[512,256]{1,0:T(8,128)(2,1)S(1)}, bf16[512,256]{1,0:T(8,128)(2,1)S(1)}, u32[]{:S(2)}, u32[]{:S(2)}) collective-permute-start(bf16[512,256]{1,0:T(8,128)(2,1)S(1)} %copy-done.1), channel_id=1, source_target_pairs={{0,16},{8,24},{16,0},{24,8},{32,48},{40,56},{48,32},{56,40},{64,80... | collective-permute-start | bytes 786440 | tf_op jit(solution)/shard_map/ppermute | solution.py:592
  16.6 27.4 %collective-permute-start = (bf16[512,256]{1,0:T(8,128)(2,1)S(1)}, bf16[512,256]{1,0:T(8,128)(2,1)S(1)}, u32[]{:S(2)}, u32[]{:S(2)}) collective-permute-start(bf16[512,256]{1,0:T(8,128)(2,1)S(1)} %copy-done.1), channel_id=1, source_target_pairs={{0,8},{8,0},{16,24},{24,16},{32,40},{40,32},{48,56},{56,48},{64,72... | collective-permute-start | bytes 786440 | tf_op jit(solution)/shard_map/ppermute | solution.py:592
  25.7 5.1 %collective-permute-start.4 = (bf16[128,512]{1,0:T(8,128)(2,1)S(1)}, bf16[128,512]{1,0:T(8,128)(2,1)S(1)}, u32[]{:S(2)}, u32[]{:S(2)}) collective-permute-start(bf16[128,512]{1,0:T(8,128)(2,1)S(1)} %collective-permute-done.3), channel_id=1, source_target_pairs={{0,1},{1,0},{2,3},{3,2},{4,5},{5,4},{6,7},{7,6},{8,9},{9,8},{10,11... | collective-permute-start | bytes 393224 | tf_op jit(solution)/shard_map/ppermute | solution.py:590
  30.9 13.2 %collective-permute-start.7 = (bf16[2,128,512]{2,1,0:T(8,128)(2,1)S(1)}, bf16[2,128,512]{2,1,0:T(8,128)(2,1)S(1)}, u32[]{:S(2)}, u32[]{:S(2)}) collective-permute-start(bf16[2,128,512]{2,1,0:T(8,128)(2,1)S(1)} %pad_maximum_fusion.refs_4_.refs_0_), channel_id=1, source_target_pairs={{0,6},{1,7},{2,4},{3,5},{4,2},{5,3},{6,0},{7,1},{8,14},{9,15},{10,... | collective-permute-start | bytes 786440 | tf_op jit(solution)/shard_map/ppermute | solution.py:591
  31.0 13.1 %collective-permute-start.6 = (bf16[2,128,512]{2,1,0:T(8,128)(2,1)S(1)}, bf16[2,128,512]{2,1,0:T(8,128)(2,1)S(1)}, u32[]{:S(2)}, u32[]{:S(2)}) collective-permute-start(bf16[2,128,512]{2,1,0:T(8,128)(2,1)S(1)} %pad_maximum_fusion.refs_4_.refs_0_), channel_id=1, source_target_pairs={{0,4},{1,5},{2,6},{3,7},{4,0},{5,1},{6,2},{7,3},{8,12},{9,13},{10,... | collective-permute-start | bytes 786440 | tf_op jit(solution)/shard_map/ppermute | solution.py:591
  32.7 12.9 %collective-permute-start.5 = (bf16[2,128,512]{2,1,0:T(8,128)(2,1)S(1)}, bf16[2,128,512]{2,1,0:T(8,128)(2,1)S(1)}, u32[]{:S(2)}, u32[]{:S(2)}) collective-permute-start(bf16[2,128,512]{2,1,0:T(8,128)(2,1)S(1)} %pad_maximum_fusion.refs_4_.refs_0_), channel_id=1, source_target_pairs={{0,2},{1,3},{2,0},{3,1},{4,6},{5,7},{6,4},{7,5},{8,10},{9,11},{10,... | collective-permute-start | bytes 786440 | tf_op jit(solution)/shard_map/ppermute | solution.py:591
  74.4 19.8 %all-to-all-start.2 = ((bf16[8,128,512]{2,1,0:T(8,128)(2,1)}), bf16[8,128,512]{2,1,0:T(8,128)(2,1)S(1)}, u32[]{:S(2)}, u32[]{:S(2)}) async-start(bf16[8,128,512]{2,1,0:T(8,128)(2,1)} %outputs.1), calls=%async_computation.2 | async-start | bytes 2097152 | tf_op jit(solution)/shard_map/all_to_all | solution.py:59
  81.8 22.0 %collective-permute-start.9 = (bf16[512,256]{1,0:T(8,128)(2,1)}, bf16[512,256]{1,0:T(8,128)(2,1)S(1)}, u32[]{:S(2)}, u32[]{:S(2)}) collective-permute-start(bf16[512,256]{1,0:T(8,128)(2,1)} %get-tuple-element.30), channel_id=1, source_target_pairs={{0,8},{8,0},{16,24},{24,16},{32,40},{40,32},{48,56},{56,48},{64,72... | collective-permute-start | bytes 786440 | tf_op jit(solution)/shard_map/ppermute | solution.py:605
  81.9 21.9 %collective-permute-start.10 = (bf16[512,256]{1,0:T(8,128)(2,1)}, bf16[512,256]{1,0:T(8,128)(2,1)S(1)}, u32[]{:S(2)}, u32[]{:S(2)}) collective-permute-start(bf16[512,256]{1,0:T(8,128)(2,1)} %get-tuple-element.31), channel_id=1, source_target_pairs={{0,16},{8,24},{16,0},{24,8},{32,48},{40,56},{48,32},{56,40},{64,80... | collective-permute-start | bytes 786440 | tf_op jit(solution)/shard_map/ppermute | solution.py:605
  82.0 21.9 %collective-permute-start.11 = (bf16[512,256]{1,0:T(8,128)(2,1)}, bf16[512,256]{1,0:T(8,128)(2,1)S(1)}, u32[]{:S(2)}, u32[]{:S(2)}) collective-permute-start(bf16[512,256]{1,0:T(8,128)(2,1)} %get-tuple-element.32), channel_id=1, source_target_pairs={{0,24},{8,16},{16,8},{24,0},{32,56},{40,48},{48,40},{56,32},{64,88... | collective-permute-start | bytes 786440 | tf_op jit(solution)/shard_map/ppermute | solution.py:605
  94.2 9.7 %copy-start.2 = (f32[512,256]{1,0:T(8,128)S(1)}, f32[512,256]{1,0:T(8,128)}, u32[]{:S(2)}) copy-start(f32[512,256]{1,0:T(8,128)} %get-tuple-element.29) | copy-start | bytes 1572868
  94.2 16.5 %all-to-all-start.3 = ((bf16[16,128,128]{2,1,0:T(8,128)(2,1)}), bf16[16,128,128]{2,1,0:T(8,128)(2,1)S(1)}, u32[]{:S(2)}, u32[]{:S(2)}) async-start(bf16[16,128,128]{2,1,0:T(8,128)(2,1)} %correlate.1), calls=%async_computation.3 | async-start | bytes 1048576 | tf_op jit(solution)/shard_map/all_to_all | solution.py:59
  98.1 16.1 %collective-permute-start.8 = (bf16[128,512]{1,0:T(8,128)(2,1)S(1)}, bf16[128,512]{1,0:T(8,128)(2,1)S(1)}, u32[]{:S(2)}, u32[]{:S(2)}) collective-permute-start(bf16[128,512]{1,0:T(8,128)(2,1)S(1)} %reduce_sum.12), channel_id=1, source_target_pairs={{0,0},{1,1},{2,32},{3,33},{4,64},{5,65},{6,96},{7,97},{8,8},{9,9},... | collective-permute-start | bytes 393224 | tf_op jit(solution)/shard_map/ppermute | solution.py:47

commit v7 on v6

--- a/solution.py
+++ b/solution.py
@@ -24,7 +24,7 @@
 BACK = 80
 VMEM_LIMIT = 48 * 1024 * 1024
 WIDE = 16
-GROUP = 11
+GROUP = 33
 
 
 def device(seq_at, chan_at):
@@ -222,7 +222,7 @@
 def backward_kernel(
     share_ref, kept_hbm, spec_hbm, taps_ref, first_hbm, ahead_hbm, behind_hbm, last_hbm,
     out_ref,
-    grad_ref, mid_ref, back_ref, column_ref,
+    grad_ref, mid_ref, back_ref, column_ref, turned_ref,
     first_ref, ahead_ref, behind_ref, last_ref, kept_ref, spec_ref, sems,
 ):
     first_copy = started(first_hbm, first_ref, sems.at[0])
@@ -246,7 +246,9 @@
     def outer(n2):
         kept = kept_ref[column_rows(n2), :]
         query = jnp.where(lane < 3 * LANE, pltpu.roll(kept, 2 * LANE, 1), pltpu.roll(kept, 3 * LANE, 1))
-        data = grad_ref[pl.ds(n2, 32, stride=64), :] * query
+        grad = grad_ref[pl.ds(n2, 32, stride=64), :]
+        turned_ref[column_rows(n2), :] = grad
+        data = grad * query
         mid_ref[pl.ds(pl.multiple_of(n2 * MID, 8), MID), :] = matmul(first_ref[n2], pieces(data))
 
     first_copy.wait()
@@ -280,7 +282,7 @@
     def final(n2):
         found = matmul(last_ref[n2], pieces(back_ref[pl.ds(n2, BACK, stride=64), :]))
         kept = kept_ref[column_rows(n2), :]
-        grad = grad_ref[pl.ds(n2, 32, stride=64), :]
+        grad = turned_ref[column_rows(n2), :]
         up, down = pltpu.roll(kept, LANE, 1), pltpu.roll(kept, 3 * LANE, 1)
         mixed = jnp.where(
             lane < LANE,
@@ -308,6 +310,7 @@
         ).astype(BF16)
 
 
+SHORT = pl.CostEstimate(flops=2_000_000_000, transcendentals=0, bytes_accessed=100_000)
 LONG = pl.CostEstimate(flops=8_000_000_000, transcendentals=0, bytes_accessed=6_000_000)
 
 
@@ -350,7 +353,7 @@
             *HELD,
         ],
         compiler_params=pltpu.CompilerParams(vmem_limit_bytes=VMEM_LIMIT),
-        cost_estimate=LONG,
+        cost_estimate=SHORT,
         interpret=interpret,
         name="convolve",
     )(signals, taps, *(resident(x) for x in consts))
@@ -369,6 +372,7 @@
             pltpu.VMEM((64 * MID, 4 * LANE), F32),
             pltpu.VMEM((64 * BACK, 4 * LANE), F32),
             pltpu.VMEM((TOKENS + 8, 4 * LANE), F32),
+            pltpu.VMEM((TOKENS, 4 * LANE), F32),
             *HELD,
         ],
         compiler_params=pltpu.CompilerParams(vmem_limit_bytes=VMEM_LIMIT),
@@ -468,36 +472,51 @@
 
 
 def output_kernel(place_ref, got_ref, *refs):
-    out_ref, weights, sems = refs[NEAR:]
+    out_hbm, weights, out_ref, sems = refs[NEAR:]
     copies = fetch_weights(place_ref, refs[:NEAR], weights, sems)
-    turned = got_ref[...].reshape(COLS, FAR * ROWS).T
+    gated = got_ref[...].reshape(COLS, FAR * ROWS)
     for copy in copies:
         copy.wait()
-    for side in range(2):
-        part = contract(turned, weights[:, side * COLS : (side + 1) * COLS], 1, 0).astype(BF16)
-        for a in range(FAR):
-            out_ref[2 * a + side] = part[a * ROWS : (a + 1) * ROWS]
+    departures = []
+    for a in range(FAR):
+        part = contract(gated[:, a * ROWS : (a + 1) * ROWS], weights[...], 0, 0).astype(BF16)
+        out_ref[2 * a] = part[:, :COLS]
+        out_ref[2 * a + 1] = part[:, COLS:]
+        span = slice(2 * a, 2 * a + 2)
+        departures.append(started(out_ref.at[span], out_hbm.at[span], sems.at[NEAR + a]))
+    for copy in departures:
+        copy.wait()
 
 
 def weight_kernel(place_ref, got_ref, *refs):
-    grad_refs, (cots, sems) = refs[FAR : FAR + NEAR], refs[FAR + NEAR :]
+    grad_hbms = refs[FAR : FAR + NEAR]
+    cots, own_ref, other_ref, sems = refs[FAR + NEAR :]
     copies = fetch_cots(place_ref, refs[:FAR], cots, sems)
     gated = got_ref[...].reshape(COLS, FAR * ROWS)
     for copy in copies:
         copy.wait()
-    for step in range(NEAR):
+    departures = []
+    for step in reversed(range(NEAR)):
         low = pl.multiple_of((place_ref[0] ^ step) * 256, 256)
         grad = contract(gated, cots[:, pl.ds(low, 256)], 1, 0)
-        grad_refs[step][...] = grad.astype(grad_refs[step].dtype)
-
-
-def call(kernel, name, out_shape, interpret, *inputs, specs=None, scratch=()):
+        if step:
+            other_ref[step - 1] = grad.astype(BF16)
+            source = other_ref.at[step - 1]
+        else:
+            own_ref[...] = grad
+            source = own_ref
+        departures.append(started(source, grad_hbms[step], sems.at[step]))
+    for copy in departures:
+        copy.wait()
+
+
+def call(kernel, name, out_shape, interpret, *inputs, specs=None, scratch=(), far_out=False):
     many = isinstance(out_shape, tuple)
     outs = out_shape if many else (out_shape,)
     in_specs = [whole(x.shape) for x in inputs]
     for at, spec in (specs or {}).items():
         in_specs[at] = spec
-    out_specs = tuple(whole(x.shape) for x in outs)
+    out_specs = tuple(FAR_OFF if far_out else whole(x.shape) for x in outs)
     return pl.pallas_call(
         kernel,
         out_shape=out_shape,
@@ -567,7 +586,7 @@
     return call(
         output_kernel, "outputs", pltpu.HBM((CHAN, ROWS, COLS), BF16), interpret,
         place, got, *weights, specs={0: SCALAR, 1: GATED, **far_off(2, 2 + NEAR)},
-        scratch=(GATHERED[0], GATHERED[2]),
+        scratch=(GATHERED[0], pltpu.VMEM((CHAN, ROWS, COLS), BF16), GATHERED[2]), far_out=True,
     )
 
 
@@ -575,7 +594,13 @@
     shapes = tuple(pltpu.HBM((COLS, width), BF16 if step else F32) for step in range(NEAR))
     return call(
         weight_kernel, "weights", shapes, interpret, place, got, *cots,
-        specs={0: SCALAR, 1: GATED, **far_off(2, 2 + FAR)}, scratch=GATHERED[1:],
+        specs={0: SCALAR, 1: GATED, **far_off(2, 2 + FAR)}, far_out=True,
+        scratch=(
+            GATHERED[1],
+            pltpu.VMEM((COLS, width), F32),
+            pltpu.VMEM((NEAR - 1, COLS, width), BF16),
+            GATHERED[2],
+        ),
     )
 
 

time: 115 us -> 112 us (0.974)
  waiting for transfers between devices: 22.5 us -> 18.4 us
  starting transfers between devices: 35.1 us -> 36.7 us
  Pallas kernels: 29.8 us -> 28.3 us
    ppermute x2, waiting for transfers between devices: 10.8 us -> 2.56 us  [swapped(): return lax.ppermute(array, ('seq', 'chan'), swap_pairs())]
    ppermute x1, waiting for transfers between devices: 4.32 us -> 7.49 us  [shards(): pair = jnp.stack([moved, lax.ppermute(moved, 'chan', chan_pairs(1))])]
    ppermute x3, waiting for transfers between devices: 1.44 us -> 2.79 us  [shards(): lax.ppermute(pair, 'chan', chan_pairs(2 * far))]
  transfers between devices with their start and end apart: 15 -> 15, of which waited for: 5 -> 5; matrix products, arithmetic and copies ran while one was open for 1% -> 1% of each run, Pallas kernels for 20% -> 22%
where the time goes in v7:
time: 112 us; the launch traced here: 111 us
  starting transfers between devices  36.7 us (33%)
  Pallas kernels  28.3 us (25%)
  blocking collectives  25.1 us (22%)
  waiting for transfers between devices  18.4 us (16%)
  other arithmetic  1.26 us (1%)
    all_to_all x1, blocking collectives, exchange(): return lax.all_to_all(array, axis, 0, 0, tiled=True)  25.1 us
    all_to_all x3, starting transfers between devices, exchange(): return lax.all_to_all(array, axis, 0, 0, tiled=True)  16.1 us
    ppermute x2, starting transfers between devices, swapped(): return lax.ppermute(array, ('seq', 'chan'), swap_pairs())  10.9 us
    pallas_call x1, Pallas kernels, correlate(): pl.pallas_call(backward_kernel, out_shape=jax.ShapeDtypeStruct((SEQ, ROWS...  9.61 us
    pallas_call x1, Pallas kernels, convolve(): pl.pallas_call(forward_kernel, out_shape=(jax.ShapeDtypeStruct((NEAR, LAN...  8.59 us
    pallas_call x4, Pallas kernels, call(): pl.pallas_call(kernel, out_shape=out_shape, grid=(1,), in_specs=in_specs,...  7.75 us
    ppermute x1, waiting for transfers between devices, shards(): pair = jnp.stack([moved, lax.ppermute(moved, 'chan', chan_pairs(1))])  7.49 us
    all_to_all x3, waiting for transfers between devices, exchange(): return lax.all_to_all(array, axis, 0, 0, tiled=True)  5.54 us
  transfers between devices with their start and end apart: 15, of which 5 were waited for; matrix products, arithmetic and copies ran while one was open for 1% of the time, Pallas kernels for 22%

profile of v7, /device:TPU:32, one launch (start us, length us, event | category | flops | bytes accessed | tf_op | source)
XLA Modules:
  0.0 111.4 jit_solution(2692097304903078206)
XLA Ops:
  0.7 4.8 %collective-permute-start.3 = (bf16[128,512]{1,0:T(8,128)(2,1)}, bf16[128,512]{1,0:T(8,128)(2,1)S(1)}, u32[]{:S(2)}, u32[]{:S(2)}) collective-permute-start(bf16[128,512]{1,0:T(8,128)(2,1)} %param.15), channel_id=1, source_target_pairs={{0,0},{1,1},{2,32},{3,33},{4,64},{5,65},{6,96},{7,97},{8,8},{9,9},... | collective-permute-start | bytes 393224 | tf_op jit(solution)/shard_map/ppermute | solution.py:47
  5.5 2.4 %pack.1 = bf16[16,128,128]{2,1,0:T(8,128)(2,1)} custom-call(bf16[3,128,512]{2,1,0:T(8,128)(2,1)} %bitcast.9, f32[128,512]{1,0:T(8,128)} %filter_hbm.1), custom_call_target="tpu_custom_call" | custom-call | tf_op jit(solution)/shard_map/pack/pallas_call | solution.py:538
  7.8 7.2 %all-to-all-start = ((bf16[16,128,128]{2,1,0:T(8,128)(2,1)}), bf16[16,128,128]{2,1,0:T(8,128)(2,1)S(1)}, u32[]{:S(2)}, u32[]{:S(2)}) async-start(bf16[16,128,128]{2,1,0:T(8,128)(2,1)} %pack.1), calls=%async_computation | async-start | bytes 1048576 | tf_op jit(solution)/shard_map/all_to_all | solution.py:59
  15.1 1.8 %collective-permute-start.2 = (bf16[512,256]{1,0:T(8,128)(2,1)S(1)}, bf16[512,256]{1,0:T(8,128)(2,1)S(1)}, u32[]{:S(2)}, u32[]{:S(2)}) collective-permute-start(bf16[512,256]{1,0:T(8,128)(2,1)S(1)} %copy-done.1), channel_id=1, source_target_pairs={{0,24},{8,16},{16,8},{24,0},{32,56},{40,48},{48,40},{56,32},{64,88... | collective-permute-start | bytes 786440 | tf_op jit(solution)/shard_map/ppermute | solution.py:617
  16.8 0.4 collective-permute-start.1
  17.2 1.5 %collective-permute-start.4 = (bf16[128,512]{1,0:T(8,128)(2,1)S(1)}, bf16[128,512]{1,0:T(8,128)(2,1)S(1)}, u32[]{:S(2)}, u32[]{:S(2)}) collective-permute-start(bf16[128,512]{1,0:T(8,128)(2,1)S(1)} %collective-permute-done.3), channel_id=1, source_target_pairs={{0,1},{1,0},{2,3},{3,2},{4,5},{5,4},{6,7},{7,6},{8,9},{9,8},{10,11... | collective-permute-start | bytes 393224 | tf_op jit(solution)/shard_map/ppermute | solution.py:615
  18.8 0.1 reshape.37
  18.9 7.5 %collective-permute-done.4 = bf16[128,512]{1,0:T(8,128)(2,1)S(1)} collective-permute-done((bf16[128,512]{1,0:T(8,128)(2,1)S(1)}, bf16[128,512]{1,0:T(8,128)(2,1)S(1)}, u32[]{:S(2)}, u32[]{:S(2)}) %collective-permute-start.4) | collective-permute-done | bytes 131104 | tf_op jit(solution)/shard_map/ppermute | solution.py:615
  26.5 0.3 collective-permute-start.7
  26.8 3.5 %collective-permute-start.6 = (bf16[2,128,512]{2,1,0:T(8,128)(2,1)S(1)}, bf16[2,128,512]{2,1,0:T(8,128)(2,1)S(1)}, u32[]{:S(2)}, u32[]{:S(2)}) collective-permute-start(bf16[2,128,512]{2,1,0:T(8,128)(2,1)S(1)} %pad_maximum_fusion.refs_4_.refs_0_), channel_id=1, source_target_pairs={{0,4},{1,5},{2,6},{3,7},{4,0},{5,1},{6,2},{7,3},{8,12},{9,13},{10,... | collective-permute-start | bytes 786440 | tf_op jit(solution)/shard_map/ppermute | solution.py:616
  30.3 0.4 collective-permute-start.5
  30.6 0.1 pad_add_fusion.place_ref
  30.7 8.6 %convolve.1 = (bf16[4,32,512]{2,1,0:T(8,128)(2,1)S(1)}, f32[2048,128]{1,0:T(8,128)}, f32[33,128,128]{2,1,0:T(8,128)}) custom-call(bf16[2048,128]{1,0:T(8,128)(2,1)S(1)} %bitcast.8, f32[3,128]{1,0:T(4,128)S(1)} %pad_maximum_fusion.1.taps_ref, bf16[64,72,96]{2,1,0:T(8,128)(2,1)} %constant.90.clone.first_hbm, bf16[128,384]{1,0:T(8,128)(2,1)} %constant.91.clone.ahead_hbm, ...), custom_call_target="tpu_custom_call" | custom-call | flops 2000000000 | bytes 100000 | tf_op jit(solution)/shard_map/convolve/pallas_call | solution.py:338
  39.3 1.0 collective-permute-done.7.refs_7_.refs_3_
  40.3 1.8 %collective-permute-done.5.refs_5_.refs_1_ = bf16[2,128,512]{2,1,0:T(8,128)(2,1)S(1)} collective-permute-done((bf16[2,128,512]{2,1,0:T(8,128)(2,1)S(1)}, bf16[2,128,512]{2,1,0:T(8,128)(2,1)S(1)}, u32[]{:S(2)}, u32[]{:S(2)}) %collective-permute-start.5) | collective-permute-done | bytes 262176 | tf_op jit(solution)/shard_map/ppermute | solution.py:616
  42.1 1.7 %send.1 = bf16[16,64,512]{2,1,0:T(8,128)(2,1)S(1)} custom-call(s32[3]{0:T(128)S(1)} %pad_add_fusion.place_ref, bf16[4,32,512]{2,1,0:T(8,128)(2,1)S(1)} %get-tuple-element.25.gated_ref, bf16[512,256]{1,0:T(8,128)(2,1)S(1)} %copy-done.1, bf16[512,256]{1,0:T(8,128)(2,1)S(1)} %collective-permute-done.refs_1_, ...), custom_call_target="tpu_custom_call" | custom-call | flops 1000000000 | bytes 2000000 | tf_op jit(solution)/shard_map/send/pallas_call | solution.py:520
  43.9 25.1 %all_to_all.20.got_ref.share_ref = bf16[16,64,512]{2,1,0:T(8,128)(2,1)S(1)} all-to-all(bf16[16,64,512]{2,1,0:T(8,128)(2,1)S(1)} %send.1), channel_id=1, replica_groups=mesh['seq'=16,'chan'=8] {'seq'}, dimensions={0} | all-to-all | bytes 2097152 | tf_op jit(solution)/shard_map/all_to_all | solution.py:59
  68.9 2.3 %outputs.1 = bf16[8,128,512]{2,1,0:T(8,128)(2,1)} custom-call(s32[3]{0:T(128)S(1)} %pad_add_fusion.place_ref, bf16[16,64,512]{2,1,0:T(8,128)(2,1)S(1)} %all_to_all.20.got_ref.share_ref, bf16[512,256]{1,0:T(8,128)(2,1)S(1)} %copy-done.1, bf16[512,256]{1,0:T(8,128)(2,1)S(1)} %collective-permute-done.refs_1_, ...), custom_call_target="tpu_custom_call" | custom-call | flops 1000000000 | bytes 2000000 | tf_op jit(solution)/shard_map/outputs/pallas_call | solution.py:520
  71.2 5.1 %all-to-all-start.2 = ((bf16[8,128,512]{2,1,0:T(8,128)(2,1)}), bf16[8,128,512]{2,1,0:T(8,128)(2,1)S(1)}, u32[]{:S(2)}, u32[]{:S(2)}) async-start(bf16[8,128,512]{2,1,0:T(8,128)(2,1)} %outputs.1), calls=%async_computation.2 | async-start | bytes 2097152 | tf_op jit(solution)/shard_map/all_to_all | solution.py:59
  76.3 2.4 %weights.1 = (f32[512,256]{1,0:T(8,128)}, bf16[512,256]{1,0:T(8,128)(2,1)}, bf16[512,256]{1,0:T(8,128)(2,1)}, bf16[512,256]{1,0:T(8,128)(2,1)}) custom-call(s32[3]{0:T(128)S(1)} %pad_add_fusion.place_ref, bf16[16,64,512]{2,1,0:T(8,128)(2,1)S(1)} %all_to_all.20.got_ref.share_ref, bf16[2,128,512]{2,1,0:T(8,128)(2,1)S(1)} %pad_maximum_fusion.refs_4_.refs_0_, ...), custom_call_target="tpu_custom_call" | custom-call | flops 1000000000 | bytes 2000000 | tf_op jit(solution)/shard_map/weights/pallas_call | solution.py:520
  78.8 0.1 collective-permute-start.9
  78.9 0.1 collective-permute-start.10
  79.0 1.8 %collective-permute-start.11 = (bf16[512,256]{1,0:T(8,128)(2,1)}, bf16[512,256]{1,0:T(8,128)(2,1)S(1)}, u32[]{:S(2)}, u32[]{:S(2)}) collective-permute-start(bf16[512,256]{1,0:T(8,128)(2,1)} %get-tuple-element.32), channel_id=1, source_target_pairs={{0,24},{8,16},{16,8},{24,0},{32,56},{40,48},{48,40},{56,32},{64,88... | collective-permute-start | bytes 786440 | tf_op jit(solution)/shard_map/ppermute | solution.py:630
  80.8 9.6 %correlate.1 = bf16[16,128,128]{2,1,0:T(8,128)(2,1)} custom-call(bf16[16,64,512]{2,1,0:T(8,128)(2,1)S(1)} %all_to_all.20.got_ref.share_ref, f32[2048,128]{1,0:T(8,128)} %get-tuple-element.26.kept_hbm, f32[33,128,128]{2,1,0:T(8,128)} %get-tuple-element.27.spec_hbm, f32[3,128]{1,0:T(4,128)S(1)} %pad_maximum_fusion.1.taps_ref, ...), custom_call_target="tpu_custom_call" | custom-call | flops 8000000000 | bytes 6000000 | tf_op jit(solution)/shard_map/correlate/pallas_call | solution.py:364
  90.4 3.7 %all-to-all-start.3 = ((bf16[16,128,128]{2,1,0:T(8,128)(2,1)}), bf16[16,128,128]{2,1,0:T(8,128)(2,1)S(1)}, u32[]{:S(2)}, u32[]{:S(2)}) async-start(bf16[16,128,128]{2,1,0:T(8,128)(2,1)} %correlate.1), calls=%async_computation.3 | async-start | bytes 1048576 | tf_op jit(solution)/shard_map/all_to_all | solution.py:59
  94.1 0.1 reduce_sum.12
  94.3 6.1 %collective-permute-start.8 = (bf16[128,512]{1,0:T(8,128)(2,1)S(1)}, bf16[128,512]{1,0:T(8,128)(2,1)S(1)}, u32[]{:S(2)}, u32[]{:S(2)}) collective-permute-start(bf16[128,512]{1,0:T(8,128)(2,1)S(1)} %reduce_sum.12), channel_id=1, source_target_pairs={{0,0},{1,1},{2,32},{3,33},{4,64},{5,65},{6,96},{7,97},{8,8},{9,9},... | collective-permute-start | bytes 393224 | tf_op jit(solution)/shard_map/ppermute | solution.py:47
  100.5 0.9 convert_add_fusion
  101.4 5.5 %all-to-all-done.3.got_ref = bf16[16,128,128]{2,1,0:T(8,128)(2,1)S(1)} async-done(((bf16[16,128,128]{2,1,0:T(8,128)(2,1)}), bf16[16,128,128]{2,1,0:T(8,128)(2,1)S(1)}, u32[]{:S(2)}, u32[]{:S(2)}) %all-to-all-start.3) | async-done | bytes 524320 | tf_op jit(solution)/shard_map/all_to_all | solution.py:59
  106.9 1.3 %unpack.1 = (bf16[3,128,512]{2,1,0:T(8,128)(2,1)}, f32[128,512]{1,0:T(8,128)}) custom-call(bf16[16,128,128]{2,1,0:T(8,128)(2,1)S(1)} %all-to-all-done.3.got_ref), custom_call_target="tpu_custom_call" | custom-call | flops 1000000000 | bytes 2000000 | tf_op jit(solution)/shard_map/unpack/pallas_call | solution.py:520
  108.2 2.6 %collective-permute-done.8 = bf16[128,512]{1,0:T(8,128)(2,1)S(1)} collective-permute-done((bf16[128,512]{1,0:T(8,128)(2,1)S(1)}, bf16[128,512]{1,0:T(8,128)(2,1)S(1)}, u32[]{:S(2)}, u32[]{:S(2)}) %collective-permute-start.8) | collective-permute-done | bytes 131104 | tf_op jit(solution)/shard_map/ppermute | solution.py:47
  110.8 0.7 copy.14
  (22 shorter events, 0.2 us)
Async XLA Ops:
  0.6 18.1 %copy-start = (f32[3,3,512]{2,1,0:T(4,128)S(1)}, f32[3,3,512]{2,1,0:T(4,128)}, u32[]{:S(2)}) copy-start(f32[3,3,512]{2,1,0:T(4,128)} %param.12) | copy-start | bytes 55300
  0.6 18.2 %copy-start.3 = (f32[3,32]{1,0:T(4,128)S(1)}, f32[3,32]{1,0:T(4,128)}, u32[]{:S(2)}) copy-start(f32[3,32]{1,0:T(4,128)} %constant.88.clone.1) | copy-start | bytes 1156
  0.7 14.4 %copy-start.1 = (bf16[512,256]{1,0:T(8,128)(2,1)S(1)}, bf16[512,256]{1,0:T(8,128)(2,1)}, u32[]{:S(2)}) copy-start(bf16[512,256]{1,0:T(8,128)(2,1)} %refs_0_.3) | copy-start | bytes 786436
  0.7 16.5 %collective-permute-start.3 = (bf16[128,512]{1,0:T(8,128)(2,1)}, bf16[128,512]{1,0:T(8,128)(2,1)S(1)}, u32[]{:S(2)}, u32[]{:S(2)}) collective-permute-start(bf16[128,512]{1,0:T(8,128)(2,1)} %param.15), channel_id=1, source_target_pairs={{0,0},{1,1},{2,32},{3,33},{4,64},{5,65},{6,96},{7,97},{8,8},{9,9},... | collective-permute-start | bytes 393224 | tf_op jit(solution)/shard_map/ppermute | solution.py:47
  7.8 22.9 %all-to-all-start = ((bf16[16,128,128]{2,1,0:T(8,128)(2,1)}), bf16[16,128,128]{2,1,0:T(8,128)(2,1)S(1)}, u32[]{:S(2)}, u32[]{:S(2)}) async-start(bf16[16,128,128]{2,1,0:T(8,128)(2,1)} %pack.1), calls=%async_computation | async-start | bytes 1048576 | tf_op jit(solution)/shard_map/all_to_all | solution.py:59
  15.1 15.2 %collective-permute-start.2 = (bf16[512,256]{1,0:T(8,128)(2,1)S(1)}, bf16[512,256]{1,0:T(8,128)(2,1)S(1)}, u32[]{:S(2)}, u32[]{:S(2)}) collective-permute-start(bf16[512,256]{1,0:T(8,128)(2,1)S(1)} %copy-done.1), channel_id=1, source_target_pairs={{0,24},{8,16},{16,8},{24,0},{32,56},{40,48},{48,40},{56,32},{64,88... | collective-permute-start | bytes 786440 | tf_op jit(solution)/shard_map/ppermute | solution.py:617
  16.8 22.5 %collective-permute-start.1 = (bf16[512,256]{1,0:T(8,128)(2,1)S(1)}, bf16[512,256]{1,0:T(8,128)(2,1)S(1)}, u32[]{:S(2)}, u32[]{:S(2)}) collective-permute-start(bf16[512,256]{1,0:T(8,128)(2,1)S(1)} %copy-done.1), channel_id=1, source_target_pairs={{0,16},{8,24},{16,0},{24,8},{32,48},{40,56},{48,32},{56,40},{64,80... | collective-permute-start | bytes 786440 | tf_op jit(solution)/shard_map/ppermute | solution.py:617
  17.2 22.1 %collective-permute-start = (bf16[512,256]{1,0:T(8,128)(2,1)S(1)}, bf16[512,256]{1,0:T(8,128)(2,1)S(1)}, u32[]{:S(2)}, u32[]{:S(2)}) collective-permute-start(bf16[512,256]{1,0:T(8,128)(2,1)S(1)} %copy-done.1), channel_id=1, source_target_pairs={{0,8},{8,0},{16,24},{24,16},{32,40},{40,32},{48,56},{56,48},{64,72... | collective-permute-start | bytes 786440 | tf_op jit(solution)/shard_map/ppermute | solution.py:617
  17.2 9.2 %collective-permute-start.4 = (bf16[128,512]{1,0:T(8,128)(2,1)S(1)}, bf16[128,512]{1,0:T(8,128)(2,1)S(1)}, u32[]{:S(2)}, u32[]{:S(2)}) collective-permute-start(bf16[128,512]{1,0:T(8,128)(2,1)S(1)} %collective-permute-done.3), channel_id=1, source_target_pairs={{0,1},{1,0},{2,3},{3,2},{4,5},{5,4},{6,7},{7,6},{8,9},{9,8},{10,11... | collective-permute-start | bytes 393224 | tf_op jit(solution)/shard_map/ppermute | solution.py:615
  26.5 13.8 %collective-permute-start.7 = (bf16[2,128,512]{2,1,0:T(8,128)(2,1)S(1)}, bf16[2,128,512]{2,1,0:T(8,128)(2,1)S(1)}, u32[]{:S(2)}, u32[]{:S(2)}) collective-permute-start(bf16[2,128,512]{2,1,0:T(8,128)(2,1)S(1)} %pad_maximum_fusion.refs_4_.refs_0_), channel_id=1, source_target_pairs={{0,6},{1,7},{2,4},{3,5},{4,2},{5,3},{6,0},{7,1},{8,14},{9,15},{10,... | collective-permute-start | bytes 786440 | tf_op jit(solution)/shard_map/ppermute | solution.py:616
  26.8 13.5 %collective-permute-start.6 = (bf16[2,128,512]{2,1,0:T(8,128)(2,1)S(1)}, bf16[2,128,512]{2,1,0:T(8,128)(2,1)S(1)}, u32[]{:S(2)}, u32[]{:S(2)}) collective-permute-start(bf16[2,128,512]{2,1,0:T(8,128)(2,1)S(1)} %pad_maximum_fusion.refs_4_.refs_0_), channel_id=1, source_target_pairs={{0,4},{1,5},{2,6},{3,7},{4,0},{5,1},{6,2},{7,3},{8,12},{9,13},{10,... | collective-permute-start | bytes 786440 | tf_op jit(solution)/shard_map/ppermute | solution.py:616
  30.3 11.9 %collective-permute-start.5 = (bf16[2,128,512]{2,1,0:T(8,128)(2,1)S(1)}, bf16[2,128,512]{2,1,0:T(8,128)(2,1)S(1)}, u32[]{:S(2)}, u32[]{:S(2)}) collective-permute-start(bf16[2,128,512]{2,1,0:T(8,128)(2,1)S(1)} %pad_maximum_fusion.refs_4_.refs_0_), channel_id=1, source_target_pairs={{0,2},{1,3},{2,0},{3,1},{4,6},{5,7},{6,4},{7,5},{8,10},{9,11},{10,... | collective-permute-start | bytes 786440 | tf_op jit(solution)/shard_map/ppermute | solution.py:616
  71.2 19.2 %all-to-all-start.2 = ((bf16[8,128,512]{2,1,0:T(8,128)(2,1)}), bf16[8,128,512]{2,1,0:T(8,128)(2,1)S(1)}, u32[]{:S(2)}, u32[]{:S(2)}) async-start(bf16[8,128,512]{2,1,0:T(8,128)(2,1)} %outputs.1), calls=%async_computation.2 | async-start | bytes 2097152 | tf_op jit(solution)/shard_map/all_to_all | solution.py:59
  78.8 21.6 %collective-permute-start.9 = (bf16[512,256]{1,0:T(8,128)(2,1)}, bf16[512,256]{1,0:T(8,128)(2,1)S(1)}, u32[]{:S(2)}, u32[]{:S(2)}) collective-permute-start(bf16[512,256]{1,0:T(8,128)(2,1)} %get-tuple-element.30), channel_id=1, source_target_pairs={{0,8},{8,0},{16,24},{24,16},{32,40},{40,32},{48,56},{56,48},{64,72... | collective-permute-start | bytes 786440 | tf_op jit(solution)/shard_map/ppermute | solution.py:630
  78.9 21.5 %collective-permute-start.10 = (bf16[512,256]{1,0:T(8,128)(2,1)}, bf16[512,256]{1,0:T(8,128)(2,1)S(1)}, u32[]{:S(2)}, u32[]{:S(2)}) collective-permute-start(bf16[512,256]{1,0:T(8,128)(2,1)} %get-tuple-element.31), channel_id=1, source_target_pairs={{0,16},{8,24},{16,0},{24,8},{32,48},{40,56},{48,32},{56,40},{64,80... | collective-permute-start | bytes 786440 | tf_op jit(solution)/shard_map/ppermute | solution.py:630
  79.0 21.5 %collective-permute-start.11 = (bf16[512,256]{1,0:T(8,128)(2,1)}, bf16[512,256]{1,0:T(8,128)(2,1)S(1)}, u32[]{:S(2)}, u32[]{:S(2)}) collective-permute-start(bf16[512,256]{1,0:T(8,128)(2,1)} %get-tuple-element.32), channel_id=1, source_target_pairs={{0,24},{8,16},{16,8},{24,0},{32,56},{40,48},{48,40},{56,32},{64,88... | collective-permute-start | bytes 786440 | tf_op jit(solution)/shard_map/ppermute | solution.py:630
  90.4 10.1 %copy-start.2 = (f32[512,256]{1,0:T(8,128)S(1)}, f32[512,256]{1,0:T(8,128)}, u32[]{:S(2)}) copy-start(f32[512,256]{1,0:T(8,128)} %get-tuple-element.29) | copy-start | bytes 1572868
  90.4 16.5 %all-to-all-start.3 = ((bf16[16,128,128]{2,1,0:T(8,128)(2,1)}), bf16[16,128,128]{2,1,0:T(8,128)(2,1)S(1)}, u32[]{:S(2)}, u32[]{:S(2)}) async-start(bf16[16,128,128]{2,1,0:T(8,128)(2,1)} %correlate.1), calls=%async_computation.3 | async-start | bytes 1048576 | tf_op jit(solution)/shard_map/all_to_all | solution.py:59
  94.3 16.5 %collective-permute-start.8 = (bf16[128,512]{1,0:T(8,128)(2,1)S(1)}, bf16[128,512]{1,0:T(8,128)(2,1)S(1)}, u32[]{:S(2)}, u32[]{:S(2)}) collective-permute-start(bf16[128,512]{1,0:T(8,128)(2,1)S(1)} %reduce_sum.12), channel_id=1, source_target_pairs={{0,0},{1,1},{2,32},{3,33},{4,64},{5,65},{6,96},{7,97},{8,8},{9,9},... | collective-permute-start | bytes 393224 | tf_op jit(solution)/shard_map/ppermute | solution.py:47

commit v8 on v7

--- a/solution.py
+++ b/solution.py
@@ -445,9 +445,9 @@
 def fetch_cots(place_ref, refs, cots, sems):
     copies = []
     for far in range(FAR):
-        row = pl.multiple_of((place_ref[1] ^ far) * ROWS, ROWS)
+        low = pl.multiple_of((place_ref[2] ^ (far % 2)) * COLS, COLS)
         for side in range(2):
-            low = pl.multiple_of((place_ref[2] ^ side) * COLS, COLS)
+            row = pl.multiple_of((place_ref[1] ^ (far // 2 + 2 * side)) * ROWS, ROWS)
             copies.append(
                 started(
                     refs[far].at[side],
@@ -612,8 +612,8 @@
 
     moved = swapped(d_out)
     signals = exchange(pack(projected.transpose(1, 0, 2), long_filter), "seq")
-    pair = jnp.stack([moved, lax.ppermute(moved, "chan", chan_pairs(1))])
-    cots = [pair] + [lax.ppermute(pair, "chan", chan_pairs(2 * far)) for far in range(1, FAR)]
+    pair = jnp.stack([moved, lax.ppermute(moved, "chan", chan_pairs(4))])
+    cots = [pair] + [lax.ppermute(pair, "chan", chan_pairs(far)) for far in range(1, FAR)]
     weights = [w_out] + [lax.ppermute(w_out, "seq", near_pairs(step)) for step in range(1, NEAR)]
 
     own = lax.dynamic_slice_in_dim(short_filter, seq_at * LANE, LANE, axis=2).reshape(3, 3 * LANE)

time: 112 us -> 109 us (0.973)
  waiting for transfers between devices: 18.4 us -> 16.1 us
    ppermute x4, waiting for transfers between devices: 10.3 us -> 6.72 us  [the longest x1 6.42 us: shards(): pair = jnp.stack([moved, lax.ppermute(moved, 'chan', chan_pairs(4))])]
    ppermute x3, waiting for transfers between devices: 0.01 us -> 1.25 us  [shards(): lax.ppermute(w_out, 'seq', near_pairs(step))]
  transfers between devices with their start and end apart: 15 -> 15, of which waited for: 5 -> 6; matrix products, arithmetic and copies ran while one was open for 1% -> 1% of each run, Pallas kernels for 22% -> 22%
where the time goes in v8:
time: 109 us
  starting transfers between devices  36.3 us (33%)
  Pallas kernels  28.3 us (26%)
  blocking collectives  25 us (23%)
  waiting for transfers between devices  16.1 us (15%)
  other arithmetic  1.26 us (1%)
    all_to_all x1, blocking collectives, exchange(): return lax.all_to_all(array, axis, 0, 0, tiled=True)  25 us
    all_to_all x3, starting transfers between devices, exchange(): return lax.all_to_all(array, axis, 0, 0, tiled=True)  16.1 us
    ppermute x2, starting transfers between devices, swapped(): return lax.ppermute(array, ('seq', 'chan'), swap_pairs())  10.9 us
    pallas_call x1, Pallas kernels, correlate(): pl.pallas_call(backward_kernel, out_shape=jax.ShapeDtypeStruct((SEQ, ROWS...  9.61 us
    pallas_call x1, Pallas kernels, convolve(): pl.pallas_call(forward_kernel, out_shape=(jax.ShapeDtypeStruct((NEAR, LAN...  8.59 us
    pallas_call x4, Pallas kernels, call(): pl.pallas_call(kernel, out_shape=out_shape, grid=(1,), in_specs=in_specs,...  7.76 us
    ppermute x1, waiting for transfers between devices, shards(): pair = jnp.stack([moved, lax.ppermute(moved, 'chan', chan_pairs(4))])  6.42 us
    all_to_all x3, waiting for transfers between devices, exchange(): return lax.all_to_all(array, axis, 0, 0, tiled=True)  5.54 us
  transfers between devices with their start and end apart: 15, of which 6 were waited for; matrix products, arithmetic and copies ran while one was open for 1% of the time, Pallas kernels for 22%

profile of v8, /device:TPU:32, one launch (start us, length us, event | category | flops | bytes accessed | tf_op | source)
XLA Modules:
  0.0 108.7 jit_solution(15085706609951610641)
XLA Ops:
  0.7 4.8 %collective-permute-start.3 = (bf16[128,512]{1,0:T(8,128)(2,1)}, bf16[128,512]{1,0:T(8,128)(2,1)S(1)}, u32[]{:S(2)}, u32[]{:S(2)}) collective-permute-start(bf16[128,512]{1,0:T(8,128)(2,1)} %param.15), channel_id=1, source_target_pairs={{0,0},{1,1},{2,32},{3,33},{4,64},{5,65},{6,96},{7,97},{8,8},{9,9},... | collective-permute-start | bytes 393224 | tf_op jit(solution)/shard_map/ppermute | solution.py:47
  5.5 2.4 %pack.1 = bf16[16,128,128]{2,1,0:T(8,128)(2,1)} custom-call(bf16[3,128,512]{2,1,0:T(8,128)(2,1)} %bitcast.9, f32[128,512]{1,0:T(8,128)} %filter_hbm.1), custom_call_target="tpu_custom_call" | custom-call | tf_op jit(solution)/shard_map/pack/pallas_call | solution.py:538
  7.8 7.2 %all-to-all-start = ((bf16[16,128,128]{2,1,0:T(8,128)(2,1)}), bf16[16,128,128]{2,1,0:T(8,128)(2,1)S(1)}, u32[]{:S(2)}, u32[]{:S(2)}) async-start(bf16[16,128,128]{2,1,0:T(8,128)(2,1)} %pack.1), calls=%async_computation | async-start | bytes 1048576 | tf_op jit(solution)/shard_map/all_to_all | solution.py:59
  15.1 1.8 %collective-permute-start.2 = (bf16[512,256]{1,0:T(8,128)(2,1)S(1)}, bf16[512,256]{1,0:T(8,128)(2,1)S(1)}, u32[]{:S(2)}, u32[]{:S(2)}) collective-permute-start(bf16[512,256]{1,0:T(8,128)(2,1)S(1)} %copy-done.1), channel_id=1, source_target_pairs={{0,24},{8,16},{16,8},{24,0},{32,56},{40,48},{48,40},{56,32},{64,88... | collective-permute-start | bytes 786440 | tf_op jit(solution)/shard_map/ppermute | solution.py:617
  16.8 0.4 collective-permute-start.1
  17.2 0.8 collective-permute-start.4
  18.0 0.1 reshape.37
  18.2 6.4 %collective-permute-done.4 = bf16[128,512]{1,0:T(8,128)(2,1)S(1)} collective-permute-done((bf16[128,512]{1,0:T(8,128)(2,1)S(1)}, bf16[128,512]{1,0:T(8,128)(2,1)S(1)}, u32[]{:S(2)}, u32[]{:S(2)}) %collective-permute-start.4) | collective-permute-done | bytes 131104 | tf_op jit(solution)/shard_map/ppermute | solution.py:615
  24.7 2.7 %collective-permute-start.7 = (bf16[2,128,512]{2,1,0:T(8,128)(2,1)S(1)}, bf16[2,128,512]{2,1,0:T(8,128)(2,1)S(1)}, u32[]{:S(2)}, u32[]{:S(2)}) collective-permute-start(bf16[2,128,512]{2,1,0:T(8,128)(2,1)S(1)} %pad_maximum_fusion.refs_4_.refs_0_), channel_id=1, source_target_pairs={{0,3},{1,2},{2,1},{3,0},{4,7},{5,6},{6,5},{7,4},{8,11},{9,10},{10,... | collective-permute-start | bytes 786440 | tf_op jit(solution)/shard_map/ppermute | solution.py:616
  27.3 0.4 collective-permute-start.6
  27.7 1.2 %collective-permute-done.2.refs_3_ = bf16[512,256]{1,0:T(8,128)(2,1)S(1)} collective-permute-done((bf16[512,256]{1,0:T(8,128)(2,1)S(1)}, bf16[512,256]{1,0:T(8,128)(2,1)S(1)}, u32[]{:S(2)}, u32[]{:S(2)}) %collective-permute-start.2) | collective-permute-done | bytes 262176 | tf_op jit(solution)/shard_map/ppermute | solution.py:617
  28.9 1.5 %collective-permute-start.5 = (bf16[2,128,512]{2,1,0:T(8,128)(2,1)S(1)}, bf16[2,128,512]{2,1,0:T(8,128)(2,1)S(1)}, u32[]{:S(2)}, u32[]{:S(2)}) collective-permute-start(bf16[2,128,512]{2,1,0:T(8,128)(2,1)S(1)} %pad_maximum_fusion.refs_4_.refs_0_), channel_id=1, source_target_pairs={{0,1},{1,0},{2,3},{3,2},{4,5},{5,4},{6,7},{7,6},{8,9},{9,8},{10,11... | collective-permute-start | bytes 786440 | tf_op jit(solution)/shard_map/ppermute | solution.py:616
  30.4 0.1 pad_add_fusion.place_ref
  30.5 8.6 %convolve.1 = (bf16[4,32,512]{2,1,0:T(8,128)(2,1)S(1)}, f32[2048,128]{1,0:T(8,128)}, f32[33,128,128]{2,1,0:T(8,128)}) custom-call(bf16[2048,128]{1,0:T(8,128)(2,1)S(1)} %bitcast.8, f32[3,128]{1,0:T(4,128)S(1)} %pad_maximum_fusion.1.taps_ref, bf16[64,72,96]{2,1,0:T(8,128)(2,1)} %constant.90.clone.first_hbm, bf16[128,384]{1,0:T(8,128)(2,1)} %constant.91.clone.ahead_hbm, ...), custom_call_target="tpu_custom_call" | custom-call | flops 2000000000 | bytes 100000 | tf_op jit(solution)/shard_map/convolve/pallas_call | solution.py:338
  39.2 0.2 collective-permute-done.5.refs_5_.refs_1_
  39.4 1.7 %send.1 = bf16[16,64,512]{2,1,0:T(8,128)(2,1)S(1)} custom-call(s32[3]{0:T(128)S(1)} %pad_add_fusion.place_ref, bf16[4,32,512]{2,1,0:T(8,128)(2,1)S(1)} %get-tuple-element.25.gated_ref, bf16[512,256]{1,0:T(8,128)(2,1)S(1)} %copy-done.1, bf16[512,256]{1,0:T(8,128)(2,1)S(1)} %collective-permute-done.refs_1_, ...), custom_call_target="tpu_custom_call" | custom-call | flops 1000000000 | bytes 2000000 | tf_op jit(solution)/shard_map/send/pallas_call | solution.py:520
  41.2 25.0 %all_to_all.20.got_ref.share_ref = bf16[16,64,512]{2,1,0:T(8,128)(2,1)S(1)} all-to-all(bf16[16,64,512]{2,1,0:T(8,128)(2,1)S(1)} %send.1), channel_id=1, replica_groups=mesh['seq'=16,'chan'=8] {'seq'}, dimensions={0} | all-to-all | bytes 2097152 | tf_op jit(solution)/shard_map/all_to_all | solution.py:59
  66.2 2.3 %outputs.1 = bf16[8,128,512]{2,1,0:T(8,128)(2,1)} custom-call(s32[3]{0:T(128)S(1)} %pad_add_fusion.place_ref, bf16[16,64,512]{2,1,0:T(8,128)(2,1)S(1)} %all_to_all.20.got_ref.share_ref, bf16[512,256]{1,0:T(8,128)(2,1)S(1)} %copy-done.1, bf16[512,256]{1,0:T(8,128)(2,1)S(1)} %collective-permute-done.refs_1_, ...), custom_call_target="tpu_custom_call" | custom-call | flops 1000000000 | bytes 2000000 | tf_op jit(solution)/shard_map/outputs/pallas_call | solution.py:520
  68.5 5.1 %all-to-all-start.2 = ((bf16[8,128,512]{2,1,0:T(8,128)(2,1)}), bf16[8,128,512]{2,1,0:T(8,128)(2,1)S(1)}, u32[]{:S(2)}, u32[]{:S(2)}) async-start(bf16[8,128,512]{2,1,0:T(8,128)(2,1)} %outputs.1), calls=%async_computation.2 | async-start | bytes 2097152 | tf_op jit(solution)/shard_map/all_to_all | solution.py:59
  73.6 2.4 %weights.1 = (f32[512,256]{1,0:T(8,128)}, bf16[512,256]{1,0:T(8,128)(2,1)}, bf16[512,256]{1,0:T(8,128)(2,1)}, bf16[512,256]{1,0:T(8,128)(2,1)}) custom-call(s32[3]{0:T(128)S(1)} %pad_add_fusion.place_ref, bf16[16,64,512]{2,1,0:T(8,128)(2,1)S(1)} %all_to_all.20.got_ref.share_ref, bf16[2,128,512]{2,1,0:T(8,128)(2,1)S(1)} %pad_maximum_fusion.refs_4_.refs_0_, ...), custom_call_target="tpu_custom_call" | custom-call | flops 1000000000 | bytes 2000000 | tf_op jit(solution)/shard_map/weights/pallas_call | solution.py:520
  76.0 0.1 collective-permute-start.9
  76.1 0.1 collective-permute-start.10
  76.2 1.8 %collective-permute-start.11 = (bf16[512,256]{1,0:T(8,128)(2,1)}, bf16[512,256]{1,0:T(8,128)(2,1)S(1)}, u32[]{:S(2)}, u32[]{:S(2)}) collective-permute-start(bf16[512,256]{1,0:T(8,128)(2,1)} %get-tuple-element.32), channel_id=1, source_target_pairs={{0,24},{8,16},{16,8},{24,0},{32,56},{40,48},{48,40},{56,32},{64,88... | collective-permute-start | bytes 786440 | tf_op jit(solution)/shard_map/ppermute | solution.py:630
  78.0 9.6 %correlate.1 = bf16[16,128,128]{2,1,0:T(8,128)(2,1)} custom-call(bf16[16,64,512]{2,1,0:T(8,128)(2,1)S(1)} %all_to_all.20.got_ref.share_ref, f32[2048,128]{1,0:T(8,128)} %get-tuple-element.26.kept_hbm, f32[33,128,128]{2,1,0:T(8,128)} %get-tuple-element.27.spec_hbm, f32[3,128]{1,0:T(4,128)S(1)} %pad_maximum_fusion.1.taps_ref, ...), custom_call_target="tpu_custom_call" | custom-call | flops 8000000000 | bytes 6000000 | tf_op jit(solution)/shard_map/correlate/pallas_call | solution.py:364
  87.6 3.7 %all-to-all-start.3 = ((bf16[16,128,128]{2,1,0:T(8,128)(2,1)}), bf16[16,128,128]{2,1,0:T(8,128)(2,1)S(1)}, u32[]{:S(2)}, u32[]{:S(2)}) async-start(bf16[16,128,128]{2,1,0:T(8,128)(2,1)} %correlate.1), calls=%async_computation.3 | async-start | bytes 1048576 | tf_op jit(solution)/shard_map/all_to_all | solution.py:59
  91.4 0.1 reduce_sum.12
  91.5 6.1 %collective-permute-start.8 = (bf16[128,512]{1,0:T(8,128)(2,1)S(1)}, bf16[128,512]{1,0:T(8,128)(2,1)S(1)}, u32[]{:S(2)}, u32[]{:S(2)}) collective-permute-start(bf16[128,512]{1,0:T(8,128)(2,1)S(1)} %reduce_sum.12), channel_id=1, source_target_pairs={{0,0},{1,1},{2,32},{3,33},{4,64},{5,65},{6,96},{7,97},{8,8},{9,9},... | collective-permute-start | bytes 393224 | tf_op jit(solution)/shard_map/ppermute | solution.py:47
  97.7 0.9 convert_add_fusion
  98.6 5.5 %all-to-all-done.3.got_ref = bf16[16,128,128]{2,1,0:T(8,128)(2,1)S(1)} async-done(((bf16[16,128,128]{2,1,0:T(8,128)(2,1)}), bf16[16,128,128]{2,1,0:T(8,128)(2,1)S(1)}, u32[]{:S(2)}, u32[]{:S(2)}) %all-to-all-start.3) | async-done | bytes 524320 | tf_op jit(solution)/shard_map/all_to_all | solution.py:59
  104.2 1.3 %unpack.1 = (bf16[3,128,512]{2,1,0:T(8,128)(2,1)}, f32[128,512]{1,0:T(8,128)}) custom-call(bf16[16,128,128]{2,1,0:T(8,128)(2,1)S(1)} %all-to-all-done.3.got_ref), custom_call_target="tpu_custom_call" | custom-call | flops 1000000000 | bytes 2000000 | tf_op jit(solution)/shard_map/unpack/pallas_call | solution.py:520
  105.5 2.6 %collective-permute-done.8 = bf16[128,512]{1,0:T(8,128)(2,1)S(1)} collective-permute-done((bf16[128,512]{1,0:T(8,128)(2,1)S(1)}, bf16[128,512]{1,0:T(8,128)(2,1)S(1)}, u32[]{:S(2)}, u32[]{:S(2)}) %collective-permute-start.8) | collective-permute-done | bytes 131104 | tf_op jit(solution)/shard_map/ppermute | solution.py:47
  108.0 0.7 copy.14
  (22 shorter events, 0.3 us)
Async XLA Ops:
  0.6 17.3 %copy-start = (f32[3,3,512]{2,1,0:T(4,128)S(1)}, f32[3,3,512]{2,1,0:T(4,128)}, u32[]{:S(2)}) copy-start(f32[3,3,512]{2,1,0:T(4,128)} %param.12) | copy-start | bytes 55300
  0.6 17.5 %copy-start.3 = (f32[3,32]{1,0:T(4,128)S(1)}, f32[3,32]{1,0:T(4,128)}, u32[]{:S(2)}) copy-start(f32[3,32]{1,0:T(4,128)} %constant.88.clone.1) | copy-start | bytes 1156
  0.7 14.4 %copy-start.1 = (bf16[512,256]{1,0:T(8,128)(2,1)S(1)}, bf16[512,256]{1,0:T(8,128)(2,1)}, u32[]{:S(2)}) copy-start(bf16[512,256]{1,0:T(8,128)(2,1)} %refs_0_.3) | copy-start | bytes 786436
  0.7 16.5 %collective-permute-start.3 = (bf16[128,512]{1,0:T(8,128)(2,1)}, bf16[128,512]{1,0:T(8,128)(2,1)S(1)}, u32[]{:S(2)}, u32[]{:S(2)}) collective-permute-start(bf16[128,512]{1,0:T(8,128)(2,1)} %param.15), channel_id=1, source_target_pairs={{0,0},{1,1},{2,32},{3,33},{4,64},{5,65},{6,96},{7,97},{8,8},{9,9},... | collective-permute-start | bytes 393224 | tf_op jit(solution)/shard_map/ppermute | solution.py:47
  7.8 22.7 %all-to-all-start = ((bf16[16,128,128]{2,1,0:T(8,128)(2,1)}), bf16[16,128,128]{2,1,0:T(8,128)(2,1)S(1)}, u32[]{:S(2)}, u32[]{:S(2)}) async-start(bf16[16,128,128]{2,1,0:T(8,128)(2,1)} %pack.1), calls=%async_computation | async-start | bytes 1048576 | tf_op jit(solution)/shard_map/all_to_all | solution.py:59
  15.1 13.9 %collective-permute-start.2 = (bf16[512,256]{1,0:T(8,128)(2,1)S(1)}, bf16[512,256]{1,0:T(8,128)(2,1)S(1)}, u32[]{:S(2)}, u32[]{:S(2)}) collective-permute-start(bf16[512,256]{1,0:T(8,128)(2,1)S(1)} %copy-done.1), channel_id=1, source_target_pairs={{0,24},{8,16},{16,8},{24,0},{32,56},{40,48},{48,40},{56,32},{64,88... | collective-permute-start | bytes 786440 | tf_op jit(solution)/shard_map/ppermute | solution.py:617
  16.8 22.3 %collective-permute-start.1 = (bf16[512,256]{1,0:T(8,128)(2,1)S(1)}, bf16[512,256]{1,0:T(8,128)(2,1)S(1)}, u32[]{:S(2)}, u32[]{:S(2)}) collective-permute-start(bf16[512,256]{1,0:T(8,128)(2,1)S(1)} %copy-done.1), channel_id=1, source_target_pairs={{0,16},{8,24},{16,0},{24,8},{32,48},{40,56},{48,32},{56,40},{64,80... | collective-permute-start | bytes 786440 | tf_op jit(solution)/shard_map/ppermute | solution.py:617
  17.2 21.9 %collective-permute-start = (bf16[512,256]{1,0:T(8,128)(2,1)S(1)}, bf16[512,256]{1,0:T(8,128)(2,1)S(1)}, u32[]{:S(2)}, u32[]{:S(2)}) collective-permute-start(bf16[512,256]{1,0:T(8,128)(2,1)S(1)} %copy-done.1), channel_id=1, source_target_pairs={{0,8},{8,0},{16,24},{24,16},{32,40},{40,32},{48,56},{56,48},{64,72... | collective-permute-start | bytes 786440 | tf_op jit(solution)/shard_map/ppermute | solution.py:617
  17.2 7.4 %collective-permute-start.4 = (bf16[128,512]{1,0:T(8,128)(2,1)S(1)}, bf16[128,512]{1,0:T(8,128)(2,1)S(1)}, u32[]{:S(2)}, u32[]{:S(2)}) collective-permute-start(bf16[128,512]{1,0:T(8,128)(2,1)S(1)} %collective-permute-done.3), channel_id=1, source_target_pairs={{0,4},{1,5},{2,6},{3,7},{4,0},{5,1},{6,2},{7,3},{8,12},{9,13},{10,... | collective-permute-start | bytes 393224 | tf_op jit(solution)/shard_map/ppermute | solution.py:615
  24.7 14.5 %collective-permute-start.7 = (bf16[2,128,512]{2,1,0:T(8,128)(2,1)S(1)}, bf16[2,128,512]{2,1,0:T(8,128)(2,1)S(1)}, u32[]{:S(2)}, u32[]{:S(2)}) collective-permute-start(bf16[2,128,512]{2,1,0:T(8,128)(2,1)S(1)} %pad_maximum_fusion.refs_4_.refs_0_), channel_id=1, source_target_pairs={{0,3},{1,2},{2,1},{3,0},{4,7},{5,6},{6,5},{7,4},{8,11},{9,10},{10,... | collective-permute-start | bytes 786440 | tf_op jit(solution)/shard_map/ppermute | solution.py:616
  27.3 11.9 %collective-permute-start.6 = (bf16[2,128,512]{2,1,0:T(8,128)(2,1)S(1)}, bf16[2,128,512]{2,1,0:T(8,128)(2,1)S(1)}, u32[]{:S(2)}, u32[]{:S(2)}) collective-permute-start(bf16[2,128,512]{2,1,0:T(8,128)(2,1)S(1)} %pad_maximum_fusion.refs_4_.refs_0_), channel_id=1, source_target_pairs={{0,2},{1,3},{2,0},{3,1},{4,6},{5,7},{6,4},{7,5},{8,10},{9,11},{10,... | collective-permute-start | bytes 786440 | tf_op jit(solution)/shard_map/ppermute | solution.py:616
  28.9 10.5 %collective-permute-start.5 = (bf16[2,128,512]{2,1,0:T(8,128)(2,1)S(1)}, bf16[2,128,512]{2,1,0:T(8,128)(2,1)S(1)}, u32[]{:S(2)}, u32[]{:S(2)}) collective-permute-start(bf16[2,128,512]{2,1,0:T(8,128)(2,1)S(1)} %pad_maximum_fusion.refs_4_.refs_0_), channel_id=1, source_target_pairs={{0,1},{1,0},{2,3},{3,2},{4,5},{5,4},{6,7},{7,6},{8,9},{9,8},{10,11... | collective-permute-start | bytes 786440 | tf_op jit(solution)/shard_map/ppermute | solution.py:616
  68.5 19.2 %all-to-all-start.2 = ((bf16[8,128,512]{2,1,0:T(8,128)(2,1)}), bf16[8,128,512]{2,1,0:T(8,128)(2,1)S(1)}, u32[]{:S(2)}, u32[]{:S(2)}) async-start(bf16[8,128,512]{2,1,0:T(8,128)(2,1)} %outputs.1), calls=%async_computation.2 | async-start | bytes 2097152 | tf_op jit(solution)/shard_map/all_to_all | solution.py:59
  76.0 21.6 %collective-permute-start.9 = (bf16[512,256]{1,0:T(8,128)(2,1)}, bf16[512,256]{1,0:T(8,128)(2,1)S(1)}, u32[]{:S(2)}, u32[]{:S(2)}) collective-permute-start(bf16[512,256]{1,0:T(8,128)(2,1)} %get-tuple-element.30), channel_id=1, source_target_pairs={{0,8},{8,0},{16,24},{24,16},{32,40},{40,32},{48,56},{56,48},{64,72... | collective-permute-start | bytes 786440 | tf_op jit(solution)/shard_map/ppermute | solution.py:630
  76.1 21.5 %collective-permute-start.10 = (bf16[512,256]{1,0:T(8,128)(2,1)}, bf16[512,256]{1,0:T(8,128)(2,1)S(1)}, u32[]{:S(2)}, u32[]{:S(2)}) collective-permute-start(bf16[512,256]{1,0:T(8,128)(2,1)} %get-tuple-element.31), channel_id=1, source_target_pairs={{0,16},{8,24},{16,0},{24,8},{32,48},{40,56},{48,32},{56,40},{64,80... | collective-permute-start | bytes 786440 | tf_op jit(solution)/shard_map/ppermute | solution.py:630
  76.2 21.5 %collective-permute-start.11 = (bf16[512,256]{1,0:T(8,128)(2,1)}, bf16[512,256]{1,0:T(8,128)(2,1)S(1)}, u32[]{:S(2)}, u32[]{:S(2)}) collective-permute-start(bf16[512,256]{1,0:T(8,128)(2,1)} %get-tuple-element.32), channel_id=1, source_target_pairs={{0,24},{8,16},{16,8},{24,0},{32,56},{40,48},{48,40},{56,32},{64,88... | collective-permute-start | bytes 786440 | tf_op jit(solution)/shard_map/ppermute | solution.py:630
  87.6 10.1 %copy-start.2 = (f32[512,256]{1,0:T(8,128)S(1)}, f32[512,256]{1,0:T(8,128)}, u32[]{:S(2)}) copy-start(f32[512,256]{1,0:T(8,128)} %get-tuple-element.29) | copy-start | bytes 1572868
  87.6 16.5 %all-to-all-start.3 = ((bf16[16,128,128]{2,1,0:T(8,128)(2,1)}), bf16[16,128,128]{2,1,0:T(8,128)(2,1)S(1)}, u32[]{:S(2)}, u32[]{:S(2)}) async-start(bf16[16,128,128]{2,1,0:T(8,128)(2,1)} %correlate.1), calls=%async_computation.3 | async-start | bytes 1048576 | tf_op jit(solution)/shard_map/all_to_all | solution.py:59
  91.5 16.5 %collective-permute-start.8 = (bf16[128,512]{1,0:T(8,128)(2,1)S(1)}, bf16[128,512]{1,0:T(8,128)(2,1)S(1)}, u32[]{:S(2)}, u32[]{:S(2)}) collective-permute-start(bf16[128,512]{1,0:T(8,128)(2,1)S(1)} %reduce_sum.12), channel_id=1, source_target_pairs={{0,0},{1,1},{2,32},{3,33},{4,64},{5,65},{6,96},{7,97},{8,8},{9,9},... | collective-permute-start | bytes 393224 | tf_op jit(solution)/shard_map/ppermute | solution.py:47

commit v9 on v8

--- a/solution.py
+++ b/solution.py
@@ -437,7 +437,7 @@
 def fetch_weights(place_ref, refs, weights, sems):
     copies = []
     for step in range(NEAR):
-        low = pl.multiple_of((place_ref[0] ^ step) * 256, 256)
+        low = pl.multiple_of((place_ref[0] ^ (-step % NEAR)) * 256, 256)
         copies.append(started(refs[step], weights.at[:, pl.ds(low, 256)], sems.at[step]))
     return copies
 
@@ -614,7 +614,9 @@
     signals = exchange(pack(projected.transpose(1, 0, 2), long_filter), "seq")
     pair = jnp.stack([moved, lax.ppermute(moved, "chan", chan_pairs(4))])
     cots = [pair] + [lax.ppermute(pair, "chan", chan_pairs(far)) for far in range(1, FAR)]
-    weights = [w_out] + [lax.ppermute(w_out, "seq", near_pairs(step)) for step in range(1, NEAR)]
+    weights = [w_out] + [
+        lax.ppermute(w_out, "seq", near_pairs(-step % NEAR)) for step in range(1, NEAR)
+    ]
 
     own = lax.dynamic_slice_in_dim(short_filter, seq_at * LANE, LANE, axis=2).reshape(3, 3 * LANE)
     plain = jnp.zeros((3, LANE), F32).at[0].set(1.0)

time: 109 us -> 109 us (level)
  starting transfers between devices: 36.3 us -> 34.9 us
    ppermute x3, waiting for transfers between devices: 0.3 us -> 2.44 us  [shards(): lax.ppermute(pair, 'chan', chan_pairs(far))]
    ppermute x3, waiting for transfers between devices: 1.25 us -> 0.01 us  [shards(): lax.ppermute(w_out, 'seq', near_pairs(-step % NEAR))]
  transfers between devices with their start and end apart: 15 -> 15, of which waited for: 6 -> 5; matrix products, arithmetic and copies ran while one was open for 1% -> 1% of each run, Pallas kernels for 22% -> 22%
where the time goes in v9:
time: 109 us; the launch traced here: 108 us
  starting transfers between devices  34.9 us (32%)
  Pallas kernels  28.3 us (26%)
  blocking collectives  25.1 us (23%)
  waiting for transfers between devices  16.9 us (16%)
  other arithmetic  1.26 us (1%)
    all_to_all x1, blocking collectives, exchange(): return lax.all_to_all(array, axis, 0, 0, tiled=True)  25.1 us
    all_to_all x3, starting transfers between devices, exchange(): return lax.all_to_all(array, axis, 0, 0, tiled=True)  15.5 us
    ppermute x2, starting transfers between devices, swapped(): return lax.ppermute(array, ('seq', 'chan'), swap_pairs())  10.9 us
    pallas_call x1, Pallas kernels, correlate(): pl.pallas_call(backward_kernel, out_shape=jax.ShapeDtypeStruct((SEQ, ROWS...  9.61 us
    pallas_call x1, Pallas kernels, convolve(): pl.pallas_call(forward_kernel, out_shape=(jax.ShapeDtypeStruct((NEAR, LAN...  8.59 us
    pallas_call x4, Pallas kernels, call(): pl.pallas_call(kernel, out_shape=out_shape, grid=(1,), in_specs=in_specs,...  7.75 us
    ppermute x1, waiting for transfers between devices, shards(): pair = jnp.stack([moved, lax.ppermute(moved, 'chan', chan_pairs(4))])  6.35 us
    all_to_all x3, waiting for transfers between devices, exchange(): return lax.all_to_all(array, axis, 0, 0, tiled=True)  5.53 us
  transfers between devices with their start and end apart: 15, of which 5 were waited for; matrix products, arithmetic and copies ran while one was open for 1% of the time, Pallas kernels for 22%

profile of v9, /device:TPU:32, one launch (start us, length us, event | category | flops | bytes accessed | tf_op | source)
XLA Modules:
  0.0 108.1 jit_solution(12120609821175517847)
XLA Ops:
  0.7 4.8 %collective-permute-start.3 = (bf16[128,512]{1,0:T(8,128)(2,1)}, bf16[128,512]{1,0:T(8,128)(2,1)S(1)}, u32[]{:S(2)}, u32[]{:S(2)}) collective-permute-start(bf16[128,512]{1,0:T(8,128)(2,1)} %param.15), channel_id=1, source_target_pairs={{0,0},{1,1},{2,32},{3,33},{4,64},{5,65},{6,96},{7,97},{8,8},{9,9},... | collective-permute-start | bytes 393224 | tf_op jit(solution)/shard_map/ppermute | solution.py:47
  5.5 2.4 %pack.1 = bf16[16,128,128]{2,1,0:T(8,128)(2,1)} custom-call(bf16[3,128,512]{2,1,0:T(8,128)(2,1)} %bitcast.9, f32[128,512]{1,0:T(8,128)} %filter_hbm.1), custom_call_target="tpu_custom_call" | custom-call | tf_op jit(solution)/shard_map/pack/pallas_call | solution.py:538
  7.8 7.2 %all-to-all-start = ((bf16[16,128,128]{2,1,0:T(8,128)(2,1)}), bf16[16,128,128]{2,1,0:T(8,128)(2,1)S(1)}, u32[]{:S(2)}, u32[]{:S(2)}) async-start(bf16[16,128,128]{2,1,0:T(8,128)(2,1)} %pack.1), calls=%async_computation | async-start | bytes 1048576 | tf_op jit(solution)/shard_map/all_to_all | solution.py:59
  15.1 0.5 collective-permute-start.2
  15.6 1.7 %collective-permute-start.1 = (bf16[512,256]{1,0:T(8,128)(2,1)S(1)}, bf16[512,256]{1,0:T(8,128)(2,1)S(1)}, u32[]{:S(2)}, u32[]{:S(2)}) collective-permute-start(bf16[512,256]{1,0:T(8,128)(2,1)S(1)} %copy-done.1), channel_id=1, source_target_pairs={{0,16},{8,24},{16,0},{24,8},{32,48},{40,56},{48,32},{56,40},{64,80... | collective-permute-start | bytes 786440 | tf_op jit(solution)/shard_map/ppermute | solution.py:618
  17.2 0.8 collective-permute-start.4
  18.1 0.1 reshape.37
  18.3 6.3 %collective-permute-done.4 = bf16[128,512]{1,0:T(8,128)(2,1)S(1)} collective-permute-done((bf16[128,512]{1,0:T(8,128)(2,1)S(1)}, bf16[128,512]{1,0:T(8,128)(2,1)S(1)}, u32[]{:S(2)}, u32[]{:S(2)}) %collective-permute-start.4) | collective-permute-done | bytes 131104 | tf_op jit(solution)/shard_map/ppermute | solution.py:615
  24.6 2.7 %collective-permute-start.7 = (bf16[2,128,512]{2,1,0:T(8,128)(2,1)S(1)}, bf16[2,128,512]{2,1,0:T(8,128)(2,1)S(1)}, u32[]{:S(2)}, u32[]{:S(2)}) collective-permute-start(bf16[2,128,512]{2,1,0:T(8,128)(2,1)S(1)} %pad_maximum_fusion.refs_4_.refs_0_), channel_id=1, source_target_pairs={{0,3},{1,2},{2,1},{3,0},{4,7},{5,6},{6,5},{7,4},{8,11},{9,10},{10,... | collective-permute-start | bytes 786440 | tf_op jit(solution)/shard_map/ppermute | solution.py:616
  27.3 0.4 collective-permute-start.6
  27.7 0.5 collective-permute-start.5
  28.2 0.1 pad_add_fusion.place_ref
  28.3 8.6 %convolve.1 = (bf16[4,32,512]{2,1,0:T(8,128)(2,1)S(1)}, f32[2048,128]{1,0:T(8,128)}, f32[33,128,128]{2,1,0:T(8,128)}) custom-call(bf16[2048,128]{1,0:T(8,128)(2,1)S(1)} %bitcast.8, f32[3,128]{1,0:T(4,128)S(1)} %pad_maximum_fusion.1.taps_ref, bf16[64,72,96]{2,1,0:T(8,128)(2,1)} %constant.90.clone.first_hbm, bf16[128,384]{1,0:T(8,128)(2,1)} %constant.91.clone.ahead_hbm, ...), custom_call_target="tpu_custom_call" | custom-call | flops 2000000000 | bytes 100000 | tf_op jit(solution)/shard_map/convolve/pallas_call | solution.py:338
  36.9 2.2 %collective-permute-done.6.refs_6_.refs_2_ = bf16[2,128,512]{2,1,0:T(8,128)(2,1)S(1)} collective-permute-done((bf16[2,128,512]{2,1,0:T(8,128)(2,1)S(1)}, bf16[2,128,512]{2,1,0:T(8,128)(2,1)S(1)}, u32[]{:S(2)}, u32[]{:S(2)}) %collective-permute-start.6) | collective-permute-done | bytes 262176 | tf_op jit(solution)/shard_map/ppermute | solution.py:616
  39.1 0.2 collective-permute-done.5.refs_5_.refs_1_
  39.4 1.7 %send.1 = bf16[16,64,512]{2,1,0:T(8,128)(2,1)S(1)} custom-call(s32[3]{0:T(128)S(1)} %pad_add_fusion.place_ref, bf16[4,32,512]{2,1,0:T(8,128)(2,1)S(1)} %get-tuple-element.25.gated_ref, bf16[512,256]{1,0:T(8,128)(2,1)S(1)} %copy-done.1, bf16[512,256]{1,0:T(8,128)(2,1)S(1)} %collective-permute-done.refs_1_, ...), custom_call_target="tpu_custom_call" | custom-call | flops 1000000000 | bytes 2000000 | tf_op jit(solution)/shard_map/send/pallas_call | solution.py:520
  41.1 25.1 %all_to_all.20.got_ref.share_ref = bf16[16,64,512]{2,1,0:T(8,128)(2,1)S(1)} all-to-all(bf16[16,64,512]{2,1,0:T(8,128)(2,1)S(1)} %send.1), channel_id=1, replica_groups=mesh['seq'=16,'chan'=8] {'seq'}, dimensions={0} | all-to-all | bytes 2097152 | tf_op jit(solution)/shard_map/all_to_all | solution.py:59
  66.2 2.3 %outputs.1 = bf16[8,128,512]{2,1,0:T(8,128)(2,1)} custom-call(s32[3]{0:T(128)S(1)} %pad_add_fusion.place_ref, bf16[16,64,512]{2,1,0:T(8,128)(2,1)S(1)} %all_to_all.20.got_ref.share_ref, bf16[512,256]{1,0:T(8,128)(2,1)S(1)} %copy-done.1, bf16[512,256]{1,0:T(8,128)(2,1)S(1)} %collective-permute-done.refs_1_, ...), custom_call_target="tpu_custom_call" | custom-call | flops 1000000000 | bytes 2000000 | tf_op jit(solution)/shard_map/outputs/pallas_call | solution.py:520
  68.4 4.6 %all-to-all-start.2 = ((bf16[8,128,512]{2,1,0:T(8,128)(2,1)}), bf16[8,128,512]{2,1,0:T(8,128)(2,1)S(1)}, u32[]{:S(2)}, u32[]{:S(2)}) async-start(bf16[8,128,512]{2,1,0:T(8,128)(2,1)} %outputs.1), calls=%async_computation.2 | async-start | bytes 2097152 | tf_op jit(solution)/shard_map/all_to_all | solution.py:59
  73.0 2.4 %weights.1 = (f32[512,256]{1,0:T(8,128)}, bf16[512,256]{1,0:T(8,128)(2,1)}, bf16[512,256]{1,0:T(8,128)(2,1)}, bf16[512,256]{1,0:T(8,128)(2,1)}) custom-call(s32[3]{0:T(128)S(1)} %pad_add_fusion.place_ref, bf16[16,64,512]{2,1,0:T(8,128)(2,1)S(1)} %all_to_all.20.got_ref.share_ref, bf16[2,128,512]{2,1,0:T(8,128)(2,1)S(1)} %pad_maximum_fusion.refs_4_.refs_0_, ...), custom_call_target="tpu_custom_call" | custom-call | flops 1000000000 | bytes 2000000 | tf_op jit(solution)/shard_map/weights/pallas_call | solution.py:520
  75.5 0.1 collective-permute-start.9
  75.6 0.1 collective-permute-start.10
  75.6 1.8 %collective-permute-start.11 = (bf16[512,256]{1,0:T(8,128)(2,1)}, bf16[512,256]{1,0:T(8,128)(2,1)S(1)}, u32[]{:S(2)}, u32[]{:S(2)}) collective-permute-start(bf16[512,256]{1,0:T(8,128)(2,1)} %get-tuple-element.32), channel_id=1, source_target_pairs={{0,24},{8,16},{16,8},{24,0},{32,56},{40,48},{48,40},{56,32},{64,88... | collective-permute-start | bytes 786440 | tf_op jit(solution)/shard_map/ppermute | solution.py:632
  77.4 9.6 %correlate.1 = bf16[16,128,128]{2,1,0:T(8,128)(2,1)} custom-call(bf16[16,64,512]{2,1,0:T(8,128)(2,1)S(1)} %all_to_all.20.got_ref.share_ref, f32[2048,128]{1,0:T(8,128)} %get-tuple-element.26.kept_hbm, f32[33,128,128]{2,1,0:T(8,128)} %get-tuple-element.27.spec_hbm, f32[3,128]{1,0:T(4,128)S(1)} %pad_maximum_fusion.1.taps_ref, ...), custom_call_target="tpu_custom_call" | custom-call | flops 8000000000 | bytes 6000000 | tf_op jit(solution)/shard_map/correlate/pallas_call | solution.py:364
  87.1 3.7 %all-to-all-start.3 = ((bf16[16,128,128]{2,1,0:T(8,128)(2,1)}), bf16[16,128,128]{2,1,0:T(8,128)(2,1)S(1)}, u32[]{:S(2)}, u32[]{:S(2)}) async-start(bf16[16,128,128]{2,1,0:T(8,128)(2,1)} %correlate.1), calls=%async_computation.3 | async-start | bytes 1048576 | tf_op jit(solution)/shard_map/all_to_all | solution.py:59
  90.8 0.1 reduce_sum.12
  90.9 6.1 %collective-permute-start.8 = (bf16[128,512]{1,0:T(8,128)(2,1)S(1)}, bf16[128,512]{1,0:T(8,128)(2,1)S(1)}, u32[]{:S(2)}, u32[]{:S(2)}) collective-permute-start(bf16[128,512]{1,0:T(8,128)(2,1)S(1)} %reduce_sum.12), channel_id=1, source_target_pairs={{0,0},{1,1},{2,32},{3,33},{4,64},{5,65},{6,96},{7,97},{8,8},{9,9},... | collective-permute-start | bytes 393224 | tf_op jit(solution)/shard_map/ppermute | solution.py:47
  97.1 0.9 convert_add_fusion
  98.1 5.5 %all-to-all-done.3.got_ref = bf16[16,128,128]{2,1,0:T(8,128)(2,1)S(1)} async-done(((bf16[16,128,128]{2,1,0:T(8,128)(2,1)}), bf16[16,128,128]{2,1,0:T(8,128)(2,1)S(1)}, u32[]{:S(2)}, u32[]{:S(2)}) %all-to-all-start.3) | async-done | bytes 524320 | tf_op jit(solution)/shard_map/all_to_all | solution.py:59
  103.6 1.3 %unpack.1 = (bf16[3,128,512]{2,1,0:T(8,128)(2,1)}, f32[128,512]{1,0:T(8,128)}) custom-call(bf16[16,128,128]{2,1,0:T(8,128)(2,1)S(1)} %all-to-all-done.3.got_ref), custom_call_target="tpu_custom_call" | custom-call | flops 1000000000 | bytes 2000000 | tf_op jit(solution)/shard_map/unpack/pallas_call | solution.py:520
  104.9 2.6 %collective-permute-done.8 = bf16[128,512]{1,0:T(8,128)(2,1)S(1)} collective-permute-done((bf16[128,512]{1,0:T(8,128)(2,1)S(1)}, bf16[128,512]{1,0:T(8,128)(2,1)S(1)}, u32[]{:S(2)}, u32[]{:S(2)}) %collective-permute-start.8) | collective-permute-done | bytes 131104 | tf_op jit(solution)/shard_map/ppermute | solution.py:47
  107.5 0.7 copy.14
  (22 shorter events, 0.2 us)
Async XLA Ops:
  0.6 17.4 %copy-start = (f32[3,3,512]{2,1,0:T(4,128)S(1)}, f32[3,3,512]{2,1,0:T(4,128)}, u32[]{:S(2)}) copy-start(f32[3,3,512]{2,1,0:T(4,128)} %param.12) | copy-start | bytes 55300
  0.6 17.5 %copy-start.3 = (f32[3,32]{1,0:T(4,128)S(1)}, f32[3,32]{1,0:T(4,128)}, u32[]{:S(2)}) copy-start(f32[3,32]{1,0:T(4,128)} %constant.88.clone.1) | copy-start | bytes 1156
  0.7 14.4 %copy-start.1 = (bf16[512,256]{1,0:T(8,128)(2,1)S(1)}, bf16[512,256]{1,0:T(8,128)(2,1)}, u32[]{:S(2)}) copy-start(bf16[512,256]{1,0:T(8,128)(2,1)} %refs_0_.3) | copy-start | bytes 786436
  0.7 16.6 %collective-permute-start.3 = (bf16[128,512]{1,0:T(8,128)(2,1)}, bf16[128,512]{1,0:T(8,128)(2,1)S(1)}, u32[]{:S(2)}, u32[]{:S(2)}) collective-permute-start(bf16[128,512]{1,0:T(8,128)(2,1)} %param.15), channel_id=1, source_target_pairs={{0,0},{1,1},{2,32},{3,33},{4,64},{5,65},{6,96},{7,97},{8,8},{9,9},... | collective-permute-start | bytes 393224 | tf_op jit(solution)/shard_map/ppermute | solution.py:47
  7.8 20.5 %all-to-all-start = ((bf16[16,128,128]{2,1,0:T(8,128)(2,1)}), bf16[16,128,128]{2,1,0:T(8,128)(2,1)S(1)}, u32[]{:S(2)}, u32[]{:S(2)}) async-start(bf16[16,128,128]{2,1,0:T(8,128)(2,1)} %pack.1), calls=%async_computation | async-start | bytes 1048576 | tf_op jit(solution)/shard_map/all_to_all | solution.py:59
  15.1 12.6 %collective-permute-start.2 = (bf16[512,256]{1,0:T(8,128)(2,1)S(1)}, bf16[512,256]{1,0:T(8,128)(2,1)S(1)}, u32[]{:S(2)}, u32[]{:S(2)}) collective-permute-start(bf16[512,256]{1,0:T(8,128)(2,1)S(1)} %copy-done.1), channel_id=1, source_target_pairs={{0,8},{8,0},{16,24},{24,16},{32,40},{40,32},{48,56},{56,48},{64,72... | collective-permute-start | bytes 786440 | tf_op jit(solution)/shard_map/ppermute | solution.py:618
  15.6 21.3 %collective-permute-start.1 = (bf16[512,256]{1,0:T(8,128)(2,1)S(1)}, bf16[512,256]{1,0:T(8,128)(2,1)S(1)}, u32[]{:S(2)}, u32[]{:S(2)}) collective-permute-start(bf16[512,256]{1,0:T(8,128)(2,1)S(1)} %copy-done.1), channel_id=1, source_target_pairs={{0,16},{8,24},{16,0},{24,8},{32,48},{40,56},{48,32},{56,40},{64,80... | collective-permute-start | bytes 786440 | tf_op jit(solution)/shard_map/ppermute | solution.py:618
  17.2 19.7 %collective-permute-start = (bf16[512,256]{1,0:T(8,128)(2,1)S(1)}, bf16[512,256]{1,0:T(8,128)(2,1)S(1)}, u32[]{:S(2)}, u32[]{:S(2)}) collective-permute-start(bf16[512,256]{1,0:T(8,128)(2,1)S(1)} %copy-done.1), channel_id=1, source_target_pairs={{0,24},{8,16},{16,8},{24,0},{32,56},{40,48},{48,40},{56,32},{64,88... | collective-permute-start | bytes 786440 | tf_op jit(solution)/shard_map/ppermute | solution.py:618
  17.2 7.4 %collective-permute-start.4 = (bf16[128,512]{1,0:T(8,128)(2,1)S(1)}, bf16[128,512]{1,0:T(8,128)(2,1)S(1)}, u32[]{:S(2)}, u32[]{:S(2)}) collective-permute-start(bf16[128,512]{1,0:T(8,128)(2,1)S(1)} %collective-permute-done.3), channel_id=1, source_target_pairs={{0,4},{1,5},{2,6},{3,7},{4,0},{5,1},{6,2},{7,3},{8,12},{9,13},{10,... | collective-permute-start | bytes 393224 | tf_op jit(solution)/shard_map/ppermute | solution.py:615
  24.6 12.3 %collective-permute-start.7 = (bf16[2,128,512]{2,1,0:T(8,128)(2,1)S(1)}, bf16[2,128,512]{2,1,0:T(8,128)(2,1)S(1)}, u32[]{:S(2)}, u32[]{:S(2)}) collective-permute-start(bf16[2,128,512]{2,1,0:T(8,128)(2,1)S(1)} %pad_maximum_fusion.refs_4_.refs_0_), channel_id=1, source_target_pairs={{0,3},{1,2},{2,1},{3,0},{4,7},{5,6},{6,5},{7,4},{8,11},{9,10},{10,... | collective-permute-start | bytes 786440 | tf_op jit(solution)/shard_map/ppermute | solution.py:616
  27.3 11.8 %collective-permute-start.6 = (bf16[2,128,512]{2,1,0:T(8,128)(2,1)S(1)}, bf16[2,128,512]{2,1,0:T(8,128)(2,1)S(1)}, u32[]{:S(2)}, u32[]{:S(2)}) collective-permute-start(bf16[2,128,512]{2,1,0:T(8,128)(2,1)S(1)} %pad_maximum_fusion.refs_4_.refs_0_), channel_id=1, source_target_pairs={{0,2},{1,3},{2,0},{3,1},{4,6},{5,7},{6,4},{7,5},{8,10},{9,11},{10,... | collective-permute-start | bytes 786440 | tf_op jit(solution)/shard_map/ppermute | solution.py:616
  27.7 11.7 %collective-permute-start.5 = (bf16[2,128,512]{2,1,0:T(8,128)(2,1)S(1)}, bf16[2,128,512]{2,1,0:T(8,128)(2,1)S(1)}, u32[]{:S(2)}, u32[]{:S(2)}) collective-permute-start(bf16[2,128,512]{2,1,0:T(8,128)(2,1)S(1)} %pad_maximum_fusion.refs_4_.refs_0_), channel_id=1, source_target_pairs={{0,1},{1,0},{2,3},{3,2},{4,5},{5,4},{6,7},{7,6},{8,9},{9,8},{10,11... | collective-permute-start | bytes 786440 | tf_op jit(solution)/shard_map/ppermute | solution.py:616
  68.4 18.6 %all-to-all-start.2 = ((bf16[8,128,512]{2,1,0:T(8,128)(2,1)}), bf16[8,128,512]{2,1,0:T(8,128)(2,1)S(1)}, u32[]{:S(2)}, u32[]{:S(2)}) async-start(bf16[8,128,512]{2,1,0:T(8,128)(2,1)} %outputs.1), calls=%async_computation.2 | async-start | bytes 2097152 | tf_op jit(solution)/shard_map/all_to_all | solution.py:59
  75.5 21.6 %collective-permute-start.9 = (bf16[512,256]{1,0:T(8,128)(2,1)}, bf16[512,256]{1,0:T(8,128)(2,1)S(1)}, u32[]{:S(2)}, u32[]{:S(2)}) collective-permute-start(bf16[512,256]{1,0:T(8,128)(2,1)} %get-tuple-element.30), channel_id=1, source_target_pairs={{0,8},{8,0},{16,24},{24,16},{32,40},{40,32},{48,56},{56,48},{64,72... | collective-permute-start | bytes 786440 | tf_op jit(solution)/shard_map/ppermute | solution.py:632
  75.6 21.5 %collective-permute-start.10 = (bf16[512,256]{1,0:T(8,128)(2,1)}, bf16[512,256]{1,0:T(8,128)(2,1)S(1)}, u32[]{:S(2)}, u32[]{:S(2)}) collective-permute-start(bf16[512,256]{1,0:T(8,128)(2,1)} %get-tuple-element.31), channel_id=1, source_target_pairs={{0,16},{8,24},{16,0},{24,8},{32,48},{40,56},{48,32},{56,40},{64,80... | collective-permute-start | bytes 786440 | tf_op jit(solution)/shard_map/ppermute | solution.py:632
  75.6 21.5 %collective-permute-start.11 = (bf16[512,256]{1,0:T(8,128)(2,1)}, bf16[512,256]{1,0:T(8,128)(2,1)S(1)}, u32[]{:S(2)}, u32[]{:S(2)}) collective-permute-start(bf16[512,256]{1,0:T(8,128)(2,1)} %get-tuple-element.32), channel_id=1, source_target_pairs={{0,24},{8,16},{16,8},{24,0},{32,56},{40,48},{48,40},{56,32},{64,88... | collective-permute-start | bytes 786440 | tf_op jit(solution)/shard_map/ppermute | solution.py:632
  87.0 10.1 %copy-start.2 = (f32[512,256]{1,0:T(8,128)S(1)}, f32[512,256]{1,0:T(8,128)}, u32[]{:S(2)}) copy-start(f32[512,256]{1,0:T(8,128)} %get-tuple-element.29) | copy-start | bytes 1572868
  87.1 16.5 %all-to-all-start.3 = ((bf16[16,128,128]{2,1,0:T(8,128)(2,1)}), bf16[16,128,128]{2,1,0:T(8,128)(2,1)S(1)}, u32[]{:S(2)}, u32[]{:S(2)}) async-start(bf16[16,128,128]{2,1,0:T(8,128)(2,1)} %correlate.1), calls=%async_computation.3 | async-start | bytes 1048576 | tf_op jit(solution)/shard_map/all_to_all | solution.py:59
  90.9 16.5 %collective-permute-start.8 = (bf16[128,512]{1,0:T(8,128)(2,1)S(1)}, bf16[128,512]{1,0:T(8,128)(2,1)S(1)}, u32[]{:S(2)}, u32[]{:S(2)}) collective-permute-start(bf16[128,512]{1,0:T(8,128)(2,1)S(1)} %reduce_sum.12), channel_id=1, source_target_pairs={{0,0},{1,1},{2,32},{3,33},{4,64},{5,65},{6,96},{7,97},{8,8},{9,9},... | collective-permute-start | bytes 393224 | tf_op jit(solution)/shard_map/ppermute | solution.py:47
